TPU v7x, 32 devices: a whole 2x2x4 slice. The times are simulated.
32 devices in a mesh: row: 8 (over y, x, core), col: 4 (over z).
Axes of the slice: x: 2, y: 2, z: 4, core: 2. Of those that a mesh axis runs over, the one named last changes fastest.
Arguments:
- panel: int32 [32], replicated, may hold values from 0 to 31, each once
- trailing: float32 [8192, 8192], P('row', 'col'), as said below
Outputs:
- factor_panels: float32 [8192, 768], P('row')
- schur: float32 [8192, 8192], P('row', 'col')
Inputs may be any that keep to these rules, and one draw needn't show every extreme that they name: panel names every block index once. In matrix order trailing is symmetric, and each diagonal block of 256 x 256 is strictly diagonally dominant with a positive diagonal.
All inputs are finite; a program needn't handle non-finite values.
Results may differ from a plain program's by a relative error of at most 0.0001.
Values sent between devices are 32-bit elements; how exact they have to be, the bound alone decides.
No kernel may reach another device: no remote copies, remote signals or barrier semaphores. Data moves between devices by JAX's collectives and lax.ppermute only.
A program may use at most 128 MiB of HBM per device.

v0:
```python
import jax
import jax.numpy as jnp
from jax import lax
from jax.experimental import pallas as pl
from jax.experimental.pallas import tpu as pltpu
from jax.sharding import PartitionSpec as P


NB = 256
PANELS = 3
AXES = ("row", "col")
INTERPRET = False


def thirds(x):
    high = x.astype(jnp.bfloat16)
    rest = x - high.astype(jnp.float32)
    mid = rest.astype(jnp.bfloat16)
    return high, mid, (rest - mid.astype(jnp.float32)).astype(jnp.bfloat16)


def bdot(a, b, cb):
    return lax.dot_general(
        a, b, (((1,), (cb,)), ((), ())), preferred_element_type=jnp.float32
    )


def dot6(a, b, cb=0):
    m = a.shape[0]
    a3 = jnp.concatenate(thirds(a), axis=0)
    high, mid, low = thirds(b)
    one = bdot(a3, high, cb)
    two = bdot(a3[: 2 * m], mid, cb)
    small = bdot(a3[:m], low, cb) + two[m:] + one[2 * m :]
    return (small + (two[:m] + one[m : 2 * m])) + one[:m]


def iotas(shape):
    return (lax.broadcasted_iota(jnp.int32, shape, 0), lax.broadcasted_iota(jnp.int32, shape, 1))


def invert_block(d_ref, w_ref, work_ref):
    n = d_ref.shape[0]
    ii, jj = iotas((n, n))
    eye = ii == jj
    d = d_ref[...]
    diag = jnp.where(eye, d, 0.0)
    by_col = lax.rsqrt(jnp.sum(diag, axis=0, keepdims=True))
    by_row = lax.rsqrt(jnp.sum(diag, axis=1, keepdims=True))

    def half(r):
        return jnp.where(ii > jj, r, jnp.where(eye, 0.5 * r, 0.0))

    res = jnp.where(eye, 0.0, d * by_row * by_col)
    w_ref[...] = jnp.where(eye, by_row, 0.0) - half(res) * by_col

    def cond(carry):
        count, size = carry
        return (count < 12) & (size > 1e-7)

    def body(carry):
        count, _ = carry
        w = w_ref[...]
        s = dot6(dot6(w, d_ref[...]), w, 1)
        res = jnp.where(eye, s - 1.0, s)
        w_ref[...] = w - dot6(half(res), w)
        return count + 1, jnp.sum(res * res)

    _, size = lax.while_loop(cond, body, (jnp.int32(0), jnp.float32(1.0)))
    low_diag = jnp.min(jnp.where(eye, w_ref[...], 1.0))

    @pl.when(jnp.logical_not((size <= 1e-7) & (low_diag > 0.0)))
    def _():
        work_ref[:, :n] = d_ref[...]
        work_ref[:, n:] = jnp.where(eye, 1.0, 0.0)
        _, lane2 = iotas((n, 2 * n))
        row1, _ = iotas((n, 1))
        lane1 = lax.broadcasted_iota(jnp.int32, (1, 2 * n), 1)

        @pl.loop(0, n)
        def _(k):
            row = work_ref[pl.ds(k, 1), :]
            scale = lax.rsqrt(jnp.sum(jnp.where(lane1 == k, row, 0.0), axis=1, keepdims=True))
            row = row * scale
            full = work_ref[...]
            col = jnp.sum(jnp.where(lane2 == k, full, 0.0), axis=1, keepdims=True) * scale
            work_ref[...] = full - jnp.where(row1 > k, col, 0.0) * row
            work_ref[pl.ds(k, 1), :] = row

        w_ref[...] = work_ref[:, n:]


def pair(a, b):
    return a * (a + 1) // 2 + b


def chain_kernel(swap_ref, k_ref, out_ref, k_s, w_s, low_s, work_s):
    n = k_ref.shape[-1]
    for i in range(k_ref.shape[0]):
        k_s[i] = k_ref[i]
    for s in range(PANELS):
        invert_block(k_s.at[pair(s, s)], w_s.at[s], work_s)
        w = w_s[s]
        for k in range(s):
            out_ref[pair(s, k)] = dot6(w, low_s[pair(s, k)])
        h = n // 2

        @pl.when(swap_ref[0] == 0)
        def _():
            out_ref[pair(s, s)] = w

        @pl.when(swap_ref[0] != 0)
        def _():
            out_ref[pair(s, s), :, :h] = w[:, h:]
            out_ref[pair(s, s), :, h:] = w[:, :h]

        for a in range(s + 1, PANELS):
            low_s[pair(a, s)] = dot6(k_s[pair(a, s)], w, 1)
        for a in range(s + 1, PANELS):
            for b in range(s + 1, a + 1):
                k_s[pair(a, b)] = k_s[pair(a, b)] - dot6(low_s[pair(a, s)], low_s[pair(b, s)], 1)


def chain(swap, corner):
    count, n, _ = corner.shape
    return pl.pallas_call(
        chain_kernel,
        out_shape=jax.ShapeDtypeStruct(corner.shape, jnp.float32),
        in_specs=[pl.BlockSpec(memory_space=pltpu.SMEM), pl.BlockSpec(memory_space=pltpu.VMEM)],
        out_specs=pl.BlockSpec(memory_space=pltpu.VMEM),
        scratch_shapes=[pltpu.VMEM((count, n, n), jnp.float32), pltpu.VMEM((PANELS, n, n), jnp.float32),
                        pltpu.VMEM((count, n, n), jnp.float32), pltpu.VMEM((n, 2 * n), jnp.float32)],
        interpret=INTERPRET,
    )(swap, corner)


def spec(space=pltpu.VMEM):
    return pl.BlockSpec(memory_space=space)


def f32(*shape):
    return jax.ShapeDtypeStruct(shape, jnp.float32)


def bf16(*shape):
    return jax.ShapeDtypeStruct(shape, jnp.bfloat16)


def gather_kernel(rows, cols, info, trailing, corner_keep, corner_give, *refs):
    keeps, (gives, sem) = refs[:PANELS], refs[PANELS:]
    my_row, my_col, mine = info[PANELS], info[PANELS + 1], info[PANELS + 2]
    half = NB // 2
    blk_cols = trailing.shape[1] // NB

    def copy(row, col, out):
        source = trailing.at[
            pl.ds(pl.multiple_of(row, half), half), pl.ds(pl.multiple_of(col, NB), NB)
        ]
        return pltpu.make_async_copy(source, out, sem)

    plans = []
    for a in range(PANELS):
        for b in range(a + 1):
            n = pair(a, b)
            owner = (lax.rem(info[a], rows) == my_row) & (lax.rem(info[b], cols) == my_col)
            per = PANELS * (PANELS + 1) // 4
            place = (n // per == mine, n % per)
            row, col = lax.div(info[a], rows) * NB, lax.div(info[b], cols) * NB
            for keep in (True, False):
                out = corner_keep if keep else corner_give
                jobs = [(row + h * half, col, out.at[2 * place[1] + h]) for h in range(2)]
                plans.append((place[0] == keep, owner, jobs))
    for s in range(PANELS):
        owner = lax.rem(info[s], rows) == my_row
        row = lax.div(info[s], rows) * NB
        jobs = []
        for j in range(blk_cols):
            jobs.append((row + mine * half, j * NB, keeps[s].at[j]))
            jobs.append((row + (1 - mine) * half, j * NB, gives.at[s * blk_cols + j]))
        plans.append((True, owner, jobs))
    for there, owner, jobs in plans:

        @pl.when(there & owner)
        def _():
            for job in jobs:
                copy(*job).start()

        @pl.when(there & jnp.logical_not(owner))
        def _():
            for _, _, out in jobs:
                out[...] = jnp.zeros_like(out)

    for there, owner, jobs in plans:

        @pl.when(there & owner)
        def _():
            for job in jobs:
                copy(*job).wait()


def gather(info, trailing, rows, cols):
    half = NB // 2
    blk_cols = trailing.shape[1] // NB
    part = f32(PANELS * (PANELS + 1) // 2, half, NB)
    shapes = [part, part] + [f32(blk_cols, half, NB)] * PANELS
    shapes.append(f32(PANELS * blk_cols, half, NB))
    return pl.pallas_call(
        lambda *refs: gather_kernel(rows, cols, *refs),
        out_shape=shapes,
        in_specs=[spec(pltpu.SMEM), spec(pl.ANY)],
        out_specs=[spec()] * len(shapes),
        scratch_shapes=[pltpu.SemaphoreType.DMA],
        interpret=INTERPRET,
        cost_estimate=pl.CostEstimate(flops=0, bytes_accessed=16 << 20, transcendentals=0),
    )(info, trailing)


def halves(x):
    high = x.astype(jnp.bfloat16)
    return high, (x - high.astype(jnp.float32)).astype(jnp.bfloat16)


def is_used(info, block, step):
    used = False
    for k in range(step):
        used = used | (block == info[k])
    return used


def col_kernel(s, cols, info, half, other, solved, *refs):
    before, outs = refs[:s], refs[s:]
    block = pl.program_id(0) * cols + info[PANELS + 1]
    fac = dot6(solved[pair(s, s)], jnp.concatenate([half[0], other[0]], axis=0))
    for k in range(s):
        fac = fac - dot6(solved[pair(s, k)], before[k][0])
    fac = jnp.where(is_used(info, block, s), 0.0, fac)
    if len(outs) == 3:
        outs[0][0] = fac
    high, low = halves(fac)
    outs[-2][0] = high
    outs[-1][0] = low


def col_factor(s, cols, info, half, other, solved, before):
    count = half.shape[0]
    last = s == PANELS - 1
    shapes = [] if last else [f32(count, NB, NB)]
    shapes += [bf16(count, NB, NB)] * 2
    part = pl.BlockSpec((1, NB // 2, NB), lambda i: (i, 0, 0))
    whole = pl.BlockSpec((1, NB, NB), lambda i: (i, 0, 0))
    return pl.pallas_call(
        lambda *refs: col_kernel(s, cols, *refs),
        grid=(count,),
        out_shape=shapes,
        in_specs=[spec(pltpu.SMEM), part, part, spec()] + [whole] * s,
        out_specs=[whole] * len(shapes),
        interpret=INTERPRET,
        cost_estimate=pl.CostEstimate(
            flops=12 * (s + 1) * count * NB**3, bytes_accessed=8 << 20, transcendentals=0
        ),
    )(info, half, other, solved, *before)


def row_kernel(s, rows, count, info, solved, *refs):
    sources, refs = refs[:count], refs[count:]
    before, (out, out_high, out_low, raw, sem) = refs[: min(s, 1)], refs[min(s, 1) :]
    step = pl.program_id(0)

    @pl.when(step == 0)
    def _():
        for which, source in enumerate(sources):

            @pl.when(info[PANELS + 3] == which)
            def _():
                copy = pltpu.make_async_copy(source, raw, sem)
                copy.start()
                copy.wait()

    block = step * rows + info[PANELS]
    full = jnp.concatenate([raw[0, step], raw[1, step]], axis=0)
    fac = dot6(full.T, solved[pair(s, s)], 1)
    for k in range(s):
        fac = fac - dot6(before[0][:, k * NB : (k + 1) * NB], solved[pair(s, k)], 1)
    fac = jnp.where(is_used(info, block, s), 0.0, fac)
    out[...] = fac
    out_high[...], out_low[...] = halves(fac)


def row_factor(s, rows, info, sources, solved, before):
    raw = sources[0].shape
    count = raw[1]
    height = count * NB
    width = PANELS * NB
    column = pl.BlockSpec((NB, NB), lambda i: (i, 0))
    return pl.pallas_call(
        lambda *refs: row_kernel(s, rows, len(sources), *refs),
        grid=(count,),
        out_shape=[f32(height, width), bf16(height, NB), bf16(height, NB)],
        in_specs=[spec(pltpu.SMEM), spec()]
        + [spec(pl.ANY)] * len(sources)
        + [pl.BlockSpec((NB, width), lambda i: (i, 0))] * len(before),
        out_specs=[pl.BlockSpec((NB, NB), lambda i: (i, s)), column, column],
        scratch_shapes=[pltpu.VMEM(raw, jnp.float32), pltpu.SemaphoreType.DMA],
        input_output_aliases={2 + len(sources): 0} if before else {},
        interpret=INTERPRET,
        cost_estimate=pl.CostEstimate(
            flops=12 * (s + 1) * count * NB**3, bytes_accessed=8 << 20, transcendentals=0
        ),
    )(info, solved, *sources, *before)


def own_kernel(ratio, info, half, other, out, sem):
    group = info[PANELS + 4]
    copies = []
    for h, part in enumerate((half, other)):
        for i in range(out.shape[1]):
            copies.append(
                pltpu.make_async_copy(part.at[i * ratio + group], out.at[h, i], sem)
            )
    for copy in copies:
        copy.start()
    for copy in copies:
        copy.wait()


def own_rows(ratio, info, half, other):
    return pl.pallas_call(
        lambda *refs: own_kernel(ratio, *refs),
        out_shape=f32(2, half.shape[0] // ratio, *half.shape[1:]),
        in_specs=[spec(pltpu.SMEM), spec(pl.ANY), spec(pl.ANY)],
        out_specs=spec(),
        scratch_shapes=[pltpu.SemaphoreType.DMA],
        interpret=INTERPRET,
        cost_estimate=pl.CostEstimate(flops=0, bytes_accessed=2 << 20, transcendentals=0),
    )(info, half, other)


def update_kernel(last, rows, cols, info, current, *refs):
    parts, out = refs[:-1], refs[-1]
    total = None
    for k in range(len(parts) // 4):
        rhigh, rlow, chigh, clow = parts[4 * k : 4 * k + 4]
        for left, right in ((rhigh, clow), (rlow, chigh), (rhigh, chigh)):
            term = jnp.dot(left[...], right[0], preferred_element_type=jnp.float32)
            total = term if total is None else total + term
    value = current[...] - total
    if not last:
        out[...] = value
        return
    dead = is_used(info, pl.program_id(0) * cols + info[PANELS + 1], PANELS)
    for i in range(value.shape[0] // NB):
        used = dead | is_used(info, i * rows + info[PANELS], PANELS)
        at = slice(i * NB, (i + 1) * NB)
        out[at, :] = jnp.where(used, 0.0, value[at])


def update(last, rows, cols, info, current, parts):
    height, width = current.shape
    strip = pl.BlockSpec((height, NB), lambda i: (0, i))
    block = pl.BlockSpec((1, NB, NB), lambda i: (i, 0, 0))
    return pl.pallas_call(
        lambda *refs: update_kernel(last, rows, cols, *refs),
        grid=(width // NB,),
        out_shape=f32(height, width),
        in_specs=[spec(pltpu.SMEM), strip] + [spec(), spec(), block, block] * (len(parts) // 4),
        out_specs=strip,
        input_output_aliases={1: 0} if last else {},
        interpret=INTERPRET,
        cost_estimate=pl.CostEstimate(
            flops=6 * (len(parts) // 4) * height * width * NB,
            bytes_accessed=24 << 20,
            transcendentals=0,
        ),
    )(info, current, *parts)


class Net:
    def __init__(self, rows, cols):
        self.rows, self.cols = rows, cols
        self.row_bits = [1 << i for i in range(1, rows.bit_length() - 1)]
        self.col_bits = [1 << i for i in range(cols.bit_length() - 1)]

    def send(self, value, target):
        pairs = []
        for r in range(self.rows):
            for c in range(self.cols):
                to = target(r, c)
                if to is not None:
                    pairs.append((r * self.cols + c, to[0] * self.cols + to[1]))
        return lax.ppermute(value, AXES, pairs)

    def core(self, value):
        return self.send(value, lambda r, c: (r ^ 1, c))

    def step_bit(self, step, core):
        return self.row_bits[(step + core) % len(self.row_bits)]

    def row_step(self, value, step, turn=0):
        return self.send(value, lambda r, c: (r ^ self.step_bit(step, (r + turn) & 1), c))

    def col_step(self, value, bit):
        return self.send(value, lambda r, c: (r, c ^ bit))

    def my_bit(self, my_row, mine, step, turn):
        even = (my_row & self.step_bit(step, turn)) != 0
        odd = (my_row & self.step_bit(step, 1 - turn)) != 0
        return jnp.where(mine == 0, even, odd).astype(jnp.int32)


def pick(value, index):
    return lax.dynamic_index_in_dim(value, index, 0, keepdims=False)


def spread_corner(net, part, my_row, mine):
    tail = part.shape[1:]
    bits = []
    turn = 1
    for step in range(len(net.row_bits)):
        bit = net.my_bit(my_row, mine, step, turn)
        bits.append(bit)
        part = part.reshape((2, -1) + tail)
        part = pick(part, bit) + net.row_step(pick(part, 1 - bit), step, turn)
    for bit in net.col_bits:
        part = part + net.col_step(part, bit)
    for step in reversed(range(len(net.row_bits))):
        other = net.row_step(part, step, turn)
        low = bits[step] == 0
        part = jnp.concatenate([jnp.where(low, part, other), jnp.where(low, other, part)])
    other = net.core(part)
    low = mine == 0
    return jnp.concatenate([jnp.where(low, part, other), jnp.where(low, other, part)])


def spread_rows(net, source, is_source):
    if (net.rows, net.cols) != (8, 4):
        value = jnp.where(is_source, source, 0.0)
        for bit in net.col_bits:
            value = value + net.col_step(value, bit)
        return [value]

    def hop(first, second):
        def target(r, c):
            up = (r // 2) % 2 == 0
            line = c if up else 3 - c
            near = (r % 2 == 0) == up
            to = (first if near else second).get(line)
            if to is None:
                return None
            return (r, to if up else 3 - to)

        return target

    got1 = net.send(source, hop({0: 1}, {1: 2}))
    got2 = net.send(got1, hop({1: 2}, {2: 3}))
    third = jnp.where(is_source, source, got2)
    got3 = net.send(third, hop({2: 3}, {1: 0}))
    return [source, got1, got2, got3]


def source_code(net, my_row, my_col):
    if (net.rows, net.cols) != (8, 4):
        return jnp.int32(0)
    up = (my_row & 2) == 0
    line = jnp.where(up, my_col, 3 - my_col)
    near = ((my_row & 1) == 0) == up
    return jnp.where(near, line, (line + 3) & 3)


def run(panel, trailing):
    rows = lax.axis_size("row")
    cols = lax.axis_size("col")
    my_row = lax.axis_index("row")
    my_col = lax.axis_index("col")
    net = Net(rows, cols)
    mine = my_row & 1
    _, loc_cols = trailing.shape
    blk_cols = loc_cols // NB
    ratio = rows // cols
    half = NB // 2
    group = lax.div(my_row, cols)
    code = source_code(net, my_row, my_col)
    extra = jnp.stack([my_row, my_col, mine, code, group])
    info = jnp.concatenate([panel[:PANELS], extra])
    is_source = my_col == lax.rem(my_row, cols)

    corner, corner_give, *keeps, gives = gather(info, trailing, rows, cols)
    got = net.core(gives).reshape(PANELS, blk_cols, half, NB)
    corner = corner + net.core(corner_give)
    corner = spread_corner(net, corner.reshape(rows, -1, NB), my_row, mine)
    solved = chain(info[PANELS + 2 : PANELS + 3], corner.reshape(-1, NB, NB))

    parts, sources = [], []
    for s in range(PANELS):
        part = keeps[s] + got[s]
        for step in range(len(net.row_bits)):
            part = part + net.row_step(part, step)
        parts.append((part, net.core(part)))
        own = own_rows(ratio, info, *parts[s])
        sources.append(spread_rows(net, own, is_source))
    out, col_f, stacked = (), [], []
    for s in range(PANELS):
        fac = col_factor(s, cols, info, *parts[s], solved, col_f)
        if s < PANELS - 1:
            col_f.append(fac[0])
        out, *rfac = row_factor(s, rows, info, sources[s], solved, [out] if s else [])
        stacked += [*rfac, *fac[-2:]]
    current = update(False, rows, cols, info, trailing, stacked[:-4])
    current = update(True, rows, cols, info, current, stacked[-4:])
    return (out, current)


def solution(mesh):
    in_specs = (P(), P("row", "col"))
    out_specs = (P("row", None), P("row", "col"))
    return jax.shard_map(run, mesh=mesh, in_specs=in_specs, out_specs=out_specs, check_vma=False)
```

profile of v0, /device:TPU:14, one launch (start us, length us, event | category | flops | bytes accessed | tf_op | source)
XLA Modules:
  0.0 253.9 jit_solution(5657686976139043378)
XLA Ops:
  0.7 1.3 concatenate.12.refs_0_
  1.9 4.6 %shard_map.41 = (f32[6,128,256]{2,1,0:T(8,128)}, f32[6,128,256]{2,1,0:T(8,128)}, f32[8,128,256]{2,1,0:T(8,128)}, f32[8,128,256]{2,1,0:T(8,128)}, f32[8,128,256]{2,1,0:T(8,128)}, /*index=5*/f32[24,128,256]{2,1,0:T(8,128)}) custom-call(s32[8]{0:T(128)} %concatenate.12.refs_0_, f32[1024,2048]{1,0:T(8,128)} %refs_1_.3), custom_call_target="tpu_custom_call" | custom-call | bytes 16777216 | tf_op jit(solution)/shard_map/pallas_call | solution.py:207
  6.6 5.9 %collective-permute-done.8 = f32[24,128,256]{2,1,0:T(8,128)S(1)} collective-permute-done((f32[24,128,256]{2,1,0:T(8,128)}, f32[24,128,256]{2,1,0:T(8,128)S(1)}, u32[]{:S(2)}, u32[]{:S(2)}) %collective-permute-start.8) | collective-permute-done | bytes 3145760 | tf_op jit(solution)/shard_map/ppermute | solution.py:390
  12.5 2.3 slice_add_fusion
  14.8 1.9 collective-permute-start.21
  16.9 2.4 collective-permute-done
  19.3 1.5 add.62
  21.1 8.7 %collective-permute-done.21 = f32[8,128,256]{2,1,0:T(8,128)} collective-permute-done((f32[8,128,256]{2,1,0:T(8,128)S(1)}, f32[8,128,256]{2,1,0:T(8,128)}, u32[]{:S(2)}, u32[]{:S(2)}) %collective-permute-start.21) | collective-permute-done | bytes 1048608 | tf_op jit(solution)/shard_map/ppermute | solution.py:390
  29.8 1.7 add.78
  31.5 1.1 collective-permute-start.22
  32.7 1.0 collective-permute-start.1
  33.7 14.7 %collective-permute-done.15 = f32[8,128,256]{2,1,0:T(8,128)} collective-permute-done((f32[8,128,256]{2,1,0:T(8,128)S(1)}, f32[8,128,256]{2,1,0:T(8,128)}, u32[]{:S(2)}, u32[]{:S(2)}) %collective-permute-start.15) | collective-permute-done | bytes 1048608 | tf_op jit(solution)/shard_map/ppermute | solution.py:390
  48.4 2.3 add.75
  50.8 0.9 collective-permute-start.16
  51.7 14.5 %collective-permute-done.1 = f32[4,96,256]{2,1,0:T(8,128)} collective-permute-done((f32[4,96,256]{2,1,0:T(8,128)S(1)}, f32[4,96,256]{2,1,0:T(8,128)}, u32[]{:S(2)}, u32[]{:S(2)}) %collective-permute-start.1) | collective-permute-done | bytes 393248 | tf_op jit(solution)/shard_map/ppermute | solution.py:390
  66.1 1.0 bitcast_add_fusion
  67.2 0.7 dynamic-slice_bitcast_fusion.1
  67.9 1.8 collective-permute-start.2
  69.7 1.2 collective-permute-done.9
  70.9 1.4 add.72
  72.3 1.0 collective-permute-start.10
  73.2 1.4 add.79.refs_1_
  74.7 1.3 collective-permute-done.2
  76.0 1.0 bitcast_add_fusion.1
  77.4 5.6 %collective-permute-done.3 = f32[2,96,256]{2,1,0:T(8,128)S(1)} collective-permute-done((f32[2,96,256]{2,1,0:T(8,128)S(1)}, f32[2,96,256]{2,1,0:T(8,128)S(1)}, u32[]{:S(2)}, u32[]{:S(2)}) %collective-permute-start.3) | collective-permute-done | bytes 196640 | tf_op jit(solution)/shard_map/ppermute | solution.py:390
  83.0 2.6 %collective-permute-start.4 = (f32[2,96,256]{2,1,0:T(8,128)S(1)}, f32[2,96,256]{2,1,0:T(8,128)S(1)}, u32[]{:S(2)}, u32[]{:S(2)}) collective-permute-start(f32[2,96,256]{2,1,0:T(8,128)S(1)} %add.69), channel_id=1, source_target_pairs={{0,2},{1,3},{2,0},{3,1},{4,6},{5,7},{6,4},{7,5},{8,10},{9,11},{10,... | collective-permute-start | bytes 589832 | tf_op jit(solution)/shard_map/ppermute | solution.py:390
  85.7 1.7 add.76.refs_1_
  87.5 5.1 %collective-permute-done.4 = f32[2,96,256]{2,1,0:T(8,128)S(1)} collective-permute-done((f32[2,96,256]{2,1,0:T(8,128)S(1)}, f32[2,96,256]{2,1,0:T(8,128)S(1)}, u32[]{:S(2)}, u32[]{:S(2)}) %collective-permute-start.4) | collective-permute-done | bytes 196640 | tf_op jit(solution)/shard_map/ppermute | solution.py:390
  92.6 0.7 collective-permute-start.5
  93.3 5.1 %collective-permute-done.5 = f32[2,96,256]{2,1,0:T(8,128)} collective-permute-done((f32[2,96,256]{2,1,0:T(8,128)S(1)}, f32[2,96,256]{2,1,0:T(8,128)}, u32[]{:S(2)}, u32[]{:S(2)}) %collective-permute-start.5) | collective-permute-done | bytes 196640 | tf_op jit(solution)/shard_map/ppermute | solution.py:390
  98.5 1.1 broadcast_select_fusion.8
  99.5 2.4 add.73.refs_1_
  101.9 2.0 collective-permute-start.6
  104.0 2.9 %shard_map.45.refs_2_ = f32[2,4,128,256]{3,2,1,0:T(8,128)} custom-call(s32[8]{0:T(128)} %concatenate.12.refs_0_, f32[8,128,256]{2,1,0:T(8,128)} %copy-done.3, f32[8,128,256]{2,1,0:T(8,128)} %collective-permute-done.23.refs_2_), custom_call_target="tpu_custom_call" | custom-call | bytes 2097152 | tf_op jit(solution)/shard_map/pallas_call | solution.py:327
  106.9 1.3 collective-permute-start.24
  108.2 3.0 %shard_map.44.refs_2_ = f32[2,4,128,256]{3,2,1,0:T(8,128)} custom-call(s32[8]{0:T(128)} %concatenate.12.refs_0_, f32[8,128,256]{2,1,0:T(8,128)} %copy-done.4, f32[8,128,256]{2,1,0:T(8,128)} %collective-permute-done.17.refs_2_), custom_call_target="tpu_custom_call" | custom-call | bytes 2097152 | tf_op jit(solution)/shard_map/pallas_call | solution.py:327
  111.2 1.3 collective-permute-start.18
  112.5 1.1 broadcast_select_fusion.6
  113.7 2.9 %shard_map.43.refs_2_ = f32[2,4,128,256]{3,2,1,0:T(8,128)} custom-call(s32[8]{0:T(128)} %concatenate.12.refs_0_, f32[8,128,256]{2,1,0:T(8,128)} %add.73.refs_1_, f32[8,128,256]{2,1,0:T(8,128)} %collective-permute-done.11.refs_2_), custom_call_target="tpu_custom_call" | custom-call | bytes 2097152 | tf_op jit(solution)/shard_map/pallas_call | solution.py:327
  116.7 1.3 collective-permute-start.12
  118.0 6.0 %collective-permute-done.24.refs_3_ = f32[2,4,128,256]{3,2,1,0:T(8,128)} collective-permute-done((f32[2,4,128,256]{3,2,1,0:T(8,128)}, f32[2,4,128,256]{3,2,1,0:T(8,128)}, u32[]{:S(2)}, u32[]{:S(2)}) %collective-permute-start.24) | collective-permute-done | bytes 1048608 | tf_op jit(solution)/shard_map/ppermute | solution.py:390
  123.9 2.3 collective-permute-start.25
  126.2 18.4 %collective-permute-done.18.refs_3_ = f32[2,4,128,256]{3,2,1,0:T(8,128)} collective-permute-done((f32[2,4,128,256]{3,2,1,0:T(8,128)}, f32[2,4,128,256]{3,2,1,0:T(8,128)}, u32[]{:S(2)}, u32[]{:S(2)}) %collective-permute-start.18) | collective-permute-done | bytes 1048608 | tf_op jit(solution)/shard_map/ppermute | solution.py:390
  144.6 1.3 collective-permute-start.19
  146.1 1.2 pad_maximum_fusion
  147.4 14.7 %shard_map.42.refs_1_.refs_3_ = f32[6,256,256]{2,1,0:T(8,128)} custom-call(s32[1]{0:T(128)} %bitcast.2.swap_ref, f32[6,256,256]{2,1,0:T(8,128)} %bitcast.17), custom_call_target="tpu_custom_call" | custom-call | tf_op jit(solution)/shard_map/pallas_call | solution.py:126
  162.1 5.0 %collective-permute-done.12.refs_3_ = f32[2,4,128,256]{3,2,1,0:T(8,128)} collective-permute-done((f32[2,4,128,256]{3,2,1,0:T(8,128)}, f32[2,4,128,256]{3,2,1,0:T(8,128)}, u32[]{:S(2)}, u32[]{:S(2)}) %collective-permute-start.12) | collective-permute-done | bytes 1048608 | tf_op jit(solution)/shard_map/ppermute | solution.py:390
  167.1 2.3 collective-permute-start.13
  169.4 8.0 %shard_map.49 = (f32[8,256,256]{2,1,0:T(8,128)}, bf16[8,256,256]{2,1,0:T(8,128)(2,1)}, bf16[8,256,256]{2,1,0:T(8,128)(2,1)}) custom-call(s32[8]{0:T(128)} %concatenate.12.refs_0_, f32[8,128,256]{2,1,0:T(8,128)} %copy-done.3, f32[8,128,256]{2,1,0:T(8,128)} %collective-permute-done.23.refs_2_, f32[6,256,256]{2,1,0:T(8,128)} %shard_map.42.refs_1_.refs_3_), custom_call_target="tpu_custom_call" | custom-call | flops 1610612736 | bytes 8388608 | tf_op jit(solution)/shard_map/pallas_call | solution.py:251
  177.4 2.4 broadcast_select_fusion
  179.8 1.7 collective-permute-start.26
  181.5 1.3 broadcast_select_fusion.1
  182.7 0.9 collective-permute-start.20
  183.7 9.6 %shard_map.50 = (f32[8,256,256]{2,1,0:T(8,128)}, bf16[8,256,256]{2,1,0:T(8,128)(2,1)}, bf16[8,256,256]{2,1,0:T(8,128)(2,1)}) custom-call(s32[8]{0:T(128)} %concatenate.12.refs_0_, f32[8,128,256]{2,1,0:T(8,128)} %copy-done.4, f32[8,128,256]{2,1,0:T(8,128)} %collective-permute-done.17.refs_2_, f32[6,256,256]{2,1,0:T(8,128)} %shard_map.42.refs_1_.refs_3_, ...), custom_call_target="tpu_custom_call" | custom-call | flops 3221225472 | bytes 8388608 | tf_op jit(solution)/shard_map/pallas_call | solution.py:251
  193.2 1.4 broadcast_select_fusion.2
  194.6 0.7 collective-permute-start.14
  195.4 10.5 %shard_map.52 = (bf16[8,256,256]{2,1,0:T(8,128)(2,1)}, bf16[8,256,256]{2,1,0:T(8,128)(2,1)}) custom-call(s32[8]{0:T(128)} %concatenate.12.refs_0_, f32[8,128,256]{2,1,0:T(8,128)} %add.73.refs_1_, f32[8,128,256]{2,1,0:T(8,128)} %collective-permute-done.11.refs_2_, f32[6,256,256]{2,1,0:T(8,128)} %shard_map.42.refs_1_.refs_3_, ...), custom_call_target="tpu_custom_call" | custom-call | flops 4831838208 | bytes 8388608 | tf_op jit(solution)/shard_map/pallas_call | solution.py:251
  205.8 5.6 %shard_map.46 = (f32[1024,768]{1,0:T(8,128)}, bf16[1024,256]{1,0:T(8,128)(2,1)}, bf16[1024,256]{1,0:T(8,128)(2,1)}) custom-call(s32[8]{0:T(128)} %concatenate.12.refs_0_, f32[6,256,256]{2,1,0:T(8,128)} %shard_map.42.refs_1_.refs_3_, f32[2,4,128,256]{3,2,1,0:T(8,128)} %shard_map.45.refs_2_, f32[2,4,128,256]{3,2,1,0:T(8,128)} %collective-permute-done.24.refs_3_, ...), custom_call_target="tpu_custom_call" | custom-call | flops 805306368 | bytes 8388608 | tf_op jit(solution)/shard_map/pallas_call | solution.py:295
  211.4 1.0 copy-done.9
  212.4 7.1 %shard_map.47 = (f32[1024,768]{1,0:T(8,128)}, bf16[1024,256]{1,0:T(8,128)(2,1)}, bf16[1024,256]{1,0:T(8,128)(2,1)}) custom-call(s32[8]{0:T(128)} %concatenate.12.refs_0_, f32[6,256,256]{2,1,0:T(8,128)} %shard_map.42.refs_1_.refs_3_, f32[2,4,128,256]{3,2,1,0:T(8,128)} %shard_map.44.refs_2_, ...), custom_call_target="tpu_custom_call", output_to_operand_aliasing={{0}: (6, {})} | custom-call | flops 1610612736 | bytes 8388608 | tf_op jit(solution)/shard_map/pallas_call | solution.py:295
  219.5 13.7 %shard_map.51.refs_1_ = f32[1024,2048]{1,0:T(8,128)} custom-call(s32[8]{0:T(128)} %concatenate.12.refs_0_, f32[1024,2048]{1,0:T(8,128)} %refs_1_.3, bf16[1024,256]{1,0:T(8,128)(2,1)} %get-tuple-element.34.refs_2_, bf16[1024,256]{1,0:T(8,128)(2,1)} %get-tuple-element.35.refs_3_, bf16[8,256,256]{2,1,0:T(8,128)(2,1)} %get-tuple-element.36.refs_4_, ...), custom_call_target="tpu_custom_call" | custom-call | flops 6442450944 | bytes 25165824 | tf_op jit(solution)/shard_map/pallas_call | solution.py:361
  233.2 1.0 copy-done.11
  234.2 7.7 %shard_map.48 = (f32[1024,768]{1,0:T(8,128)}, bf16[1024,256]{1,0:T(8,128)(2,1)}, bf16[1024,256]{1,0:T(8,128)(2,1)}) custom-call(s32[8]{0:T(128)} %concatenate.12.refs_0_, f32[6,256,256]{2,1,0:T(8,128)} %shard_map.42.refs_1_.refs_3_, f32[2,4,128,256]{3,2,1,0:T(8,128)} %shard_map.43.refs_2_, ...), custom_call_target="tpu_custom_call", output_to_operand_aliasing={{0}: (6, {})} | custom-call | flops 2415919104 | bytes 8388608 | tf_op jit(solution)/shard_map/pallas_call | solution.py:295
  241.9 12.0 %shard_map.53 = f32[1024,2048]{1,0:T(8,128)} custom-call(s32[8]{0:T(128)} %concatenate.12.refs_0_, f32[1024,2048]{1,0:T(8,128)} %shard_map.51.refs_1_, bf16[1024,256]{1,0:T(8,128)(2,1)} %get-tuple-element.43.refs_2_, bf16[1024,256]{1,0:T(8,128)(2,1)} %get-tuple-element.44.refs_3_, ...), custom_call_target="tpu_custom_call", output_to_operand_aliasing={{}: (1, {})} | custom-call | flops 3221225472 | bytes 25165824 | tf_op jit(solution)/shard_map/pallas_call | solution.py:361
  (51 shorter events, 1.7 us)
Async XLA Ops:
  6.5 5.9 %collective-permute-start.8 = (f32[24,128,256]{2,1,0:T(8,128)}, f32[24,128,256]{2,1,0:T(8,128)S(1)}, u32[]{:S(2)}, u32[]{:S(2)}) collective-permute-start(f32[24,128,256]{2,1,0:T(8,128)} %get-tuple-element.28), channel_id=1, source_target_pairs={{0,4},{1,5},{2,6},{3,7},{4,0},{5,1},{6,2},{7,3},{8,12},{9,13},{10,... | collective-permute-start | bytes 9437192 | tf_op jit(solution)/shard_map/ppermute | solution.py:390
  14.8 6.3 %copy-start.2 = (f32[8,128,256]{2,1,0:T(8,128)}, f32[8,128,256]{2,1,0:T(8,128)S(1)}, u32[]{:S(2)}) copy-start(f32[8,128,256]{2,1,0:T(8,128)S(1)} %get-tuple-element.48) | copy-start | bytes 3145732
  14.8 15.0 %collective-permute-start.21 = (f32[8,128,256]{2,1,0:T(8,128)S(1)}, f32[8,128,256]{2,1,0:T(8,128)}, u32[]{:S(2)}, u32[]{:S(2)}) collective-permute-start(f32[8,128,256]{2,1,0:T(8,128)S(1)} %get-tuple-element.48), channel_id=1, source_target_pairs={{0,8},{1,9},{2,10},{3,11},{4,20},{5,21},{6,22},{7,23},{8,0},{9,1},... | collective-permute-start | bytes 3145736 | tf_op jit(solution)/shard_map/ppermute | solution.py:390
  16.7 2.6 %collective-permute-start = (f32[6,128,256]{2,1,0:T(8,128)}, f32[6,128,256]{2,1,0:T(8,128)}, u32[]{:S(2)}, u32[]{:S(2)}) collective-permute-start(f32[6,128,256]{2,1,0:T(8,128)} %get-tuple-element.26), channel_id=1, source_target_pairs={{0,4},{1,5},{2,6},{3,7},{4,0},{5,1},{6,2},{7,3},{8,12},{9,13},{10,... | collective-permute-start | bytes 2359304 | tf_op jit(solution)/shard_map/ppermute | solution.py:390
  16.7 31.7 %collective-permute-start.15 = (f32[8,128,256]{2,1,0:T(8,128)S(1)}, f32[8,128,256]{2,1,0:T(8,128)}, u32[]{:S(2)}, u32[]{:S(2)}) collective-permute-start(f32[8,128,256]{2,1,0:T(8,128)S(1)} %get-tuple-element.49), channel_id=1, source_target_pairs={{0,8},{1,9},{2,10},{3,11},{4,20},{5,21},{6,22},{7,23},{8,0},{9,1},... | collective-permute-start | bytes 3145736 | tf_op jit(solution)/shard_map/ppermute | solution.py:390
  20.8 11.8 %copy-start.7 = (f32[6,128,256]{2,1,0:T(8,128)}, f32[6,128,256]{2,1,0:T(8,128)S(1)}, u32[]{:S(2)}) copy-start(f32[6,128,256]{2,1,0:T(8,128)S(1)} %add.62) | copy-start | bytes 2359300
  20.8 50.1 %collective-permute-start.9 = (f32[8,128,256]{2,1,0:T(8,128)S(1)}, f32[8,128,256]{2,1,0:T(8,128)}, u32[]{:S(2)}, u32[]{:S(2)}) collective-permute-start(f32[8,128,256]{2,1,0:T(8,128)S(1)} %get-tuple-element.50), channel_id=1, source_target_pairs={{0,8},{1,9},{2,10},{3,11},{4,20},{5,21},{6,22},{7,23},{8,0},{9,1},... | collective-permute-start | bytes 3145736 | tf_op jit(solution)/shard_map/ppermute | solution.py:390
  31.5 41.7 %collective-permute-start.22 = (f32[8,128,256]{2,1,0:T(8,128)S(1)}, f32[8,128,256]{2,1,0:T(8,128)}, u32[]{:S(2)}, u32[]{:S(2)}) collective-permute-start(f32[8,128,256]{2,1,0:T(8,128)S(1)} %add.78), channel_id=1, source_target_pairs={{0,16},{1,17},{2,18},{3,19},{4,12},{5,13},{6,14},{7,15},{8,24},{9,... | collective-permute-start | bytes 3145736 | tf_op jit(solution)/shard_map/ppermute | solution.py:390
  32.7 33.5 %collective-permute-start.1 = (f32[4,96,256]{2,1,0:T(8,128)S(1)}, f32[4,96,256]{2,1,0:T(8,128)}, u32[]{:S(2)}, u32[]{:S(2)}) collective-permute-start(f32[4,96,256]{2,1,0:T(8,128)S(1)} %dynamic-slice_bitcast_fusion), channel_id=1, source_target_pairs={{0,16},{1,17},{2,18},{3,19},{4,12},{5,13},{6,14},{7,15},{8,24},{9,... | collective-permute-start | bytes 1179656 | tf_op jit(solution)/shard_map/ppermute | solution.py:390
  33.7 32.4 %copy-start.8 = (f32[6,128,256]{2,1,0:T(8,128)S(1)}, f32[6,128,256]{2,1,0:T(8,128)}, u32[]{:S(2)}) copy-start(f32[6,128,256]{2,1,0:T(8,128)} %copy-done.7) | copy-start | bytes 2359300
  50.8 34.9 %collective-permute-start.16 = (f32[8,128,256]{2,1,0:T(8,128)}, f32[8,128,256]{2,1,0:T(8,128)}, u32[]{:S(2)}, u32[]{:S(2)}) collective-permute-start(f32[8,128,256]{2,1,0:T(8,128)} %add.75), channel_id=1, source_target_pairs={{0,16},{1,17},{2,18},{3,19},{4,12},{5,13},{6,14},{7,15},{8,24},{9,... | collective-permute-start | bytes 3145736 | tf_op jit(solution)/shard_map/ppermute | solution.py:390
  67.9 8.1 %collective-permute-start.2 = (f32[2,96,256]{2,1,0:T(8,128)}, f32[2,96,256]{2,1,0:T(8,128)}, u32[]{:S(2)}, u32[]{:S(2)}) collective-permute-start(f32[2,96,256]{2,1,0:T(8,128)} %dynamic-slice_bitcast_fusion.1), channel_id=1, source_target_pairs={{0,8},{1,9},{2,10},{3,11},{4,20},{5,21},{6,22},{7,23},{8,0},{9,1},... | collective-permute-start | bytes 589832 | tf_op jit(solution)/shard_map/ppermute | solution.py:390
  72.3 27.3 %collective-permute-start.10 = (f32[8,128,256]{2,1,0:T(8,128)S(1)}, f32[8,128,256]{2,1,0:T(8,128)}, u32[]{:S(2)}, u32[]{:S(2)}) collective-permute-start(f32[8,128,256]{2,1,0:T(8,128)S(1)} %add.72), channel_id=1, source_target_pairs={{0,16},{1,17},{2,18},{3,19},{4,12},{5,13},{6,14},{7,15},{8,24},{9,... | collective-permute-start | bytes 3145736 | tf_op jit(solution)/shard_map/ppermute | solution.py:390
  74.6 27.3 %copy-start.3 = (f32[8,128,256]{2,1,0:T(8,128)}, f32[8,128,256]{2,1,0:T(8,128)S(1)}, u32[]{:S(2)}) copy-start(f32[8,128,256]{2,1,0:T(8,128)S(1)} %add.79.refs_1_) | copy-start | bytes 3145732
  74.6 29.4 %collective-permute-start.23 = (f32[8,128,256]{2,1,0:T(8,128)S(1)}, f32[8,128,256]{2,1,0:T(8,128)}, u32[]{:S(2)}, u32[]{:S(2)}) collective-permute-start(f32[8,128,256]{2,1,0:T(8,128)S(1)} %add.79.refs_1_), channel_id=1, source_target_pairs={{0,4},{1,5},{2,6},{3,7},{4,0},{5,1},{6,2},{7,3},{8,12},{9,13},{10,... | collective-permute-start | bytes 3145736 | tf_op jit(solution)/shard_map/ppermute | solution.py:390
  76.9 6.1 %collective-permute-start.3 = (f32[2,96,256]{2,1,0:T(8,128)S(1)}, f32[2,96,256]{2,1,0:T(8,128)S(1)}, u32[]{:S(2)}, u32[]{:S(2)}) collective-permute-start(f32[2,96,256]{2,1,0:T(8,128)S(1)} %bitcast_add_fusion.1), channel_id=1, source_target_pairs={{0,1},{1,0},{2,3},{3,2},{4,5},{5,4},{6,7},{7,6},{8,9},{9,8},{10,11... | collective-permute-start | bytes 589832 | tf_op jit(solution)/shard_map/ppermute | solution.py:390
  83.0 9.5 %collective-permute-start.4 = (f32[2,96,256]{2,1,0:T(8,128)S(1)}, f32[2,96,256]{2,1,0:T(8,128)S(1)}, u32[]{:S(2)}, u32[]{:S(2)}) collective-permute-start(f32[2,96,256]{2,1,0:T(8,128)S(1)} %add.69), channel_id=1, source_target_pairs={{0,2},{1,3},{2,0},{3,1},{4,6},{5,7},{6,4},{7,5},{8,10},{9,11},{10,... | collective-permute-start | bytes 589832 | tf_op jit(solution)/shard_map/ppermute | solution.py:390
  87.4 19.5 %copy-start.4 = (f32[8,128,256]{2,1,0:T(8,128)}, f32[8,128,256]{2,1,0:T(8,128)S(1)}, u32[]{:S(2)}) copy-start(f32[8,128,256]{2,1,0:T(8,128)S(1)} %add.76.refs_1_) | copy-start | bytes 3145732
  87.4 20.8 %collective-permute-start.17 = (f32[8,128,256]{2,1,0:T(8,128)S(1)}, f32[8,128,256]{2,1,0:T(8,128)}, u32[]{:S(2)}, u32[]{:S(2)}) collective-permute-start(f32[8,128,256]{2,1,0:T(8,128)S(1)} %add.76.refs_1_), channel_id=1, source_target_pairs={{0,4},{1,5},{2,6},{3,7},{4,0},{5,1},{6,2},{7,3},{8,12},{9,13},{10,... | collective-permute-start | bytes 3145736 | tf_op jit(solution)/shard_map/ppermute | solution.py:390
  92.6 0.7 copy-start.10
  92.6 5.8 %collective-permute-start.5 = (f32[2,96,256]{2,1,0:T(8,128)S(1)}, f32[2,96,256]{2,1,0:T(8,128)}, u32[]{:S(2)}, u32[]{:S(2)}) collective-permute-start(f32[2,96,256]{2,1,0:T(8,128)S(1)} %add.70), channel_id=1, source_target_pairs={{0,8},{1,9},{2,10},{3,11},{4,20},{5,21},{6,22},{7,23},{8,0},{9,1},... | collective-permute-start | bytes 589832 | tf_op jit(solution)/shard_map/ppermute | solution.py:390
  101.9 11.8 %collective-permute-start.11 = (f32[8,128,256]{2,1,0:T(8,128)}, f32[8,128,256]{2,1,0:T(8,128)}, u32[]{:S(2)}, u32[]{:S(2)}) collective-permute-start(f32[8,128,256]{2,1,0:T(8,128)} %add.73.refs_1_), channel_id=1, source_target_pairs={{0,4},{1,5},{2,6},{3,7},{4,0},{5,1},{6,2},{7,3},{8,12},{9,13},{10,... | collective-permute-start | bytes 3145736 | tf_op jit(solution)/shard_map/ppermute | solution.py:390
  101.9 10.6 %collective-permute-start.6 = (f32[4,96,256]{2,1,0:T(8,128)S(1)}, f32[4,96,256]{2,1,0:T(8,128)}, u32[]{:S(2)}, u32[]{:S(2)}) collective-permute-start(f32[4,96,256]{2,1,0:T(8,128)S(1)} %pad_maximum_fusion.2), channel_id=1, source_target_pairs={{0,16},{1,17},{2,18},{3,19},{4,12},{5,13},{6,14},{7,15},{8,24},{9,... | collective-permute-start | bytes 1179656 | tf_op jit(solution)/shard_map/ppermute | solution.py:390
  106.9 17.0 %collective-permute-start.24 = (f32[2,4,128,256]{3,2,1,0:T(8,128)}, f32[2,4,128,256]{3,2,1,0:T(8,128)}, u32[]{:S(2)}, u32[]{:S(2)}) collective-permute-start(f32[2,4,128,256]{3,2,1,0:T(8,128)} %shard_map.45.refs_2_), channel_id=1, source_target_pairs={{0,1},{5,6},{10,9},{15,14},{16,17},{21,22},{26,25},{31,30}} | collective-permute-start | bytes 3145736 | tf_op jit(solution)/shard_map/ppermute | solution.py:390
  111.2 33.4 %collective-permute-start.18 = (f32[2,4,128,256]{3,2,1,0:T(8,128)}, f32[2,4,128,256]{3,2,1,0:T(8,128)}, u32[]{:S(2)}, u32[]{:S(2)}) collective-permute-start(f32[2,4,128,256]{3,2,1,0:T(8,128)} %shard_map.44.refs_2_), channel_id=1, source_target_pairs={{0,1},{5,6},{10,9},{15,14},{16,17},{21,22},{26,25},{31,30}} | collective-permute-start | bytes 3145736 | tf_op jit(solution)/shard_map/ppermute | solution.py:390
  113.6 32.3 %collective-permute-start.7 = (f32[8,96,256]{2,1,0:T(8,128)S(1)}, f32[8,96,256]{2,1,0:T(8,128)S(1)}, u32[]{:S(2)}, u32[]{:S(2)}) collective-permute-start(f32[8,96,256]{2,1,0:T(8,128)S(1)} %pad_maximum_fusion.1), channel_id=1, source_target_pairs={{0,4},{1,5},{2,6},{3,7},{4,0},{5,1},{6,2},{7,3},{8,12},{9,13},{10,... | collective-permute-start | bytes 2359304 | tf_op jit(solution)/shard_map/ppermute | solution.py:390
  116.7 50.4 %collective-permute-start.12 = (f32[2,4,128,256]{3,2,1,0:T(8,128)}, f32[2,4,128,256]{3,2,1,0:T(8,128)}, u32[]{:S(2)}, u32[]{:S(2)}) collective-permute-start(f32[2,4,128,256]{3,2,1,0:T(8,128)} %shard_map.43.refs_2_), channel_id=1, source_target_pairs={{0,1},{5,6},{10,9},{15,14},{16,17},{21,22},{26,25},{31,30}} | collective-permute-start | bytes 3145736 | tf_op jit(solution)/shard_map/ppermute | solution.py:390
  123.9 53.5 %collective-permute-start.25 = (f32[2,4,128,256]{3,2,1,0:T(8,128)}, f32[2,4,128,256]{3,2,1,0:T(8,128)}, u32[]{:S(2)}, u32[]{:S(2)}) collective-permute-start(f32[2,4,128,256]{3,2,1,0:T(8,128)} %collective-permute-done.24.refs_3_), channel_id=1, source_target_pairs={{1,2},{6,7},{9,8},{14,13},{17,18},{22,23},{25,24},{30,29}} | collective-permute-start | bytes 3145736 | tf_op jit(solution)/shard_map/ppermute | solution.py:390
  144.6 36.8 %collective-permute-start.19 = (f32[2,4,128,256]{3,2,1,0:T(8,128)}, f32[2,4,128,256]{3,2,1,0:T(8,128)S(1)}, u32[]{:S(2)}, u32[]{:S(2)}) collective-permute-start(f32[2,4,128,256]{3,2,1,0:T(8,128)} %collective-permute-done.18.refs_3_), channel_id=1, source_target_pairs={{1,2},{6,7},{9,8},{14,13},{17,18},{22,23},{25,24},{30,29}} | collective-permute-start | bytes 3145736 | tf_op jit(solution)/shard_map/ppermute | solution.py:390
  162.1 15.3 %copy-start.1 = (f32[2,4,128,256]{3,2,1,0:T(8,128)S(1)}, f32[2,4,128,256]{3,2,1,0:T(8,128)}, u32[]{:S(2)}) copy-start(f32[2,4,128,256]{3,2,1,0:T(8,128)} %shard_map.45.refs_2_) | copy-start | bytes 3145732
  162.1 19.4 %copy-start = (f32[2,4,128,256]{3,2,1,0:T(8,128)S(1)}, f32[2,4,128,256]{3,2,1,0:T(8,128)}, u32[]{:S(2)}) copy-start(f32[2,4,128,256]{3,2,1,0:T(8,128)} %shard_map.44.refs_2_) | copy-start | bytes 3145732
  167.1 26.1 %collective-permute-start.13 = (f32[2,4,128,256]{3,2,1,0:T(8,128)}, f32[2,4,128,256]{3,2,1,0:T(8,128)}, u32[]{:S(2)}, u32[]{:S(2)}) collective-permute-start(f32[2,4,128,256]{3,2,1,0:T(8,128)} %collective-permute-done.12.refs_3_), channel_id=1, source_target_pairs={{1,2},{6,7},{9,8},{14,13},{17,18},{22,23},{25,24},{30,29}} | collective-permute-start | bytes 3145736 | tf_op jit(solution)/shard_map/ppermute | solution.py:390
  179.8 26.0 %collective-permute-start.26 = (f32[2,4,128,256]{3,2,1,0:T(8,128)}, f32[2,4,128,256]{3,2,1,0:T(8,128)}, u32[]{:S(2)}, u32[]{:S(2)}) collective-permute-start(f32[2,4,128,256]{3,2,1,0:T(8,128)} %broadcast_select_fusion), channel_id=1, source_target_pairs={{2,3},{5,4},{10,11},{13,12},{18,19},{21,20},{26,27},{29,28}} | collective-permute-start | bytes 3145736 | tf_op jit(solution)/shard_map/ppermute | solution.py:390
  181.5 11.8 %copy-start.5 = (f32[2,4,128,256]{3,2,1,0:T(8,128)}, f32[2,4,128,256]{3,2,1,0:T(8,128)S(1)}, u32[]{:S(2)}) copy-start(f32[2,4,128,256]{3,2,1,0:T(8,128)S(1)} %collective-permute-done.19.refs_4_) | copy-start | bytes 3145732
  182.7 28.7 %collective-permute-start.20 = (f32[2,4,128,256]{3,2,1,0:T(8,128)}, f32[2,4,128,256]{3,2,1,0:T(8,128)S(1)}, u32[]{:S(2)}, u32[]{:S(2)}) collective-permute-start(f32[2,4,128,256]{3,2,1,0:T(8,128)} %broadcast_select_fusion.1), channel_id=1, source_target_pairs={{2,3},{5,4},{10,11},{13,12},{18,19},{21,20},{26,27},{29,28}} | collective-permute-start | bytes 3145736 | tf_op jit(solution)/shard_map/ppermute | solution.py:390
  183.7 9.6 %copy-start.6 = (f32[2,4,128,256]{3,2,1,0:T(8,128)S(1)}, f32[2,4,128,256]{3,2,1,0:T(8,128)}, u32[]{:S(2)}) copy-start(f32[2,4,128,256]{3,2,1,0:T(8,128)} %shard_map.43.refs_2_) | copy-start | bytes 3145732
  194.6 38.5 %collective-permute-start.14 = (f32[2,4,128,256]{3,2,1,0:T(8,128)S(1)}, f32[2,4,128,256]{3,2,1,0:T(8,128)S(1)}, u32[]{:S(2)}, u32[]{:S(2)}) collective-permute-start(f32[2,4,128,256]{3,2,1,0:T(8,128)S(1)} %broadcast_select_fusion.2), channel_id=1, source_target_pairs={{2,3},{5,4},{10,11},{13,12},{18,19},{21,20},{26,27},{29,28}} | collective-permute-start | bytes 3145736 | tf_op jit(solution)/shard_map/ppermute | solution.py:390
  211.4 1.0 copy-start.9
  233.2 1.0 copy-start.11
where the time goes:
time: 256 us; the launch traced here: 254 us
  Pallas kernels  102 us (40%)
  waiting for transfers between devices  93.9 us (37%)
  starting transfers between devices  27.4 us (11%)
  other arithmetic  25.3 us (10%)
  local copies, waits for them, and re-layouts  4.02 us (2%)
    ppermute x27, waiting for transfers between devices, send(): return lax.ppermute(value, AXES, pairs)  93.9 us
    pallas_call x3, Pallas kernels, col_factor(): pl.pallas_call(lambda *refs: col_kernel(s, cols, *refs), grid=(count,), o...  28.1 us
    ppermute x27, starting transfers between devices, send(): return lax.ppermute(value, AXES, pairs)  27.4 us
    pallas_call x2, Pallas kernels, update(): pl.pallas_call(lambda *refs: update_kernel(last, rows, cols, *refs), grid...  25.7 us
    pallas_call x3, Pallas kernels, row_factor(): pl.pallas_call(lambda *refs: row_kernel(s, rows, len(sources), *refs), gr...  20.4 us
    pallas_call x1, Pallas kernels, chain(): pl.pallas_call(chain_kernel, out_shape=jax.ShapeDtypeStruct(corner.shape,...  14.7 us
    add x6, other arithmetic, run(): part = part + net.row_step(part, step)  10.8 us
    pallas_call x3, Pallas kernels, own_rows(): pl.pallas_call(lambda *refs: own_kernel(ratio, *refs), out_shape=f32(2, h...  8.81 us
  transfers between devices with their start and end apart: 27, of which 13 were waited for; matrix products, arithmetic and copies ran while one was open for 9% of the time, Pallas kernels for 31%

commit v1 on v0

--- a/solution.py
+++ b/solution.py
@@ -10,6 +10,7 @@
 PANELS = 3
 AXES = ("row", "col")
 INTERPRET = False
+VMEM_LIMIT = 24 << 20
 
 
 def thirds(x):
@@ -19,20 +20,14 @@
     return high, mid, (rest - mid.astype(jnp.float32)).astype(jnp.bfloat16)
 
 
-def bdot(a, b, cb):
+def dot6(a, b, cb=0):
+    ah, am, al = thirds(a)
+    bh, bm, bl = thirds(b)
+    left = jnp.concatenate([am, al, ah, am, ah, ah], axis=1)
+    right = jnp.concatenate([bm, bh, bl, bh, bm, bh], axis=cb)
     return lax.dot_general(
-        a, b, (((1,), (cb,)), ((), ())), preferred_element_type=jnp.float32
+        left, right, (((1,), (cb,)), ((), ())), preferred_element_type=jnp.float32
     )
-
-
-def dot6(a, b, cb=0):
-    m = a.shape[0]
-    a3 = jnp.concatenate(thirds(a), axis=0)
-    high, mid, low = thirds(b)
-    one = bdot(a3, high, cb)
-    two = bdot(a3[: 2 * m], mid, cb)
-    small = bdot(a3[:m], low, cb) + two[m:] + one[2 * m :]
-    return (small + (two[:m] + one[m : 2 * m])) + one[:m]
 
 
 def iotas(shape):
@@ -227,86 +222,133 @@
     return used
 
 
-def col_kernel(s, cols, info, half, other, solved, *refs):
-    before, outs = refs[:s], refs[s:]
+def params():
+    return pltpu.CompilerParams(vmem_limit_bytes=VMEM_LIMIT)
+
+
+def cost(flops, mib):
+    return pl.CostEstimate(flops=flops, bytes_accessed=mib << 20, transcendentals=0)
+
+
+def block_of(name):
+    return pl.BlockSpec((1, NB, NB), lambda i: (pair(*name), 0, 0))
+
+
+def col_kernel(cols, info, *refs):
+    raw, solved, (parts, rest) = refs[: 2 * PANELS - 2], refs[2 * PANELS - 2 : -2], refs[-2:]
     block = pl.program_id(0) * cols + info[PANELS + 1]
-    fac = dot6(solved[pair(s, s)], jnp.concatenate([half[0], other[0]], axis=0))
-    for k in range(s):
-        fac = fac - dot6(solved[pair(s, k)], before[k][0])
-    fac = jnp.where(is_used(info, block, s), 0.0, fac)
-    if len(outs) == 3:
-        outs[0][0] = fac
-    high, low = halves(fac)
-    outs[-2][0] = high
-    outs[-1][0] = low
-
-
-def col_factor(s, cols, info, half, other, solved, before):
-    count = half.shape[0]
-    last = s == PANELS - 1
-    shapes = [] if last else [f32(count, NB, NB)]
-    shapes += [bf16(count, NB, NB)] * 2
+    facs = []
+    last = PANELS - 1
+    for s in range(last):
+        full = jnp.concatenate([raw[2 * s][0], raw[2 * s + 1][0]], axis=0)
+        fac = dot6(solved[pair(s, s)][0], full)
+        for k in range(s):
+            fac = fac - dot6(solved[pair(s, k)][0], facs[k])
+        facs.append(jnp.where(is_used(info, block, s), 0.0, fac))
+        for i, part in enumerate(halves(facs[s])):
+            at = (2 * s + i) * NB
+            parts[0, at : at + NB] = part
+    total = None
+    for k in range(last):
+        term = dot6(solved[pair(last, k)][0], facs[k])
+        total = term if total is None else total + term
+    rest[0] = total
+
+
+def col_factor(cols, info, raw, solved):
+    count = raw[0].shape[0]
+    last = PANELS - 1
+    names = [(a, b) for a in range(PANELS) for b in range(a + 1)][:-1]
     part = pl.BlockSpec((1, NB // 2, NB), lambda i: (i, 0, 0))
-    whole = pl.BlockSpec((1, NB, NB), lambda i: (i, 0, 0))
     return pl.pallas_call(
-        lambda *refs: col_kernel(s, cols, *refs),
+        lambda *refs: col_kernel(cols, *refs),
         grid=(count,),
-        out_shape=shapes,
-        in_specs=[spec(pltpu.SMEM), part, part, spec()] + [whole] * s,
-        out_specs=[whole] * len(shapes),
+        out_shape=[bf16(count, 2 * last * NB, NB), f32(count, NB, NB)],
+        in_specs=[spec(pltpu.SMEM)] + [part] * len(raw) + [block_of(n) for n in names],
+        out_specs=[
+            pl.BlockSpec((1, 2 * last * NB, NB), lambda i: (i, 0, 0)),
+            pl.BlockSpec((1, NB, NB), lambda i: (i, 0, 0)),
+        ],
+        compiler_params=params(),
         interpret=INTERPRET,
-        cost_estimate=pl.CostEstimate(
-            flops=12 * (s + 1) * count * NB**3, bytes_accessed=8 << 20, transcendentals=0
-        ),
-    )(info, half, other, solved, *before)
-
-
-def row_kernel(s, rows, count, info, solved, *refs):
+        cost_estimate=cost(60 * count * NB**3, 12),
+    )(info, *raw, *[solved] * len(names))
+
+
+def fetch(info, sources, raw, sem):
+    for which, source in enumerate(sources):
+
+        @pl.when(info[PANELS + 3] == which)
+        def _():
+            copy = pltpu.make_async_copy(source, raw, sem)
+            copy.start()
+            copy.wait()
+
+
+def row_kernel(s, rows, count, info, *refs):
     sources, refs = refs[:count], refs[count:]
-    before, (out, out_high, out_low, raw, sem) = refs[: min(s, 1)], refs[min(s, 1) :]
+    last = PANELS - 1
+    total = (s + 1) + (PANELS - 1 if s == last - 1 else 0)
+    solved, refs = refs[:total], refs[total:]
+    before, refs = refs[:s], refs[s:]
+    out, parts, raw, sem = refs[0], refs[1], refs[-2], refs[-1]
     step = pl.program_id(0)
 
     @pl.when(step == 0)
     def _():
-        for which, source in enumerate(sources):
-
-            @pl.when(info[PANELS + 3] == which)
-            def _():
-                copy = pltpu.make_async_copy(source, raw, sem)
-                copy.start()
-                copy.wait()
-
-    block = step * rows + info[PANELS]
+        fetch(info, sources, raw, sem)
+
     full = jnp.concatenate([raw[0, step], raw[1, step]], axis=0)
-    fac = dot6(full.T, solved[pair(s, s)], 1)
+    fac = dot6(full.T, solved[s][0], 1)
+    facs = [ref[...] for ref in before]
     for k in range(s):
-        fac = fac - dot6(before[0][:, k * NB : (k + 1) * NB], solved[pair(s, k)], 1)
-    fac = jnp.where(is_used(info, block, s), 0.0, fac)
+        fac = fac - dot6(facs[k], solved[k][0], 1)
+    fac = jnp.where(is_used(info, step * rows + info[PANELS], s), 0.0, fac)
     out[...] = fac
-    out_high[...], out_low[...] = halves(fac)
+    for i, part in enumerate(halves(fac)):
+        parts[:, i * NB : (i + 1) * NB] = part
+    if s == last - 1:
+        facs.append(fac)
+        rest = None
+        for k in range(last):
+            term = dot6(facs[k], solved[s + 1 + k][0], 1)
+            rest = term if rest is None else rest + term
+        refs[2][...] = rest
 
 
 def row_factor(s, rows, info, sources, solved, before):
     raw = sources[0].shape
     count = raw[1]
     height = count * NB
-    width = PANELS * NB
-    column = pl.BlockSpec((NB, NB), lambda i: (i, 0))
+    names = [(s, k) for k in range(s + 1)]
+    shapes = [f32(height, PANELS * NB), bf16(height, 2 * NB)]
+    specs = [
+        pl.BlockSpec((NB, NB), lambda i: (i, s)),
+        pl.BlockSpec((NB, 2 * NB), lambda i: (i, 0)),
+    ]
+    if s == PANELS - 2:
+        names += [(PANELS - 1, k) for k in range(PANELS - 1)]
+        shapes.append(f32(height, NB))
+        specs.append(pl.BlockSpec((NB, NB), lambda i: (i, 0)))
+
+    def column(k):
+        return pl.BlockSpec((NB, NB), lambda i: (i, k))
+
     return pl.pallas_call(
         lambda *refs: row_kernel(s, rows, len(sources), *refs),
         grid=(count,),
-        out_shape=[f32(height, width), bf16(height, NB), bf16(height, NB)],
-        in_specs=[spec(pltpu.SMEM), spec()]
+        out_shape=shapes,
+        in_specs=[spec(pltpu.SMEM)]
         + [spec(pl.ANY)] * len(sources)
-        + [pl.BlockSpec((NB, width), lambda i: (i, 0))] * len(before),
-        out_specs=[pl.BlockSpec((NB, NB), lambda i: (i, s)), column, column],
+        + [block_of(n) for n in names]
+        + [column(k) for k in range(s)],
+        out_specs=specs,
         scratch_shapes=[pltpu.VMEM(raw, jnp.float32), pltpu.SemaphoreType.DMA],
-        input_output_aliases={2 + len(sources): 0} if before else {},
+        input_output_aliases={1 + len(sources) + len(names): 0} if s else {},
+        compiler_params=params(),
         interpret=INTERPRET,
-        cost_estimate=pl.CostEstimate(
-            flops=12 * (s + 1) * count * NB**3, bytes_accessed=8 << 20, transcendentals=0
-        ),
-    )(info, solved, *sources, *before)
+        cost_estimate=cost(12 * len(names) * count * NB**3, 8),
+    )(info, *sources, *[solved] * len(names), *before * s)
 
 
 def own_kernel(ratio, info, half, other, out, sem):
@@ -335,43 +377,121 @@
     )(info, half, other)
 
 
-def update_kernel(last, rows, cols, info, current, *refs):
-    parts, out = refs[:-1], refs[-1]
-    total = None
-    for k in range(len(parts) // 4):
-        rhigh, rlow, chigh, clow = parts[4 * k : 4 * k + 4]
-        for left, right in ((rhigh, clow), (rlow, chigh), (rhigh, chigh)):
-            term = jnp.dot(left[...], right[0], preferred_element_type=jnp.float32)
-            total = term if total is None else total + term
-    value = current[...] - total
-    if not last:
-        out[...] = value
-        return
-    dead = is_used(info, pl.program_id(0) * cols + info[PANELS + 1], PANELS)
-    for i in range(value.shape[0] // NB):
+def set_left(left, parts):
+    for k, part in enumerate(parts):
+        for i, at in enumerate((0, 1, 0)):
+            to = (3 * k + i) * NB
+            left[:, to : to + NB] = part[:, at * NB : (at + 1) * NB]
+
+
+def early_kernel(info, current, cparts, *refs):
+    rparts, out, left = refs[:-2], refs[-2], refs[-1]
+
+    @pl.when(pl.program_id(0) == 0)
+    def _():
+        set_left(left, rparts)
+
+    blocks = []
+    for k in range(len(rparts)):
+        high = cparts[0, 2 * k * NB : (2 * k + 1) * NB]
+        low = cparts[0, (2 * k + 1) * NB : (2 * k + 2) * NB]
+        blocks += [low, high, high]
+    right = jnp.concatenate(blocks, axis=0)
+    out[...] = current[...] - jnp.dot(left[...], right, preferred_element_type=jnp.float32)
+
+
+def early_update(info, current, cparts, rparts):
+    height, width = current.shape
+    strip = pl.BlockSpec((height, NB), lambda i: (0, i))
+    return pl.pallas_call(
+        early_kernel,
+        grid=(width // NB,),
+        out_shape=f32(height, width),
+        in_specs=[
+            spec(pltpu.SMEM),
+            strip,
+            pl.BlockSpec((1,) + cparts.shape[1:], lambda i: (i, 0, 0)),
+        ]
+        + [spec()] * len(rparts),
+        out_specs=strip,
+        scratch_shapes=[pltpu.VMEM((height, 3 * len(rparts) * NB), jnp.bfloat16)],
+        compiler_params=params(),
+        interpret=INTERPRET,
+        cost_estimate=cost(12 * height * width * NB, 24),
+    )(info, current, cparts, *rparts)
+
+
+def last_kernel(rows, cols, count, info, *refs):
+    sources, refs = refs[:count], refs[count:]
+    current, half, other, rest, w, row_rest, _, out, fout = refs[:9]
+    raw, fac_s, parts, left, sem, out_sem = refs[9:]
+    last = PANELS - 1
+    step = pl.program_id(0)
+    blk_rows = raw.shape[1]
+    write = pltpu.make_async_copy(fac_s, fout.at[:, pl.ds(last * NB, NB)], out_sem)
+
+    @pl.when(step == 0)
+    def _():
+        fetch(info, sources, raw, sem)
+        for i in range(blk_rows):
+            at = slice(i * NB, (i + 1) * NB)
+            full = jnp.concatenate([raw[0, i], raw[1, i]], axis=0)
+            fac = dot6(full.T, w[0], 1) - row_rest[at]
+            fac = jnp.where(is_used(info, i * rows + info[PANELS], last), 0.0, fac)
+            fac_s[at] = fac
+            high, low = halves(fac)
+            parts[at, :NB] = high
+            parts[at, NB:] = low
+        set_left(left, [parts])
+
+    @pl.when(step == 1)
+    def _():
+        write.start()
+
+    block = step * cols + info[PANELS + 1]
+    fac = dot6(w[0], jnp.concatenate([half[0], other[0]], axis=0)) - rest[0]
+    high, low = halves(jnp.where(is_used(info, block, last), 0.0, fac))
+    right = jnp.concatenate([low, high, high], axis=0)
+    value = current[...] - jnp.dot(left[...], right, preferred_element_type=jnp.float32)
+    dead = is_used(info, block, PANELS)
+    for i in range(blk_rows):
         used = dead | is_used(info, i * rows + info[PANELS], PANELS)
         at = slice(i * NB, (i + 1) * NB)
         out[at, :] = jnp.where(used, 0.0, value[at])
 
-
-def update(last, rows, cols, info, current, parts):
+    @pl.when(step == pl.num_programs(0) - 1)
+    def _():
+        write.wait()
+
+
+def last_update(rows, cols, info, sources, current, raw, rest, solved, row_rest, out):
     height, width = current.shape
     strip = pl.BlockSpec((height, NB), lambda i: (0, i))
-    block = pl.BlockSpec((1, NB, NB), lambda i: (i, 0, 0))
+    part = pl.BlockSpec((1, NB // 2, NB), lambda i: (i, 0, 0))
+    last = PANELS - 1
+    count = len(sources)
     return pl.pallas_call(
-        lambda *refs: update_kernel(last, rows, cols, *refs),
+        lambda *refs: last_kernel(rows, cols, count, *refs),
         grid=(width // NB,),
-        out_shape=f32(height, width),
-        in_specs=[spec(pltpu.SMEM), strip] + [spec(), spec(), block, block] * (len(parts) // 4),
-        out_specs=strip,
-        input_output_aliases={1: 0} if last else {},
+        out_shape=[f32(height, width), f32(*out.shape)],
+        in_specs=[spec(pltpu.SMEM)]
+        + [spec(pl.ANY)] * count
+        + [strip, part, part, pl.BlockSpec((1, NB, NB), lambda i: (i, 0, 0))]
+        + [block_of((last, last)), spec(), spec(pl.ANY)],
+        out_specs=[strip, spec(pl.ANY)],
+        scratch_shapes=[
+            pltpu.VMEM(sources[0].shape, jnp.float32),
+            pltpu.VMEM((height, NB), jnp.float32),
+            pltpu.VMEM((height, 2 * NB), jnp.bfloat16),
+            pltpu.VMEM((height, 3 * NB), jnp.bfloat16),
+            pltpu.SemaphoreType.DMA,
+            pltpu.SemaphoreType.DMA,
+        ],
+        input_output_aliases={count + 7: 1},
+        compiler_params=params(),
         interpret=INTERPRET,
-        cost_estimate=pl.CostEstimate(
-            flops=6 * (len(parts) // 4) * height * width * NB,
-            bytes_accessed=24 << 20,
-            transcendentals=0,
-        ),
-    )(info, current, *parts)
+        cost_estimate=cost(6 * height * width * NB, 24),
+    )(info, *sources, current, *raw, rest, solved, row_rest, out)
 
 
 class Net:
@@ -414,7 +534,7 @@
 def spread_corner(net, part, my_row, mine):
     tail = part.shape[1:]
     bits = []
-    turn = 1
+    turn = 0
     for step in range(len(net.row_bits)):
         bit = net.my_bit(my_row, mine, step, turn)
         bits.append(bit)
@@ -497,15 +617,15 @@
         parts.append((part, net.core(part)))
         own = own_rows(ratio, info, *parts[s])
         sources.append(spread_rows(net, own, is_source))
-    out, col_f, stacked = (), [], []
-    for s in range(PANELS):
-        fac = col_factor(s, cols, info, *parts[s], solved, col_f)
-        if s < PANELS - 1:
-            col_f.append(fac[0])
-        out, *rfac = row_factor(s, rows, info, sources[s], solved, [out] if s else [])
-        stacked += [*rfac, *fac[-2:]]
-    current = update(False, rows, cols, info, trailing, stacked[:-4])
-    current = update(True, rows, cols, info, current, stacked[-4:])
+    cparts, col_rest = col_factor(cols, info, [v for p in parts[:-1] for v in p], solved)
+    out, rparts = (), []
+    for s in range(PANELS - 1):
+        out, *got = row_factor(s, rows, info, sources[s], solved, [out])
+        rparts.append(got[0])
+    current = early_update(info, trailing, cparts, rparts)
+    current, out = last_update(
+        rows, cols, info, sources[-1], current, parts[-1], col_rest, solved, got[1], out
+    )
     return (out, current)
 
 

time: 256 us -> 264 us (1.031)
  the two profiles are of different devices: /device:TPU:14 before, /device:TPU:2 now
where the time goes in v1:
time: 264 us; the launch traced here: 263 us
  waiting for transfers between devices  120 us (45%)
  Pallas kernels  85.5 us (32%)
  starting transfers between devices  30.5 us (12%)
  other arithmetic  22.5 us (9%)
  local copies, waits for them, and re-layouts  3.05 us (1%)
    ppermute x27, waiting for transfers between devices, send(): return lax.ppermute(value, AXES, pairs)  120 us
    ppermute x27, starting transfers between devices, send(): return lax.ppermute(value, AXES, pairs)  30.5 us
    pallas_call x1, Pallas kernels, col_factor(): pl.pallas_call(lambda *refs: col_kernel(cols, *refs), grid=(count,), out_...  18.2 us
    pallas_call x2, Pallas kernels, row_factor(): pl.pallas_call(lambda *refs: row_kernel(s, rows, len(sources), *refs), gr...  15.1 us
    pallas_call x1, Pallas kernels, chain(): pl.pallas_call(chain_kernel, out_shape=jax.ShapeDtypeStruct(corner.shape,...  14.8 us
    pallas_call x1, Pallas kernels, last_update(): pl.pallas_call(lambda *refs: last_kernel(rows, cols, count, *refs), grid=...  14.1 us
    add x6, other arithmetic, run(): part = part + net.row_step(part, step)  11.1 us
    pallas_call x1, Pallas kernels, early_update(): pl.pallas_call(early_kernel, grid=(width // NB,), out_shape=f32(height, w...  9.91 us
  transfers between devices with their start and end apart: 27, of which 12 were waited for; matrix products, arithmetic and copies ran while one was open for 8% of the time, Pallas kernels for 25%

profile of v1, /device:TPU:2, one launch (start us, length us, event | category | flops | bytes accessed | tf_op | source)
XLA Modules:
  0.0 263.2 jit_solution(12055944053622540753)
XLA Ops:
  0.7 1.3 concatenate.12.refs_0_.info
  1.9 4.6 %shard_map.41 = (f32[6,128,256]{2,1,0:T(8,128)}, f32[6,128,256]{2,1,0:T(8,128)}, f32[8,128,256]{2,1,0:T(8,128)}, f32[8,128,256]{2,1,0:T(8,128)}, f32[8,128,256]{2,1,0:T(8,128)}, /*index=5*/f32[24,128,256]{2,1,0:T(8,128)}) custom-call(s32[8]{0:T(128)} %concatenate.12.refs_0_.info, f32[1024,2048]{1,0:T(8,128)} %current.1), custom_call_target="tpu_custom_call" | custom-call | bytes 16777216 | tf_op jit(solution)/shard_map/pallas_call | solution.py:202
  6.5 1.0 collective-permute-start
  7.5 5.5 %collective-permute-done = f32[24,128,256]{2,1,0:T(8,128)S(1)} collective-permute-done((f32[24,128,256]{2,1,0:T(8,128)}, f32[24,128,256]{2,1,0:T(8,128)S(1)}, u32[]{:S(2)}, u32[]{:S(2)}) %collective-permute-start) | collective-permute-done | bytes 3145760 | tf_op jit(solution)/shard_map/ppermute | solution.py:510
  13.0 2.3 slice_add_fusion
  15.5 0.8 collective-permute-start.13
  16.3 1.8 collective-permute-start.7
  18.0 0.3 collective-permute-start.1
  18.3 0.2 collective-permute-done.13
  18.5 1.5 add.71
  20.0 10.3 %collective-permute-done.10 = f32[8,128,256]{2,1,0:T(8,128)} collective-permute-done((f32[8,128,256]{2,1,0:T(8,128)S(1)}, f32[8,128,256]{2,1,0:T(8,128)}, u32[]{:S(2)}, u32[]{:S(2)}) %collective-permute-start.10) | collective-permute-done | bytes 1048608 | tf_op jit(solution)/shard_map/ppermute | solution.py:510
  30.3 1.7 add.69
  32.1 1.0 collective-permute-start.11
  33.1 1.8 collective-permute-start.14
  34.9 13.9 %collective-permute-done.7 = f32[8,128,256]{2,1,0:T(8,128)} collective-permute-done((f32[8,128,256]{2,1,0:T(8,128)S(1)}, f32[8,128,256]{2,1,0:T(8,128)}, u32[]{:S(2)}, u32[]{:S(2)}) %collective-permute-start.7) | collective-permute-done | bytes 1048608 | tf_op jit(solution)/shard_map/ppermute | solution.py:510
  48.8 1.7 add.66
  50.5 1.2 collective-permute-start.8
  51.8 19.5 %collective-permute-done.1 = f32[8,128,256]{2,1,0:T(8,128)} collective-permute-done((f32[8,128,256]{2,1,0:T(8,128)S(1)}, f32[8,128,256]{2,1,0:T(8,128)}, u32[]{:S(2)}, u32[]{:S(2)}) %collective-permute-start.1) | collective-permute-done | bytes 1048608 | tf_op jit(solution)/shard_map/ppermute | solution.py:510
  71.3 2.3 add.63
  73.6 1.2 collective-permute-start.2
  74.8 4.9 %collective-permute-done.14 = f32[4,96,256]{2,1,0:T(8,128)} collective-permute-done((f32[4,96,256]{2,1,0:T(8,128)S(1)}, f32[4,96,256]{2,1,0:T(8,128)}, u32[]{:S(2)}, u32[]{:S(2)}) %collective-permute-start.14) | collective-permute-done | bytes 393248 | tf_op jit(solution)/shard_map/ppermute | solution.py:510
  79.7 1.0 bitcast_add_fusion
  80.8 0.7 dynamic-slice_bitcast_fusion.1
  81.5 1.2 collective-permute-start.15
  82.6 1.4 add.70.refs_3_.refs_1_
  84.1 8.2 %collective-permute-done.15 = f32[2,96,256]{2,1,0:T(8,128)} collective-permute-done((f32[2,96,256]{2,1,0:T(8,128)}, f32[2,96,256]{2,1,0:T(8,128)}, u32[]{:S(2)}, u32[]{:S(2)}) %collective-permute-start.15) | collective-permute-done | bytes 196640 | tf_op jit(solution)/shard_map/ppermute | solution.py:510
  92.2 1.0 bitcast_add_fusion.1
  93.2 1.6 collective-permute-start.16
  94.8 2.3 add.67.refs_1_
  97.2 0.1 collective-permute-start.9
  97.3 3.2 %collective-permute-done.16 = f32[2,96,256]{2,1,0:T(8,128)S(1)} collective-permute-done((f32[2,96,256]{2,1,0:T(8,128)S(1)}, f32[2,96,256]{2,1,0:T(8,128)S(1)}, u32[]{:S(2)}, u32[]{:S(2)}) %collective-permute-start.16) | collective-permute-done | bytes 196640 | tf_op jit(solution)/shard_map/ppermute | solution.py:510
  100.5 2.7 %collective-permute-start.17 = (f32[2,96,256]{2,1,0:T(8,128)S(1)}, f32[2,96,256]{2,1,0:T(8,128)S(1)}, u32[]{:S(2)}, u32[]{:S(2)}) collective-permute-start(f32[2,96,256]{2,1,0:T(8,128)S(1)} %add.78), channel_id=1, source_target_pairs={{0,2},{1,3},{2,0},{3,1},{4,6},{5,7},{6,4},{7,5},{8,10},{9,11},{10,... | collective-permute-start | bytes 589832 | tf_op jit(solution)/shard_map/ppermute | solution.py:510
  103.2 1.7 add.64.refs_1_.refs_6_
  105.0 7.1 %collective-permute-done.17 = f32[2,96,256]{2,1,0:T(8,128)S(1)} collective-permute-done((f32[2,96,256]{2,1,0:T(8,128)S(1)}, f32[2,96,256]{2,1,0:T(8,128)S(1)}, u32[]{:S(2)}, u32[]{:S(2)}) %collective-permute-start.17) | collective-permute-done | bytes 196640 | tf_op jit(solution)/shard_map/ppermute | solution.py:510
  112.1 1.3 collective-permute-start.18
  113.4 4.6 %collective-permute-done.18 = f32[2,96,256]{2,1,0:T(8,128)} collective-permute-done((f32[2,96,256]{2,1,0:T(8,128)S(1)}, f32[2,96,256]{2,1,0:T(8,128)}, u32[]{:S(2)}, u32[]{:S(2)}) %collective-permute-start.18) | collective-permute-done | bytes 196640 | tf_op jit(solution)/shard_map/ppermute | solution.py:510
  117.9 1.1 broadcast_select_fusion.8
  119.0 3.0 %shard_map.47.refs_1_ = f32[2,4,128,256]{3,2,1,0:T(8,128)} custom-call(s32[8]{0:T(128)} %concatenate.12.refs_0_.info, f32[8,128,256]{2,1,0:T(8,128)} %copy-done.6, f32[8,128,256]{2,1,0:T(8,128)} %collective-permute-done.12.refs_4_.refs_2_), custom_call_target="tpu_custom_call" | custom-call | bytes 2097152 | tf_op jit(solution)/shard_map/pallas_call | solution.py:369
  122.0 1.6 collective-permute-start.24
  123.7 3.0 %collective-permute-start.19 = (f32[4,96,256]{2,1,0:T(8,128)S(1)}, f32[4,96,256]{2,1,0:T(8,128)S(1)}, u32[]{:S(2)}, u32[]{:S(2)}) collective-permute-start(f32[4,96,256]{2,1,0:T(8,128)S(1)} %pad_maximum_fusion.2), channel_id=1, source_target_pairs={{0,8},{1,9},{2,10},{3,11},{4,20},{5,21},{6,22},{7,23},{8,0},{9,1},... | collective-permute-start | bytes 1179656 | tf_op jit(solution)/shard_map/ppermute | solution.py:510
  126.6 2.9 %shard_map.45.refs_1_ = f32[2,4,128,256]{3,2,1,0:T(8,128)} custom-call(s32[8]{0:T(128)} %concatenate.12.refs_0_.info, f32[8,128,256]{2,1,0:T(8,128)} %add.67.refs_1_, f32[8,128,256]{2,1,0:T(8,128)} %collective-permute-done.9.refs_2_), custom_call_target="tpu_custom_call" | custom-call | bytes 2097152 | tf_op jit(solution)/shard_map/pallas_call | solution.py:369
  129.6 1.6 collective-permute-start.21
  131.2 1.0 copy-done.8
  132.2 2.9 %shard_map.42.refs_1_ = f32[2,4,128,256]{3,2,1,0:T(8,128)} custom-call(s32[8]{0:T(128)} %concatenate.12.refs_0_.info, f32[8,128,256]{2,1,0:T(8,128)} %copy-done.1, f32[8,128,256]{2,1,0:T(8,128)} %copy-done.8), custom_call_target="tpu_custom_call" | custom-call | bytes 2097152 | tf_op jit(solution)/shard_map/pallas_call | solution.py:369
  135.1 1.7 collective-permute-start.4
  137.1 1.3 collective-permute-start.25
  138.4 1.3 collective-permute-start.22
  139.7 1.3 collective-permute-start.5
  141.0 0.1 broadcast_select_fusion.4
  141.1 1.2 pad_maximum_fusion
  142.4 14.8 %shard_map.43.refs_5_.refs_6_.refs_7_.refs_8_.refs_9_ = f32[6,256,256]{2,1,0:T(8,128)} custom-call(s32[1]{0:T(128)} %bitcast.2.swap_ref, f32[6,256,256]{2,1,0:T(8,128)} %bitcast.19), custom_call_target="tpu_custom_call" | custom-call | tf_op jit(solution)/shard_map/pallas_call | solution.py:121
  157.2 1.5 broadcast_select_fusion
  158.7 0.9 collective-permute-start.26
  159.6 19.5 %collective-permute-done.22.refs_3_ = f32[2,4,128,256]{3,2,1,0:T(8,128)} collective-permute-done((f32[2,4,128,256]{3,2,1,0:T(8,128)}, f32[2,4,128,256]{3,2,1,0:T(8,128)}, u32[]{:S(2)}, u32[]{:S(2)}) %collective-permute-start.22) | collective-permute-done | bytes 1048608 | tf_op jit(solution)/shard_map/ppermute | solution.py:510
  179.1 1.4 broadcast_select_fusion.1
  180.5 0.7 collective-permute-start.23
  181.2 23.3 %collective-permute-done.5.refs_3_ = f32[2,4,128,256]{3,2,1,0:T(8,128)S(1)} collective-permute-done((f32[2,4,128,256]{3,2,1,0:T(8,128)}, f32[2,4,128,256]{3,2,1,0:T(8,128)S(1)}, u32[]{:S(2)}, u32[]{:S(2)}) %collective-permute-start.5) | collective-permute-done | bytes 1048608 | tf_op jit(solution)/shard_map/ppermute | solution.py:510
  204.6 0.1 broadcast_select_fusion.2
  204.7 0.9 collective-permute-start.6
  205.7 18.2 %shard_map.44 = (bf16[8,1024,256]{2,1,0:T(8,128)(2,1)S(1)}, f32[8,256,256]{2,1,0:T(8,128)S(1)}) custom-call(s32[8]{0:T(128)S(1)} %copy-done.10, f32[8,128,256]{2,1,0:T(8,128)} %add.67.refs_1_, f32[8,128,256]{2,1,0:T(8,128)} %collective-permute-done.9.refs_2_, f32[8,128,256]{2,1,0:T(8,128)S(1)} %copy-done.7, ...), custom_call_target="tpu_custom_call" | custom-call | flops 8053063680 | bytes 12582912 | tf_op jit(solution)/shard_map/pallas_call | solution.py:263
  223.9 4.8 %shard_map.46 = (f32[1024,768]{1,0:T(8,128)}, bf16[1024,512]{1,0:T(8,128)(2,1)S(1)}) custom-call(s32[8]{0:T(128)S(1)} %copy-done.10, f32[2,4,128,256]{3,2,1,0:T(8,128)S(1)} %copy-done.4, f32[2,4,128,256]{3,2,1,0:T(8,128)} %collective-permute-done.21.refs_2_, f32[2,4,128,256]{3,2,1,0:T(8,128)} %collective-permute-done.22.refs_3_, ...), custom_call_target="tpu_custom_call" | custom-call | flops 805306368 | bytes 8388608 | tf_op jit(solution)/shard_map/pallas_call | solution.py:337
  228.7 10.3 %shard_map.48 = (f32[1024,768]{1,0:T(8,128)}, bf16[1024,512]{1,0:T(8,128)(2,1)S(1)}, f32[1024,256]{1,0:T(8,128)S(1)}) custom-call(s32[8]{0:T(128)S(1)} %copy-done.10, f32[2,4,128,256]{3,2,1,0:T(8,128)S(1)} %copy-done.5, f32[2,4,128,256]{3,2,1,0:T(8,128)} %collective-permute-done.24.refs_2_, ...), custom_call_target="tpu_custom_call", output_to_operand_aliasing={{0}: (9, {})} | custom-call | flops 3221225472 | bytes 8388608 | tf_op jit(solution)/shard_map/pallas_call | solution.py:337
  239.0 9.9 %shard_map.49.refs_5_ = f32[1024,2048]{1,0:T(8,128)S(1)} custom-call(s32[8]{0:T(128)S(1)} %copy-done.10, f32[1024,2048]{1,0:T(8,128)S(1)} %bitcast.18, bf16[8,1024,256]{2,1,0:T(8,128)(2,1)S(1)} %get-tuple-element.23.cparts, bf16[1024,512]{1,0:T(8,128)(2,1)S(1)} %get-tuple-element.24.refs_0_, bf16[1024,512]{1,0:T(8,128)(2,1)S(1)} %get-tuple-element.26.refs_1_), custom_call_target="tpu_custom_call" | custom-call | flops 6442450944 | bytes 25165824 | tf_op jit(solution)/shard_map/pallas_call | solution.py:406
  249.0 14.1 %shard_map.50 = (f32[1024,2048]{1,0:T(8,128)}, f32[1024,768]{1,0:T(8,128)}) custom-call(s32[8]{0:T(128)S(1)} %copy-done.10, f32[2,4,128,256]{3,2,1,0:T(8,128)S(1)} %copy-done.3, f32[2,4,128,256]{3,2,1,0:T(8,128)} %collective-permute-done.4.refs_2_, f32[2,4,128,256]{3,2,1,0:T(8,128)S(1)} %collective-permute-done.5.refs_3_, ...), custom_call_target="tpu_custom_call", output_to_operand_aliasing={{1}: (11, {})} | custom-call | flops 3221225472 | bytes 25165824 | tf_op jit(solution)/shard_map/pallas_call | solution.py:473
  (61 shorter events, 0.6 us)
Async XLA Ops:
  6.5 6.5 %collective-permute-start = (f32[24,128,256]{2,1,0:T(8,128)}, f32[24,128,256]{2,1,0:T(8,128)S(1)}, u32[]{:S(2)}, u32[]{:S(2)}) collective-permute-start(f32[24,128,256]{2,1,0:T(8,128)} %get-tuple-element.18), channel_id=1, source_target_pairs={{0,4},{1,5},{2,6},{3,7},{4,0},{5,1},{6,2},{7,3},{8,12},{9,13},{10,... | collective-permute-start | bytes 9437192 | tf_op jit(solution)/shard_map/ppermute | solution.py:510
  15.3 4.6 %copy-start.12 = (f32[8,128,256]{2,1,0:T(8,128)}, f32[8,128,256]{2,1,0:T(8,128)S(1)}, u32[]{:S(2)}) copy-start(f32[8,128,256]{2,1,0:T(8,128)S(1)} %get-tuple-element.32) | copy-start | bytes 3145732
  15.4 17.7 %copy-start.11 = (f32[8,128,256]{2,1,0:T(8,128)}, f32[8,128,256]{2,1,0:T(8,128)S(1)}, u32[]{:S(2)}) copy-start(f32[8,128,256]{2,1,0:T(8,128)S(1)} %get-tuple-element.33) | copy-start | bytes 3145732
  15.4 15.0 %collective-permute-start.10 = (f32[8,128,256]{2,1,0:T(8,128)S(1)}, f32[8,128,256]{2,1,0:T(8,128)}, u32[]{:S(2)}, u32[]{:S(2)}) collective-permute-start(f32[8,128,256]{2,1,0:T(8,128)S(1)} %get-tuple-element.32), channel_id=1, source_target_pairs={{0,8},{1,9},{2,10},{3,11},{4,20},{5,21},{6,22},{7,23},{8,0},{9,1},... | collective-permute-start | bytes 3145736 | tf_op jit(solution)/shard_map/ppermute | solution.py:510
  15.5 3.1 %collective-permute-start.13 = (f32[6,128,256]{2,1,0:T(8,128)}, f32[6,128,256]{2,1,0:T(8,128)}, u32[]{:S(2)}, u32[]{:S(2)}) collective-permute-start(f32[6,128,256]{2,1,0:T(8,128)} %get-tuple-element.22), channel_id=1, source_target_pairs={{0,4},{1,5},{2,6},{3,7},{4,0},{5,1},{6,2},{7,3},{8,12},{9,13},{10,... | collective-permute-start | bytes 2359304 | tf_op jit(solution)/shard_map/ppermute | solution.py:510
  16.3 32.6 %collective-permute-start.7 = (f32[8,128,256]{2,1,0:T(8,128)S(1)}, f32[8,128,256]{2,1,0:T(8,128)}, u32[]{:S(2)}, u32[]{:S(2)}) collective-permute-start(f32[8,128,256]{2,1,0:T(8,128)S(1)} %get-tuple-element.33), channel_id=1, source_target_pairs={{0,8},{1,9},{2,10},{3,11},{4,20},{5,21},{6,22},{7,23},{8,0},{9,1},... | collective-permute-start | bytes 3145736 | tf_op jit(solution)/shard_map/ppermute | solution.py:510
  18.0 53.3 %collective-permute-start.1 = (f32[8,128,256]{2,1,0:T(8,128)S(1)}, f32[8,128,256]{2,1,0:T(8,128)}, u32[]{:S(2)}, u32[]{:S(2)}) collective-permute-start(f32[8,128,256]{2,1,0:T(8,128)S(1)} %get-tuple-element.34), channel_id=1, source_target_pairs={{0,8},{1,9},{2,10},{3,11},{4,20},{5,21},{6,22},{7,23},{8,0},{9,1},... | collective-permute-start | bytes 3145736 | tf_op jit(solution)/shard_map/ppermute | solution.py:510
  20.0 30.5 %copy-start.13 = (f32[6,128,256]{2,1,0:T(8,128)}, f32[6,128,256]{2,1,0:T(8,128)S(1)}, u32[]{:S(2)}) copy-start(f32[6,128,256]{2,1,0:T(8,128)S(1)} %add.71) | copy-start | bytes 2359300
  32.1 50.6 %collective-permute-start.11 = (f32[8,128,256]{2,1,0:T(8,128)S(1)}, f32[8,128,256]{2,1,0:T(8,128)}, u32[]{:S(2)}, u32[]{:S(2)}) collective-permute-start(f32[8,128,256]{2,1,0:T(8,128)S(1)} %add.69), channel_id=1, source_target_pairs={{0,16},{1,17},{2,18},{3,19},{4,12},{5,13},{6,14},{7,15},{8,24},{9,... | collective-permute-start | bytes 3145736 | tf_op jit(solution)/shard_map/ppermute | solution.py:510
  33.1 46.6 %collective-permute-start.14 = (f32[4,96,256]{2,1,0:T(8,128)S(1)}, f32[4,96,256]{2,1,0:T(8,128)}, u32[]{:S(2)}, u32[]{:S(2)}) collective-permute-start(f32[4,96,256]{2,1,0:T(8,128)S(1)} %dynamic-slice_bitcast_fusion), channel_id=1, source_target_pairs={{0,8},{1,9},{2,10},{3,11},{4,20},{5,21},{6,22},{7,23},{8,0},{9,1},... | collective-permute-start | bytes 1179656 | tf_op jit(solution)/shard_map/ppermute | solution.py:510
  50.5 44.3 %collective-permute-start.8 = (f32[8,128,256]{2,1,0:T(8,128)S(1)}, f32[8,128,256]{2,1,0:T(8,128)}, u32[]{:S(2)}, u32[]{:S(2)}) collective-permute-start(f32[8,128,256]{2,1,0:T(8,128)S(1)} %add.66), channel_id=1, source_target_pairs={{0,16},{1,17},{2,18},{3,19},{4,12},{5,13},{6,14},{7,15},{8,24},{9,... | collective-permute-start | bytes 3145736 | tf_op jit(solution)/shard_map/ppermute | solution.py:510
  51.8 27.9 %copy-start.14 = (f32[6,128,256]{2,1,0:T(8,128)S(1)}, f32[6,128,256]{2,1,0:T(8,128)}, u32[]{:S(2)}) copy-start(f32[6,128,256]{2,1,0:T(8,128)} %copy-done.13) | copy-start | bytes 2359300
  73.6 29.6 %collective-permute-start.2 = (f32[8,128,256]{2,1,0:T(8,128)}, f32[8,128,256]{2,1,0:T(8,128)}, u32[]{:S(2)}, u32[]{:S(2)}) collective-permute-start(f32[8,128,256]{2,1,0:T(8,128)} %add.63), channel_id=1, source_target_pairs={{0,16},{1,17},{2,18},{3,19},{4,12},{5,13},{6,14},{7,15},{8,24},{9,... | collective-permute-start | bytes 3145736 | tf_op jit(solution)/shard_map/ppermute | solution.py:510
  81.5 10.8 %collective-permute-start.15 = (f32[2,96,256]{2,1,0:T(8,128)}, f32[2,96,256]{2,1,0:T(8,128)}, u32[]{:S(2)}, u32[]{:S(2)}) collective-permute-start(f32[2,96,256]{2,1,0:T(8,128)} %dynamic-slice_bitcast_fusion.1), channel_id=1, source_target_pairs={{0,16},{1,17},{2,18},{3,19},{4,12},{5,13},{6,14},{7,15},{8,24},{9,... | collective-permute-start | bytes 589832 | tf_op jit(solution)/shard_map/ppermute | solution.py:510
  84.0 20.9 %copy-start.6 = (f32[8,128,256]{2,1,0:T(8,128)}, f32[8,128,256]{2,1,0:T(8,128)S(1)}, u32[]{:S(2)}) copy-start(f32[8,128,256]{2,1,0:T(8,128)S(1)} %add.70.refs_3_.refs_1_) | copy-start | bytes 3145732
  84.0 35.0 %collective-permute-start.12 = (f32[8,128,256]{2,1,0:T(8,128)S(1)}, f32[8,128,256]{2,1,0:T(8,128)}, u32[]{:S(2)}, u32[]{:S(2)}) collective-permute-start(f32[8,128,256]{2,1,0:T(8,128)S(1)} %add.70.refs_3_.refs_1_), channel_id=1, source_target_pairs={{0,4},{1,5},{2,6},{3,7},{4,0},{5,1},{6,2},{7,3},{8,12},{9,13},{10,... | collective-permute-start | bytes 3145736 | tf_op jit(solution)/shard_map/ppermute | solution.py:510
  93.2 7.3 %collective-permute-start.16 = (f32[2,96,256]{2,1,0:T(8,128)S(1)}, f32[2,96,256]{2,1,0:T(8,128)S(1)}, u32[]{:S(2)}, u32[]{:S(2)}) collective-permute-start(f32[2,96,256]{2,1,0:T(8,128)S(1)} %bitcast_add_fusion.1), channel_id=1, source_target_pairs={{0,1},{1,0},{2,3},{3,2},{4,5},{5,4},{6,7},{7,6},{8,9},{9,8},{10,11... | collective-permute-start | bytes 589832 | tf_op jit(solution)/shard_map/ppermute | solution.py:510
  97.2 29.5 %collective-permute-start.9 = (f32[8,128,256]{2,1,0:T(8,128)}, f32[8,128,256]{2,1,0:T(8,128)}, u32[]{:S(2)}, u32[]{:S(2)}) collective-permute-start(f32[8,128,256]{2,1,0:T(8,128)} %add.67.refs_1_), channel_id=1, source_target_pairs={{0,4},{1,5},{2,6},{3,7},{4,0},{5,1},{6,2},{7,3},{8,12},{9,13},{10,... | collective-permute-start | bytes 3145736 | tf_op jit(solution)/shard_map/ppermute | solution.py:510
  100.5 11.5 %collective-permute-start.17 = (f32[2,96,256]{2,1,0:T(8,128)S(1)}, f32[2,96,256]{2,1,0:T(8,128)S(1)}, u32[]{:S(2)}, u32[]{:S(2)}) collective-permute-start(f32[2,96,256]{2,1,0:T(8,128)S(1)} %add.78), channel_id=1, source_target_pairs={{0,2},{1,3},{2,0},{3,1},{4,6},{5,7},{6,4},{7,5},{8,10},{9,11},{10,... | collective-permute-start | bytes 589832 | tf_op jit(solution)/shard_map/ppermute | solution.py:510
  104.9 24.7 %copy-start.1 = (f32[8,128,256]{2,1,0:T(8,128)}, f32[8,128,256]{2,1,0:T(8,128)S(1)}, u32[]{:S(2)}) copy-start(f32[8,128,256]{2,1,0:T(8,128)S(1)} %add.64.refs_1_.refs_6_) | copy-start | bytes 3145732
  104.9 26.3 %collective-permute-start.3 = (f32[8,128,256]{2,1,0:T(8,128)S(1)}, f32[8,128,256]{2,1,0:T(8,128)S(1)}, u32[]{:S(2)}, u32[]{:S(2)}) collective-permute-start(f32[8,128,256]{2,1,0:T(8,128)S(1)} %add.64.refs_1_.refs_6_), channel_id=1, source_target_pairs={{0,4},{1,5},{2,6},{3,7},{4,0},{5,1},{6,2},{7,3},{8,12},{9,13},{10,... | collective-permute-start | bytes 3145736 | tf_op jit(solution)/shard_map/ppermute | solution.py:510
  112.1 1.3 copy-start.15
  112.1 5.8 %collective-permute-start.18 = (f32[2,96,256]{2,1,0:T(8,128)S(1)}, f32[2,96,256]{2,1,0:T(8,128)}, u32[]{:S(2)}, u32[]{:S(2)}) collective-permute-start(f32[2,96,256]{2,1,0:T(8,128)S(1)} %add.79), channel_id=1, source_target_pairs={{0,16},{1,17},{2,18},{3,19},{4,12},{5,13},{6,14},{7,15},{8,24},{9,... | collective-permute-start | bytes 589832 | tf_op jit(solution)/shard_map/ppermute | solution.py:510
  122.0 15.0 %collective-permute-start.24 = (f32[2,4,128,256]{3,2,1,0:T(8,128)}, f32[2,4,128,256]{3,2,1,0:T(8,128)}, u32[]{:S(2)}, u32[]{:S(2)}) collective-permute-start(f32[2,4,128,256]{3,2,1,0:T(8,128)} %shard_map.47.refs_1_), channel_id=1, source_target_pairs={{0,1},{5,6},{10,9},{15,14},{16,17},{21,22},{26,25},{31,30}} | collective-permute-start | bytes 3145736 | tf_op jit(solution)/shard_map/ppermute | solution.py:510
  123.7 13.2 %collective-permute-start.19 = (f32[4,96,256]{2,1,0:T(8,128)S(1)}, f32[4,96,256]{2,1,0:T(8,128)S(1)}, u32[]{:S(2)}, u32[]{:S(2)}) collective-permute-start(f32[4,96,256]{2,1,0:T(8,128)S(1)} %pad_maximum_fusion.2), channel_id=1, source_target_pairs={{0,8},{1,9},{2,10},{3,11},{4,20},{5,21},{6,22},{7,23},{8,0},{9,1},... | collective-permute-start | bytes 1179656 | tf_op jit(solution)/shard_map/ppermute | solution.py:510
  129.6 8.8 %collective-permute-start.21 = (f32[2,4,128,256]{3,2,1,0:T(8,128)}, f32[2,4,128,256]{3,2,1,0:T(8,128)}, u32[]{:S(2)}, u32[]{:S(2)}) collective-permute-start(f32[2,4,128,256]{3,2,1,0:T(8,128)} %shard_map.45.refs_1_), channel_id=1, source_target_pairs={{0,1},{5,6},{10,9},{15,14},{16,17},{21,22},{26,25},{31,30}} | collective-permute-start | bytes 3145736 | tf_op jit(solution)/shard_map/ppermute | solution.py:510
  131.2 1.0 copy-start.8
  135.1 4.6 %collective-permute-start.4 = (f32[2,4,128,256]{3,2,1,0:T(8,128)}, f32[2,4,128,256]{3,2,1,0:T(8,128)}, u32[]{:S(2)}, u32[]{:S(2)}) collective-permute-start(f32[2,4,128,256]{3,2,1,0:T(8,128)} %shard_map.42.refs_1_), channel_id=1, source_target_pairs={{0,1},{5,6},{10,9},{15,14},{16,17},{21,22},{26,25},{31,30}} | collective-permute-start | bytes 3145736 | tf_op jit(solution)/shard_map/ppermute | solution.py:510
  137.0 4.0 %collective-permute-start.20 = (f32[8,96,256]{2,1,0:T(8,128)S(1)}, f32[8,96,256]{2,1,0:T(8,128)S(1)}, u32[]{:S(2)}, u32[]{:S(2)}) collective-permute-start(f32[8,96,256]{2,1,0:T(8,128)S(1)} %pad_maximum_fusion.1), channel_id=1, source_target_pairs={{0,4},{1,5},{2,6},{3,7},{4,0},{5,1},{6,2},{7,3},{8,12},{9,13},{10,... | collective-permute-start | bytes 2359304 | tf_op jit(solution)/shard_map/ppermute | solution.py:510
  137.1 20.2 %collective-permute-start.25 = (f32[2,4,128,256]{3,2,1,0:T(8,128)}, f32[2,4,128,256]{3,2,1,0:T(8,128)}, u32[]{:S(2)}, u32[]{:S(2)}) collective-permute-start(f32[2,4,128,256]{3,2,1,0:T(8,128)} %collective-permute-done.24.refs_2_), channel_id=1, source_target_pairs={{1,2},{6,7},{9,8},{14,13},{17,18},{22,23},{25,24},{30,29}} | collective-permute-start | bytes 3145736 | tf_op jit(solution)/shard_map/ppermute | solution.py:510
  138.4 40.7 %collective-permute-start.22 = (f32[2,4,128,256]{3,2,1,0:T(8,128)}, f32[2,4,128,256]{3,2,1,0:T(8,128)}, u32[]{:S(2)}, u32[]{:S(2)}) collective-permute-start(f32[2,4,128,256]{3,2,1,0:T(8,128)} %collective-permute-done.21.refs_2_), channel_id=1, source_target_pairs={{1,2},{6,7},{9,8},{14,13},{17,18},{22,23},{25,24},{30,29}} | collective-permute-start | bytes 3145736 | tf_op jit(solution)/shard_map/ppermute | solution.py:510
  139.7 64.9 %collective-permute-start.5 = (f32[2,4,128,256]{3,2,1,0:T(8,128)}, f32[2,4,128,256]{3,2,1,0:T(8,128)S(1)}, u32[]{:S(2)}, u32[]{:S(2)}) collective-permute-start(f32[2,4,128,256]{3,2,1,0:T(8,128)} %collective-permute-done.4.refs_2_), channel_id=1, source_target_pairs={{1,2},{6,7},{9,8},{14,13},{17,18},{22,23},{25,24},{30,29}} | collective-permute-start | bytes 3145736 | tf_op jit(solution)/shard_map/ppermute | solution.py:510
  141.1 16.1 %copy-start.5 = (f32[2,4,128,256]{3,2,1,0:T(8,128)S(1)}, f32[2,4,128,256]{3,2,1,0:T(8,128)}, u32[]{:S(2)}) copy-start(f32[2,4,128,256]{3,2,1,0:T(8,128)} %shard_map.47.refs_1_) | copy-start | bytes 3145732
  142.4 36.7 %copy-start.4 = (f32[2,4,128,256]{3,2,1,0:T(8,128)S(1)}, f32[2,4,128,256]{3,2,1,0:T(8,128)}, u32[]{:S(2)}) copy-start(f32[2,4,128,256]{3,2,1,0:T(8,128)} %shard_map.45.refs_1_) | copy-start | bytes 3145732
  157.2 47.3 %copy-start.3 = (f32[2,4,128,256]{3,2,1,0:T(8,128)S(1)}, f32[2,4,128,256]{3,2,1,0:T(8,128)}, u32[]{:S(2)}) copy-start(f32[2,4,128,256]{3,2,1,0:T(8,128)} %shard_map.42.refs_1_) | copy-start | bytes 3145732
  158.7 46.9 %copy-start = (f32[6,256,256]{2,1,0:T(8,128)S(1)}, f32[6,256,256]{2,1,0:T(8,128)}, u32[]{:S(2)}) copy-start(f32[6,256,256]{2,1,0:T(8,128)} %shard_map.43.refs_5_.refs_6_.refs_7_.refs_8_.refs_9_) | copy-start | bytes 4718596
  158.7 46.9 %copy-start.7 = (f32[8,128,256]{2,1,0:T(8,128)S(1)}, f32[8,128,256]{2,1,0:T(8,128)}, u32[]{:S(2)}) copy-start(f32[8,128,256]{2,1,0:T(8,128)} %copy-done.6) | copy-start | bytes 3145732
  158.7 46.9 %copy-start.10 = (s32[8]{0:T(128)S(1)}, s32[8]{0:T(128)}, u32[]{:S(2)}) copy-start(s32[8]{0:T(128)} %concatenate.12.refs_0_.info) | copy-start | bytes 100
  158.7 70.0 %collective-permute-start.26 = (f32[2,4,128,256]{3,2,1,0:T(8,128)S(1)}, f32[2,4,128,256]{3,2,1,0:T(8,128)S(1)}, u32[]{:S(2)}, u32[]{:S(2)}) collective-permute-start(f32[2,4,128,256]{3,2,1,0:T(8,128)S(1)} %broadcast_select_fusion), channel_id=1, source_target_pairs={{2,3},{5,4},{10,11},{13,12},{18,19},{21,20},{26,27},{29,28}} | collective-permute-start | bytes 3145736 | tf_op jit(solution)/shard_map/ppermute | solution.py:510
  180.5 43.3 %collective-permute-start.23 = (f32[2,4,128,256]{3,2,1,0:T(8,128)S(1)}, f32[2,4,128,256]{3,2,1,0:T(8,128)S(1)}, u32[]{:S(2)}, u32[]{:S(2)}) collective-permute-start(f32[2,4,128,256]{3,2,1,0:T(8,128)S(1)} %broadcast_select_fusion.1), channel_id=1, source_target_pairs={{2,3},{5,4},{10,11},{13,12},{18,19},{21,20},{26,27},{29,28}} | collective-permute-start | bytes 3145736 | tf_op jit(solution)/shard_map/ppermute | solution.py:510
  204.7 44.2 %collective-permute-start.6 = (f32[2,4,128,256]{3,2,1,0:T(8,128)S(1)}, f32[2,4,128,256]{3,2,1,0:T(8,128)S(1)}, u32[]{:S(2)}, u32[]{:S(2)}) collective-permute-start(f32[2,4,128,256]{3,2,1,0:T(8,128)S(1)} %broadcast_select_fusion.2), channel_id=1, source_target_pairs={{2,3},{5,4},{10,11},{13,12},{18,19},{21,20},{26,27},{29,28}} | collective-permute-start | bytes 3145736 | tf_op jit(solution)/shard_map/ppermute | solution.py:510
  223.8 15.1 %slice-start = ((s8[8388608]{0:T(1024)(128)(4,1)}), s8[4194304]{0:T(1024)(128)(4,1)S(1)}, s32[]{:S(2)}) async-start(s8[8388608]{0:T(1024)(128)(4,1)} %bitcast.17), calls=%async_computation | async-start | bytes 8388608
  228.7 10.3 %slice-start.1 = ((s8[8388608]{0:T(1024)(128)(4,1)}), s8[4194304]{0:T(1024)(128)(4,1)S(1)}, s32[]{:S(2)}) async-start(s8[8388608]{0:T(1024)(128)(4,1)} %bitcast.17), calls=%async_computation.1 | async-start | bytes 8388608
  239.0 10.0 %copy-start.2 = (f32[8,128,256]{2,1,0:T(8,128)S(1)}, f32[8,128,256]{2,1,0:T(8,128)}, u32[]{:S(2)}) copy-start(f32[8,128,256]{2,1,0:T(8,128)} %copy-done.1) | copy-start | bytes 3145732
  239.0 10.0 %copy-start.9 = (f32[8,128,256]{2,1,0:T(8,128)S(1)}, f32[8,128,256]{2,1,0:T(8,128)}, u32[]{:S(2)}) copy-start(f32[8,128,256]{2,1,0:T(8,128)} %copy-done.8) | copy-start | bytes 3145732

commit v2 on v1

--- a/solution.py
+++ b/solution.py
@@ -20,14 +20,24 @@
     return high, mid, (rest - mid.astype(jnp.float32)).astype(jnp.bfloat16)
 
 
-def dot6(a, b, cb=0):
-    ah, am, al = thirds(a)
-    bh, bm, bl = thirds(b)
-    left = jnp.concatenate([am, al, ah, am, ah, ah], axis=1)
-    right = jnp.concatenate([bm, bh, bl, bh, bm, bh], axis=cb)
+def left6(a):
+    high, mid, low = thirds(a)
+    return jnp.concatenate([mid, low, high, mid, high, high], axis=1)
+
+
+def right6(b, axis=0):
+    high, mid, low = thirds(b)
+    return jnp.concatenate([mid, high, low, high, mid, high], axis=axis)
+
+
+def bdot(left, right, axis=0):
     return lax.dot_general(
-        left, right, (((1,), (cb,)), ((), ())), preferred_element_type=jnp.float32
+        left, right, (((1,), (axis,)), ((), ())), preferred_element_type=jnp.float32
     )
+
+
+def dot6(a, b, axis=0):
+    return bdot(left6(a), right6(b, axis), axis)
 
 
 def iotas(shape):
@@ -235,22 +245,30 @@
 
 
 def col_kernel(cols, info, *refs):
-    raw, solved, (parts, rest) = refs[: 2 * PANELS - 2], refs[2 * PANELS - 2 : -2], refs[-2:]
+    raw, solved = refs[: 2 * PANELS - 2], refs[2 * PANELS - 2 : -3]
+    parts, rest, left = refs[-3:]
     block = pl.program_id(0) * cols + info[PANELS + 1]
+    last = PANELS - 1
+
+    @pl.when(pl.program_id(0) == 0)
+    def _():
+        for n, ref in enumerate(solved):
+            left[n] = left6(ref[0])
+
     facs = []
-    last = PANELS - 1
     for s in range(last):
         full = jnp.concatenate([raw[2 * s][0], raw[2 * s + 1][0]], axis=0)
-        fac = dot6(solved[pair(s, s)][0], full)
+        fac = bdot(left[pair(s, s)], right6(full))
         for k in range(s):
-            fac = fac - dot6(solved[pair(s, k)][0], facs[k])
-        facs.append(jnp.where(is_used(info, block, s), 0.0, fac))
-        for i, part in enumerate(halves(facs[s])):
+            fac = fac - bdot(left[pair(s, k)], facs[k])
+        fac = jnp.where(is_used(info, block, s), 0.0, fac)
+        facs.append(right6(fac))
+        for i, part in enumerate(halves(fac)):
             at = (2 * s + i) * NB
             parts[0, at : at + NB] = part
     total = None
     for k in range(last):
-        term = dot6(solved[pair(last, k)][0], facs[k])
+        term = bdot(left[pair(last, k)], facs[k])
         total = term if total is None else total + term
     rest[0] = total
 
@@ -269,6 +287,7 @@
             pl.BlockSpec((1, 2 * last * NB, NB), lambda i: (i, 0, 0)),
             pl.BlockSpec((1, NB, NB), lambda i: (i, 0, 0)),
         ],
+        scratch_shapes=[pltpu.VMEM((len(names), NB, 6 * NB), jnp.bfloat16)],
         compiler_params=params(),
         interpret=INTERPRET,
         cost_estimate=cost(60 * count * NB**3, 12),
@@ -424,7 +443,7 @@
 def last_kernel(rows, cols, count, info, *refs):
     sources, refs = refs[:count], refs[count:]
     current, half, other, rest, w, row_rest, _, out, fout = refs[:9]
-    raw, fac_s, parts, left, sem, out_sem = refs[9:]
+    raw, fac_s, parts, left, w6, sem, out_sem = refs[9:]
     last = PANELS - 1
     step = pl.program_id(0)
     blk_rows = raw.shape[1]
@@ -433,10 +452,11 @@
     @pl.when(step == 0)
     def _():
         fetch(info, sources, raw, sem)
+        w6[...] = left6(w[0])
         for i in range(blk_rows):
             at = slice(i * NB, (i + 1) * NB)
             full = jnp.concatenate([raw[0, i], raw[1, i]], axis=0)
-            fac = dot6(full.T, w[0], 1) - row_rest[at]
+            fac = bdot(w6[...], right6(full)).T - row_rest[at]
             fac = jnp.where(is_used(info, i * rows + info[PANELS], last), 0.0, fac)
             fac_s[at] = fac
             high, low = halves(fac)
@@ -449,7 +469,7 @@
         write.start()
 
     block = step * cols + info[PANELS + 1]
-    fac = dot6(w[0], jnp.concatenate([half[0], other[0]], axis=0)) - rest[0]
+    fac = bdot(w6[...], right6(jnp.concatenate([half[0], other[0]], axis=0))) - rest[0]
     high, low = halves(jnp.where(is_used(info, block, last), 0.0, fac))
     right = jnp.concatenate([low, high, high], axis=0)
     value = current[...] - jnp.dot(left[...], right, preferred_element_type=jnp.float32)
@@ -484,6 +504,7 @@
             pltpu.VMEM((height, NB), jnp.float32),
             pltpu.VMEM((height, 2 * NB), jnp.bfloat16),
             pltpu.VMEM((height, 3 * NB), jnp.bfloat16),
+            pltpu.VMEM((NB, 6 * NB), jnp.bfloat16),
             pltpu.SemaphoreType.DMA,
             pltpu.SemaphoreType.DMA,
         ],
@@ -551,7 +572,7 @@
     return jnp.concatenate([jnp.where(low, part, other), jnp.where(low, other, part)])
 
 
-def spread_rows(net, source, is_source):
+def spread_rows(net, source, is_source, direct):
     if (net.rows, net.cols) != (8, 4):
         value = jnp.where(is_source, source, 0.0)
         for bit in net.col_bits:
@@ -571,6 +592,10 @@
         return target
 
     got1 = net.send(source, hop({0: 1}, {1: 2}))
+    if direct:
+        got2 = net.send(source, hop({0: 2}, {1: 3}))
+        got3 = net.send(source, hop({0: 3}, {1: 0}))
+        return [source, got1, got2, got3]
     got2 = net.send(got1, hop({1: 2}, {2: 3}))
     third = jnp.where(is_source, source, got2)
     got3 = net.send(third, hop({2: 3}, {1: 0}))
@@ -616,7 +641,7 @@
             part = part + net.row_step(part, step)
         parts.append((part, net.core(part)))
         own = own_rows(ratio, info, *parts[s])
-        sources.append(spread_rows(net, own, is_source))
+        sources.append(spread_rows(net, own, is_source, s == PANELS - 1))
     cparts, col_rest = col_factor(cols, info, [v for p in parts[:-1] for v in p], solved)
     out, rparts = (), []
     for s in range(PANELS - 1):

time: 264 us -> 253 us (0.958)
  the two profiles are of different devices: /device:TPU:2 before, /device:TPU:6 now
where the time goes in v2:
time: 253 us
  waiting for transfers between devices  104 us (41%)
  Pallas kernels  86 us (34%)
  starting transfers between devices  32.9 us (13%)
  other arithmetic  22 us (9%)
  local copies, waits for them, and re-layouts  6.79 us (3%)
    ppermute x27, waiting for transfers between devices, send(): return lax.ppermute(value, AXES, pairs)  104 us
    ppermute x27, starting transfers between devices, send(): return lax.ppermute(value, AXES, pairs)  32.9 us
    pallas_call x1, Pallas kernels, col_factor(): pl.pallas_call(lambda *refs: col_kernel(cols, *refs), grid=(count,), out_...  18.2 us
    pallas_call x2, Pallas kernels, row_factor(): pl.pallas_call(lambda *refs: row_kernel(s, rows, len(sources), *refs), gr...  15.1 us
    pallas_call x1, Pallas kernels, chain(): pl.pallas_call(chain_kernel, out_shape=jax.ShapeDtypeStruct(corner.shape,...  14.7 us
    pallas_call x1, Pallas kernels, last_update(): pl.pallas_call(lambda *refs: last_kernel(rows, cols, count, *refs), grid=...  14.4 us
    pallas_call x1, Pallas kernels, early_update(): pl.pallas_call(early_kernel, grid=(width // NB,), out_shape=f32(height, w...  9.91 us
    pallas_call x3, Pallas kernels, own_rows(): pl.pallas_call(lambda *refs: own_kernel(ratio, *refs), out_shape=f32(2, h...  8.91 us
  transfers between devices with their start and end apart: 27, of which 11 were waited for; matrix products, arithmetic and copies ran while one was open for 8% of the time, Pallas kernels for 26%

profile of v2, /device:TPU:6, one launch (start us, length us, event | category | flops | bytes accessed | tf_op | source)
XLA Modules:
  0.0 252.6 jit_solution(18245930584037459733)
XLA Ops:
  0.7 1.3 concatenate.12.refs_0_.info
  2.0 4.6 %shard_map.41 = (f32[6,128,256]{2,1,0:T(8,128)}, f32[6,128,256]{2,1,0:T(8,128)}, f32[8,128,256]{2,1,0:T(8,128)}, f32[8,128,256]{2,1,0:T(8,128)}, f32[8,128,256]{2,1,0:T(8,128)}, /*index=5*/f32[24,128,256]{2,1,0:T(8,128)}) custom-call(s32[8]{0:T(128)} %concatenate.12.refs_0_.info, f32[1024,2048]{1,0:T(8,128)} %current.1), custom_call_target="tpu_custom_call" | custom-call | bytes 16777216 | tf_op jit(solution)/shard_map/pallas_call | solution.py:212
  6.7 5.9 %collective-permute-done = f32[24,128,256]{2,1,0:T(8,128)S(1)} collective-permute-done((f32[24,128,256]{2,1,0:T(8,128)}, f32[24,128,256]{2,1,0:T(8,128)S(1)}, u32[]{:S(2)}, u32[]{:S(2)}) %collective-permute-start) | collective-permute-done | bytes 3145760 | tf_op jit(solution)/shard_map/ppermute | solution.py:531
  12.5 3.3 %slice_add_fusion = (f32[8,128,256]{2,1,0:T(8,128)S(1)}, f32[8,128,256]{2,1,0:T(8,128)S(1)}, f32[8,128,256]{2,1,0:T(8,128)}) fusion(f32[8,128,256]{2,1,0:T(8,128)} %get-tuple-element.20, f32[24,128,256]{2,1,0:T(8,128)S(1)} %collective-permute-done, f32[8,128,256]{2,1,0:T(8,128)} %get-tuple-element.19, f32[8,128,256]{2,1,0:T(8,128)} %get-tuple-element.17), kind=kLoop, calls=%fused_computation.1 | loop fusion | flops 786432 | bytes 9437184 | tf_op jit(solution)/shard_map/add | solution.py:639
  15.9 1.8 collective-permute-start.10
  17.6 0.3 collective-permute-start.7
  17.9 12.8 %collective-permute-done.10 = f32[8,128,256]{2,1,0:T(8,128)S(1)} collective-permute-done((f32[8,128,256]{2,1,0:T(8,128)S(1)}, f32[8,128,256]{2,1,0:T(8,128)S(1)}, u32[]{:S(2)}, u32[]{:S(2)}) %collective-permute-start.10) | collective-permute-done | bytes 1048608 | tf_op jit(solution)/shard_map/ppermute | solution.py:531
  30.7 0.1 add.69
  30.8 1.1 collective-permute-start.11
  32.0 19.1 %collective-permute-done.7 = f32[8,128,256]{2,1,0:T(8,128)S(1)} collective-permute-done((f32[8,128,256]{2,1,0:T(8,128)S(1)}, f32[8,128,256]{2,1,0:T(8,128)S(1)}, u32[]{:S(2)}, u32[]{:S(2)}) %collective-permute-start.7) | collective-permute-done | bytes 1048608 | tf_op jit(solution)/shard_map/ppermute | solution.py:531
  51.0 0.1 add.66
  51.2 0.9 collective-permute-start.8
  52.1 1.2 add.71
  53.4 1.6 add.70.refs_3_.refs_1_
  55.2 1.3 collective-permute-start.14
  56.5 13.9 %collective-permute-done.8 = f32[8,128,256]{2,1,0:T(8,128)} collective-permute-done((f32[8,128,256]{2,1,0:T(8,128)S(1)}, f32[8,128,256]{2,1,0:T(8,128)}, u32[]{:S(2)}, u32[]{:S(2)}) %collective-permute-start.8) | collective-permute-done | bytes 1048608 | tf_op jit(solution)/shard_map/ppermute | solution.py:531
  70.4 1.7 add.67.refs_1_
  72.1 0.1 collective-permute-start.9
  72.2 1.4 bitcast_add_fusion
  73.7 0.7 dynamic-slice_bitcast_fusion.1
  74.3 0.9 collective-permute-start.15
  75.2 0.9 collective-permute-start.1
  76.2 1.0 copy-done.11
  77.1 2.9 %shard_map.47.refs_1_ = f32[2,4,128,256]{3,2,1,0:T(8,128)} custom-call(s32[8]{0:T(128)} %concatenate.12.refs_0_.info, f32[8,128,256]{2,1,0:T(8,128)} %copy-done.6, f32[8,128,256]{2,1,0:T(8,128)} %copy-done.11), custom_call_target="tpu_custom_call" | custom-call | bytes 2097152 | tf_op jit(solution)/shard_map/pallas_call | solution.py:388
  80.1 1.8 collective-permute-start.24
  81.9 1.0 bitcast_add_fusion.1
  82.8 1.4 collective-permute-start.16
  84.2 2.9 %shard_map.45.refs_1_ = f32[2,4,128,256]{3,2,1,0:T(8,128)} custom-call(s32[8]{0:T(128)} %concatenate.12.refs_0_.info, f32[8,128,256]{2,1,0:T(8,128)} %copy-done.8, f32[8,128,256]{2,1,0:T(8,128)} %collective-permute-done.9.refs_2_), custom_call_target="tpu_custom_call" | custom-call | bytes 2097152 | tf_op jit(solution)/shard_map/pallas_call | solution.py:388
  87.1 1.6 collective-permute-start.21
  88.8 0.8 collective-permute-done.16
  89.6 5.4 %collective-permute-start.17 = (f32[2,96,256]{2,1,0:T(8,128)S(1)}, f32[2,96,256]{2,1,0:T(8,128)S(1)}, u32[]{:S(2)}, u32[]{:S(2)}) collective-permute-start(f32[2,96,256]{2,1,0:T(8,128)S(1)} %add.78), channel_id=1, source_target_pairs={{0,2},{1,3},{2,0},{3,1},{4,6},{5,7},{6,4},{7,5},{8,10},{9,11},{10,... | collective-permute-start | bytes 589832 | tf_op jit(solution)/shard_map/ppermute | solution.py:531
  95.1 20.7 %collective-permute-done.17 = f32[2,96,256]{2,1,0:T(8,128)S(1)} collective-permute-done((f32[2,96,256]{2,1,0:T(8,128)S(1)}, f32[2,96,256]{2,1,0:T(8,128)S(1)}, u32[]{:S(2)}, u32[]{:S(2)}) %collective-permute-start.17) | collective-permute-done | bytes 196640 | tf_op jit(solution)/shard_map/ppermute | solution.py:531
  115.8 4.2 %collective-permute-start.18 = (f32[2,96,256]{2,1,0:T(8,128)S(1)}, f32[2,96,256]{2,1,0:T(8,128)S(1)}, u32[]{:S(2)}, u32[]{:S(2)}) collective-permute-start(f32[2,96,256]{2,1,0:T(8,128)S(1)} %add.79), channel_id=1, source_target_pairs={{0,16},{1,17},{2,18},{3,19},{4,12},{5,13},{6,14},{7,15},{8,24},{9,... | collective-permute-start | bytes 589832 | tf_op jit(solution)/shard_map/ppermute | solution.py:531
  119.9 5.8 %collective-permute-done.18 = f32[2,96,256]{2,1,0:T(8,128)S(1)} collective-permute-done((f32[2,96,256]{2,1,0:T(8,128)S(1)}, f32[2,96,256]{2,1,0:T(8,128)S(1)}, u32[]{:S(2)}, u32[]{:S(2)}) %collective-permute-start.18) | collective-permute-done | bytes 196640 | tf_op jit(solution)/shard_map/ppermute | solution.py:531
  125.7 1.4 add.63
  127.1 2.1 collective-permute-start.2
  129.2 1.3 collective-permute-start.25
  130.6 1.3 collective-permute-start.22
  131.9 6.4 %collective-permute-done.19 = f32[4,96,256]{2,1,0:T(8,128)S(1)} collective-permute-done((f32[4,96,256]{2,1,0:T(8,128)S(1)}, f32[4,96,256]{2,1,0:T(8,128)S(1)}, u32[]{:S(2)}, u32[]{:S(2)}) %collective-permute-start.19) | collective-permute-done | bytes 393248 | tf_op jit(solution)/shard_map/ppermute | solution.py:531
  138.4 0.9 pad_maximum_fusion.1
  139.4 2.7 %collective-permute-done.2 = f32[8,128,256]{2,1,0:T(8,128)} collective-permute-done((f32[8,128,256]{2,1,0:T(8,128)S(1)}, f32[8,128,256]{2,1,0:T(8,128)}, u32[]{:S(2)}, u32[]{:S(2)}) %collective-permute-start.2) | collective-permute-done | bytes 1048608 | tf_op jit(solution)/shard_map/ppermute | solution.py:531
  142.1 1.7 add.64.refs_1_.refs_6_
  143.8 0.1 collective-permute-start.3
  143.9 2.3 collective-permute-done.25.refs_3_
  146.2 2.4 broadcast_select_fusion
  148.6 1.6 collective-permute-start.26
  150.2 13.1 %collective-permute-done.22.refs_3_ = f32[2,4,128,256]{3,2,1,0:T(8,128)} collective-permute-done((f32[2,4,128,256]{3,2,1,0:T(8,128)}, f32[2,4,128,256]{3,2,1,0:T(8,128)}, u32[]{:S(2)}, u32[]{:S(2)}) %collective-permute-start.22) | collective-permute-done | bytes 1048608 | tf_op jit(solution)/shard_map/ppermute | solution.py:531
  163.3 2.4 broadcast_select_fusion.1
  165.7 1.6 collective-permute-start.23
  167.4 1.3 broadcast_select_fusion.3
  168.6 1.2 pad_maximum_fusion
  169.9 14.7 %shard_map.43.refs_5_.refs_6_.refs_7_.refs_8_.refs_9_ = f32[6,256,256]{2,1,0:T(8,128)} custom-call(s32[1]{0:T(128)} %bitcast.2.swap_ref, f32[6,256,256]{2,1,0:T(8,128)} %bitcast.19), custom_call_target="tpu_custom_call" | custom-call | tf_op jit(solution)/shard_map/pallas_call | solution.py:131
  184.6 3.1 %shard_map.42.refs_1_ = f32[2,4,128,256]{3,2,1,0:T(8,128)} custom-call(s32[8]{0:T(128)} %concatenate.12.refs_0_.info, f32[8,128,256]{2,1,0:T(8,128)} %copy-done.1, f32[8,128,256]{2,1,0:T(8,128)} %collective-permute-done.3.refs_2_.refs_7_), custom_call_target="tpu_custom_call" | custom-call | bytes 2097152 | tf_op jit(solution)/shard_map/pallas_call | solution.py:388
  187.7 0.9 collective-permute-start.6
  188.6 1.3 collective-permute-start.5
  189.9 0.9 collective-permute-start.4
  190.8 1.2 copy-done.7
  192.1 1.2 copy-done.9
  193.3 1.2 copy-done.12
  194.5 18.2 %shard_map.44 = (bf16[8,1024,256]{2,1,0:T(8,128)(2,1)S(1)}, f32[8,256,256]{2,1,0:T(8,128)S(1)}) custom-call(s32[8]{0:T(128)S(1)} %copy-done.13, f32[8,128,256]{2,1,0:T(8,128)S(1)} %copy-done.9, f32[8,128,256]{2,1,0:T(8,128)} %collective-permute-done.9.refs_2_, f32[8,128,256]{2,1,0:T(8,128)S(1)} %copy-done.7, f32[8,128,256]{2,1,0:T(8,128)S(1)} %copy-done.12, ...), custom_call_target="tpu_custom_call" | custom-call | flops 8053063680 | bytes 12582912 | tf_op jit(solution)/shard_map/pallas_call | solution.py:281
  212.8 4.8 %shard_map.46 = (f32[1024,768]{1,0:T(8,128)}, bf16[1024,512]{1,0:T(8,128)(2,1)S(1)}) custom-call(s32[8]{0:T(128)S(1)} %copy-done.13, f32[2,4,128,256]{3,2,1,0:T(8,128)S(1)} %copy-done.4, f32[2,4,128,256]{3,2,1,0:T(8,128)} %collective-permute-done.21.refs_2_, f32[2,4,128,256]{3,2,1,0:T(8,128)} %collective-permute-done.22.refs_3_, ...), custom_call_target="tpu_custom_call" | custom-call | flops 805306368 | bytes 8388608 | tf_op jit(solution)/shard_map/pallas_call | solution.py:356
  217.7 10.3 %shard_map.48 = (f32[1024,768]{1,0:T(8,128)}, bf16[1024,512]{1,0:T(8,128)(2,1)S(1)}, f32[1024,256]{1,0:T(8,128)S(1)}) custom-call(s32[8]{0:T(128)S(1)} %copy-done.13, f32[2,4,128,256]{3,2,1,0:T(8,128)S(1)} %copy-done.5, f32[2,4,128,256]{3,2,1,0:T(8,128)} %collective-permute-done.24.refs_2_, ...), custom_call_target="tpu_custom_call", output_to_operand_aliasing={{0}: (9, {})} | custom-call | flops 3221225472 | bytes 8388608 | tf_op jit(solution)/shard_map/pallas_call | solution.py:356
  228.0 9.9 %shard_map.49.refs_5_ = f32[1024,2048]{1,0:T(8,128)S(1)} custom-call(s32[8]{0:T(128)S(1)} %copy-done.13, f32[1024,2048]{1,0:T(8,128)S(1)} %bitcast.18, bf16[8,1024,256]{2,1,0:T(8,128)(2,1)S(1)} %get-tuple-element.23.cparts, bf16[1024,512]{1,0:T(8,128)(2,1)S(1)} %get-tuple-element.24.refs_0_, bf16[1024,512]{1,0:T(8,128)(2,1)S(1)} %get-tuple-element.26.refs_1_), custom_call_target="tpu_custom_call" | custom-call | flops 6442450944 | bytes 25165824 | tf_op jit(solution)/shard_map/pallas_call | solution.py:425
  238.0 14.4 %shard_map.50 = (f32[1024,2048]{1,0:T(8,128)}, f32[1024,768]{1,0:T(8,128)}) custom-call(s32[8]{0:T(128)S(1)} %copy-done.13, f32[2,4,128,256]{3,2,1,0:T(8,128)S(1)} %copy-done.10, f32[2,4,128,256]{3,2,1,0:T(8,128)S(1)} %collective-permute-done.4.refs_2_, f32[2,4,128,256]{3,2,1,0:T(8,128)S(1)} %collective-permute-done.5.refs_3_, ...), custom_call_target="tpu_custom_call", output_to_operand_aliasing={{1}: (11, {})} | custom-call | flops 3221225472 | bytes 25165824 | tf_op jit(solution)/shard_map/pallas_call | solution.py:493
  (66 shorter events, 0.6 us)
Async XLA Ops:
  6.6 5.9 %collective-permute-start = (f32[24,128,256]{2,1,0:T(8,128)}, f32[24,128,256]{2,1,0:T(8,128)S(1)}, u32[]{:S(2)}, u32[]{:S(2)}) collective-permute-start(f32[24,128,256]{2,1,0:T(8,128)} %get-tuple-element.18), channel_id=1, source_target_pairs={{0,4},{1,5},{2,6},{3,7},{4,0},{5,1},{6,2},{7,3},{8,12},{9,13},{10,... | collective-permute-start | bytes 9437192 | tf_op jit(solution)/shard_map/ppermute | solution.py:531
  15.9 14.8 %collective-permute-start.10 = (f32[8,128,256]{2,1,0:T(8,128)S(1)}, f32[8,128,256]{2,1,0:T(8,128)S(1)}, u32[]{:S(2)}, u32[]{:S(2)}) collective-permute-start(f32[8,128,256]{2,1,0:T(8,128)S(1)} %get-tuple-element.32), channel_id=1, source_target_pairs={{0,8},{1,9},{2,10},{3,11},{4,20},{5,21},{6,22},{7,23},{8,0},{9,1},... | collective-permute-start | bytes 3145736 | tf_op jit(solution)/shard_map/ppermute | solution.py:531
  17.6 34.5 %copy-start.18 = (f32[6,128,256]{2,1,0:T(8,128)S(1)}, f32[6,128,256]{2,1,0:T(8,128)}, u32[]{:S(2)}) copy-start(f32[6,128,256]{2,1,0:T(8,128)} %get-tuple-element.21) | copy-start | bytes 2359300
  17.6 33.4 %collective-permute-start.7 = (f32[8,128,256]{2,1,0:T(8,128)S(1)}, f32[8,128,256]{2,1,0:T(8,128)S(1)}, u32[]{:S(2)}, u32[]{:S(2)}) collective-permute-start(f32[8,128,256]{2,1,0:T(8,128)S(1)} %get-tuple-element.33), channel_id=1, source_target_pairs={{0,8},{1,9},{2,10},{3,11},{4,20},{5,21},{6,22},{7,23},{8,0},{9,1},... | collective-permute-start | bytes 3145736 | tf_op jit(solution)/shard_map/ppermute | solution.py:531
  30.8 22.6 %collective-permute-start.11 = (f32[8,128,256]{2,1,0:T(8,128)S(1)}, f32[8,128,256]{2,1,0:T(8,128)}, u32[]{:S(2)}, u32[]{:S(2)}) collective-permute-start(f32[8,128,256]{2,1,0:T(8,128)S(1)} %add.69), channel_id=1, source_target_pairs={{0,16},{1,17},{2,18},{3,19},{4,12},{5,13},{6,14},{7,15},{8,24},{9,... | collective-permute-start | bytes 3145736 | tf_op jit(solution)/shard_map/ppermute | solution.py:531
  31.9 20.2 %collective-permute-start.13 = (f32[6,128,256]{2,1,0:T(8,128)}, f32[6,128,256]{2,1,0:T(8,128)}, u32[]{:S(2)}, u32[]{:S(2)}) collective-permute-start(f32[6,128,256]{2,1,0:T(8,128)} %get-tuple-element.22), channel_id=1, source_target_pairs={{0,4},{1,5},{2,6},{3,7},{4,0},{5,1},{6,2},{7,3},{8,12},{9,13},{10,... | collective-permute-start | bytes 2359304 | tf_op jit(solution)/shard_map/ppermute | solution.py:531
  51.2 4.0 %copy-start.15 = (f32[8,128,256]{2,1,0:T(8,128)}, f32[8,128,256]{2,1,0:T(8,128)S(1)}, u32[]{:S(2)}) copy-start(f32[8,128,256]{2,1,0:T(8,128)S(1)} %add.66) | copy-start | bytes 3145732
  51.2 19.2 %collective-permute-start.8 = (f32[8,128,256]{2,1,0:T(8,128)S(1)}, f32[8,128,256]{2,1,0:T(8,128)}, u32[]{:S(2)}, u32[]{:S(2)}) collective-permute-start(f32[8,128,256]{2,1,0:T(8,128)S(1)} %add.66), channel_id=1, source_target_pairs={{0,16},{1,17},{2,18},{3,19},{4,12},{5,13},{6,14},{7,15},{8,24},{9,... | collective-permute-start | bytes 3145736 | tf_op jit(solution)/shard_map/ppermute | solution.py:531
  53.4 18.7 %copy-start.17 = (f32[6,128,256]{2,1,0:T(8,128)}, f32[6,128,256]{2,1,0:T(8,128)S(1)}, u32[]{:S(2)}) copy-start(f32[6,128,256]{2,1,0:T(8,128)S(1)} %add.71) | copy-start | bytes 2359300
  55.0 21.1 %copy-start.6 = (f32[8,128,256]{2,1,0:T(8,128)}, f32[8,128,256]{2,1,0:T(8,128)S(1)}, u32[]{:S(2)}) copy-start(f32[8,128,256]{2,1,0:T(8,128)S(1)} %add.70.refs_3_.refs_1_) | copy-start | bytes 3145732
  55.0 21.1 %collective-permute-start.12 = (f32[8,128,256]{2,1,0:T(8,128)S(1)}, f32[8,128,256]{2,1,0:T(8,128)S(1)}, u32[]{:S(2)}, u32[]{:S(2)}) collective-permute-start(f32[8,128,256]{2,1,0:T(8,128)S(1)} %add.70.refs_3_.refs_1_), channel_id=1, source_target_pairs={{0,4},{1,5},{2,6},{3,7},{4,0},{5,1},{6,2},{7,3},{8,12},{9,13},{10,... | collective-permute-start | bytes 3145736 | tf_op jit(solution)/shard_map/ppermute | solution.py:531
  55.2 17.0 %collective-permute-start.14 = (f32[4,96,256]{2,1,0:T(8,128)S(1)}, f32[4,96,256]{2,1,0:T(8,128)}, u32[]{:S(2)}, u32[]{:S(2)}) collective-permute-start(f32[4,96,256]{2,1,0:T(8,128)S(1)} %dynamic-slice_bitcast_fusion), channel_id=1, source_target_pairs={{0,8},{1,9},{2,10},{3,11},{4,20},{5,21},{6,22},{7,23},{8,0},{9,1},... | collective-permute-start | bytes 1179656 | tf_op jit(solution)/shard_map/ppermute | solution.py:531
  72.1 12.1 %copy-start.8 = (f32[8,128,256]{2,1,0:T(8,128)}, f32[8,128,256]{2,1,0:T(8,128)S(1)}, u32[]{:S(2)}) copy-start(f32[8,128,256]{2,1,0:T(8,128)S(1)} %add.67.refs_1_) | copy-start | bytes 3145732
  72.1 12.1 %collective-permute-start.9 = (f32[8,128,256]{2,1,0:T(8,128)S(1)}, f32[8,128,256]{2,1,0:T(8,128)}, u32[]{:S(2)}, u32[]{:S(2)}) collective-permute-start(f32[8,128,256]{2,1,0:T(8,128)S(1)} %add.67.refs_1_), channel_id=1, source_target_pairs={{0,4},{1,5},{2,6},{3,7},{4,0},{5,1},{6,2},{7,3},{8,12},{9,13},{10,... | collective-permute-start | bytes 3145736 | tf_op jit(solution)/shard_map/ppermute | solution.py:531
  74.3 7.5 %collective-permute-start.15 = (f32[2,96,256]{2,1,0:T(8,128)}, f32[2,96,256]{2,1,0:T(8,128)}, u32[]{:S(2)}, u32[]{:S(2)}) collective-permute-start(f32[2,96,256]{2,1,0:T(8,128)} %dynamic-slice_bitcast_fusion.1), channel_id=1, source_target_pairs={{0,16},{1,17},{2,18},{3,19},{4,12},{5,13},{6,14},{7,15},{8,24},{9,... | collective-permute-start | bytes 589832 | tf_op jit(solution)/shard_map/ppermute | solution.py:531
  75.2 50.5 %collective-permute-start.1 = (f32[8,128,256]{2,1,0:T(8,128)}, f32[8,128,256]{2,1,0:T(8,128)}, u32[]{:S(2)}, u32[]{:S(2)}) collective-permute-start(f32[8,128,256]{2,1,0:T(8,128)} %get-tuple-element.34), channel_id=1, source_target_pairs={{0,8},{1,9},{2,10},{3,11},{4,20},{5,21},{6,22},{7,23},{8,0},{9,1},... | collective-permute-start | bytes 3145736 | tf_op jit(solution)/shard_map/ppermute | solution.py:531
  76.2 1.0 copy-start.11
  80.1 45.7 %copy-start.14 = (f32[8,128,256]{2,1,0:T(8,128)S(1)}, f32[8,128,256]{2,1,0:T(8,128)}, u32[]{:S(2)}) copy-start(f32[8,128,256]{2,1,0:T(8,128)} %get-tuple-element.34) | copy-start | bytes 3145732
  80.1 49.1 %collective-permute-start.24 = (f32[2,4,128,256]{3,2,1,0:T(8,128)}, f32[2,4,128,256]{3,2,1,0:T(8,128)}, u32[]{:S(2)}, u32[]{:S(2)}) collective-permute-start(f32[2,4,128,256]{3,2,1,0:T(8,128)} %shard_map.47.refs_1_), channel_id=1, source_target_pairs={{0,1},{5,6},{10,9},{15,14},{16,17},{21,22},{26,25},{31,30}} | collective-permute-start | bytes 3145736 | tf_op jit(solution)/shard_map/ppermute | solution.py:531
  82.8 6.8 %collective-permute-start.16 = (f32[2,96,256]{2,1,0:T(8,128)S(1)}, f32[2,96,256]{2,1,0:T(8,128)S(1)}, u32[]{:S(2)}, u32[]{:S(2)}) collective-permute-start(f32[2,96,256]{2,1,0:T(8,128)S(1)} %bitcast_add_fusion.1), channel_id=1, source_target_pairs={{0,1},{1,0},{2,3},{3,2},{4,5},{5,4},{6,7},{7,6},{8,9},{9,8},{10,11... | collective-permute-start | bytes 589832 | tf_op jit(solution)/shard_map/ppermute | solution.py:531
  87.1 43.5 %collective-permute-start.21 = (f32[2,4,128,256]{3,2,1,0:T(8,128)}, f32[2,4,128,256]{3,2,1,0:T(8,128)}, u32[]{:S(2)}, u32[]{:S(2)}) collective-permute-start(f32[2,4,128,256]{3,2,1,0:T(8,128)} %shard_map.45.refs_1_), channel_id=1, source_target_pairs={{0,1},{5,6},{10,9},{15,14},{16,17},{21,22},{26,25},{31,30}} | collective-permute-start | bytes 3145736 | tf_op jit(solution)/shard_map/ppermute | solution.py:531
  89.6 26.1 %collective-permute-start.17 = (f32[2,96,256]{2,1,0:T(8,128)S(1)}, f32[2,96,256]{2,1,0:T(8,128)S(1)}, u32[]{:S(2)}, u32[]{:S(2)}) collective-permute-start(f32[2,96,256]{2,1,0:T(8,128)S(1)} %add.78), channel_id=1, source_target_pairs={{0,2},{1,3},{2,0},{3,1},{4,6},{5,7},{6,4},{7,5},{8,10},{9,11},{10,... | collective-permute-start | bytes 589832 | tf_op jit(solution)/shard_map/ppermute | solution.py:531
  115.8 9.9 %collective-permute-start.18 = (f32[2,96,256]{2,1,0:T(8,128)S(1)}, f32[2,96,256]{2,1,0:T(8,128)S(1)}, u32[]{:S(2)}, u32[]{:S(2)}) collective-permute-start(f32[2,96,256]{2,1,0:T(8,128)S(1)} %add.79), channel_id=1, source_target_pairs={{0,16},{1,17},{2,18},{3,19},{4,12},{5,13},{6,14},{7,15},{8,24},{9,... | collective-permute-start | bytes 589832 | tf_op jit(solution)/shard_map/ppermute | solution.py:531
  127.1 12.3 %copy-start.16 = (f32[8,128,256]{2,1,0:T(8,128)}, f32[8,128,256]{2,1,0:T(8,128)S(1)}, u32[]{:S(2)}) copy-start(f32[8,128,256]{2,1,0:T(8,128)S(1)} %add.63) | copy-start | bytes 3145732
  127.1 15.0 %collective-permute-start.2 = (f32[8,128,256]{2,1,0:T(8,128)S(1)}, f32[8,128,256]{2,1,0:T(8,128)}, u32[]{:S(2)}, u32[]{:S(2)}) collective-permute-start(f32[8,128,256]{2,1,0:T(8,128)S(1)} %add.63), channel_id=1, source_target_pairs={{0,16},{1,17},{2,18},{3,19},{4,12},{5,13},{6,14},{7,15},{8,24},{9,... | collective-permute-start | bytes 3145736 | tf_op jit(solution)/shard_map/ppermute | solution.py:531
  129.2 17.0 %collective-permute-start.25 = (f32[2,4,128,256]{3,2,1,0:T(8,128)}, f32[2,4,128,256]{3,2,1,0:T(8,128)}, u32[]{:S(2)}, u32[]{:S(2)}) collective-permute-start(f32[2,4,128,256]{3,2,1,0:T(8,128)} %collective-permute-done.24.refs_2_), channel_id=1, source_target_pairs={{1,2},{6,7},{9,8},{14,13},{17,18},{22,23},{25,24},{30,29}} | collective-permute-start | bytes 3145736 | tf_op jit(solution)/shard_map/ppermute | solution.py:531
  130.5 7.8 %collective-permute-start.19 = (f32[4,96,256]{2,1,0:T(8,128)S(1)}, f32[4,96,256]{2,1,0:T(8,128)S(1)}, u32[]{:S(2)}, u32[]{:S(2)}) collective-permute-start(f32[4,96,256]{2,1,0:T(8,128)S(1)} %pad_maximum_fusion.2), channel_id=1, source_target_pairs={{0,8},{1,9},{2,10},{3,11},{4,20},{5,21},{6,22},{7,23},{8,0},{9,1},... | collective-permute-start | bytes 1179656 | tf_op jit(solution)/shard_map/ppermute | solution.py:531
  130.6 32.7 %collective-permute-start.22 = (f32[2,4,128,256]{3,2,1,0:T(8,128)}, f32[2,4,128,256]{3,2,1,0:T(8,128)}, u32[]{:S(2)}, u32[]{:S(2)}) collective-permute-start(f32[2,4,128,256]{3,2,1,0:T(8,128)} %collective-permute-done.21.refs_2_), channel_id=1, source_target_pairs={{1,2},{6,7},{9,8},{14,13},{17,18},{22,23},{25,24},{30,29}} | collective-permute-start | bytes 3145736 | tf_op jit(solution)/shard_map/ppermute | solution.py:531
  139.4 24.0 %copy-start.3 = (f32[2,4,128,256]{3,2,1,0:T(8,128)S(1)}, f32[2,4,128,256]{3,2,1,0:T(8,128)}, u32[]{:S(2)}) copy-start(f32[2,4,128,256]{3,2,1,0:T(8,128)} %shard_map.45.refs_1_) | copy-start | bytes 3145732
  139.4 28.0 %collective-permute-start.20 = (f32[8,96,256]{2,1,0:T(8,128)}, f32[8,96,256]{2,1,0:T(8,128)}, u32[]{:S(2)}, u32[]{:S(2)}) collective-permute-start(f32[8,96,256]{2,1,0:T(8,128)} %pad_maximum_fusion.1), channel_id=1, source_target_pairs={{0,4},{1,5},{2,6},{3,7},{4,0},{5,1},{6,2},{7,3},{8,12},{9,13},{10,... | collective-permute-start | bytes 2359304 | tf_op jit(solution)/shard_map/ppermute | solution.py:531
  143.8 22.0 %copy-start.1 = (f32[8,128,256]{2,1,0:T(8,128)}, f32[8,128,256]{2,1,0:T(8,128)S(1)}, u32[]{:S(2)}) copy-start(f32[8,128,256]{2,1,0:T(8,128)S(1)} %add.64.refs_1_.refs_6_) | copy-start | bytes 3145732
  143.8 40.9 %collective-permute-start.3 = (f32[8,128,256]{2,1,0:T(8,128)S(1)}, f32[8,128,256]{2,1,0:T(8,128)}, u32[]{:S(2)}, u32[]{:S(2)}) collective-permute-start(f32[8,128,256]{2,1,0:T(8,128)S(1)} %add.64.refs_1_.refs_6_), channel_id=1, source_target_pairs={{0,4},{1,5},{2,6},{3,7},{4,0},{5,1},{6,2},{7,3},{8,12},{9,13},{10,... | collective-permute-start | bytes 3145736 | tf_op jit(solution)/shard_map/ppermute | solution.py:531
  148.6 69.1 %collective-permute-start.26 = (f32[2,4,128,256]{3,2,1,0:T(8,128)}, f32[2,4,128,256]{3,2,1,0:T(8,128)}, u32[]{:S(2)}, u32[]{:S(2)}) collective-permute-start(f32[2,4,128,256]{3,2,1,0:T(8,128)} %broadcast_select_fusion), channel_id=1, source_target_pairs={{2,3},{5,4},{10,11},{13,12},{18,19},{21,20},{26,27},{29,28}} | collective-permute-start | bytes 3145736 | tf_op jit(solution)/shard_map/ppermute | solution.py:531
  165.7 47.0 %collective-permute-start.23 = (f32[2,4,128,256]{3,2,1,0:T(8,128)}, f32[2,4,128,256]{3,2,1,0:T(8,128)}, u32[]{:S(2)}, u32[]{:S(2)}) collective-permute-start(f32[2,4,128,256]{3,2,1,0:T(8,128)} %broadcast_select_fusion.1), channel_id=1, source_target_pairs={{2,3},{5,4},{10,11},{13,12},{18,19},{21,20},{26,27},{29,28}} | collective-permute-start | bytes 3145736 | tf_op jit(solution)/shard_map/ppermute | solution.py:531
  169.9 20.9 %copy-start.13 = (s32[8]{0:T(128)S(1)}, s32[8]{0:T(128)}, u32[]{:S(2)}) copy-start(s32[8]{0:T(128)} %concatenate.12.refs_0_.info) | copy-start | bytes 100
  184.6 6.2 %copy-start = (f32[6,256,256]{2,1,0:T(8,128)S(1)}, f32[6,256,256]{2,1,0:T(8,128)}, u32[]{:S(2)}) copy-start(f32[6,256,256]{2,1,0:T(8,128)} %shard_map.43.refs_5_.refs_6_.refs_7_.refs_8_.refs_9_) | copy-start | bytes 4718596
  187.7 25.1 %copy-start.4 = (f32[2,4,128,256]{3,2,1,0:T(8,128)S(1)}, f32[2,4,128,256]{3,2,1,0:T(8,128)}, u32[]{:S(2)}) copy-start(f32[2,4,128,256]{3,2,1,0:T(8,128)} %shard_map.45.refs_1_) | copy-start | bytes 3145732
  187.7 50.2 %collective-permute-start.6 = (f32[2,4,128,256]{3,2,1,0:T(8,128)}, f32[2,4,128,256]{3,2,1,0:T(8,128)S(1)}, u32[]{:S(2)}, u32[]{:S(2)}) collective-permute-start(f32[2,4,128,256]{3,2,1,0:T(8,128)} %shard_map.42.refs_1_), channel_id=1, source_target_pairs={{0,3},{5,4},{10,11},{15,12},{16,19},{21,20},{26,27},{31,28}} | collective-permute-start | bytes 3145736 | tf_op jit(solution)/shard_map/ppermute | solution.py:531
  188.6 49.3 %collective-permute-start.5 = (f32[2,4,128,256]{3,2,1,0:T(8,128)}, f32[2,4,128,256]{3,2,1,0:T(8,128)S(1)}, u32[]{:S(2)}, u32[]{:S(2)}) collective-permute-start(f32[2,4,128,256]{3,2,1,0:T(8,128)} %shard_map.42.refs_1_), channel_id=1, source_target_pairs={{0,2},{5,7},{10,8},{15,13},{16,18},{21,23},{26,24},{31,29}} | collective-permute-start | bytes 3145736 | tf_op jit(solution)/shard_map/ppermute | solution.py:531
  189.9 48.1 %collective-permute-start.4 = (f32[2,4,128,256]{3,2,1,0:T(8,128)}, f32[2,4,128,256]{3,2,1,0:T(8,128)S(1)}, u32[]{:S(2)}, u32[]{:S(2)}) collective-permute-start(f32[2,4,128,256]{3,2,1,0:T(8,128)} %shard_map.42.refs_1_), channel_id=1, source_target_pairs={{0,1},{5,6},{10,9},{15,14},{16,17},{21,22},{26,25},{31,30}} | collective-permute-start | bytes 3145736 | tf_op jit(solution)/shard_map/ppermute | solution.py:531
  190.8 1.2 copy-start.7
  192.1 1.2 copy-start.9
  193.3 1.2 copy-start.12
  212.7 4.9 %copy-start.5 = (f32[2,4,128,256]{3,2,1,0:T(8,128)S(1)}, f32[2,4,128,256]{3,2,1,0:T(8,128)}, u32[]{:S(2)}) copy-start(f32[2,4,128,256]{3,2,1,0:T(8,128)} %shard_map.47.refs_1_) | copy-start | bytes 3145732
  212.8 15.2 %slice-start = ((s8[8388608]{0:T(1024)(128)(4,1)}), s8[4194304]{0:T(1024)(128)(4,1)S(1)}, s32[]{:S(2)}) async-start(s8[8388608]{0:T(1024)(128)(4,1)} %bitcast.17), calls=%async_computation | async-start | bytes 8388608
  217.7 10.3 %slice-start.1 = ((s8[8388608]{0:T(1024)(128)(4,1)}), s8[4194304]{0:T(1024)(128)(4,1)S(1)}, s32[]{:S(2)}) async-start(s8[8388608]{0:T(1024)(128)(4,1)} %bitcast.17), calls=%async_computation.1 | async-start | bytes 8388608
  228.0 10.0 %copy-start.2 = (f32[8,128,256]{2,1,0:T(8,128)S(1)}, f32[8,128,256]{2,1,0:T(8,128)}, u32[]{:S(2)}) copy-start(f32[8,128,256]{2,1,0:T(8,128)} %copy-done.1) | copy-start | bytes 3145732
  228.0 10.0 %copy-start.10 = (f32[2,4,128,256]{3,2,1,0:T(8,128)S(1)}, f32[2,4,128,256]{3,2,1,0:T(8,128)}, u32[]{:S(2)}) copy-start(f32[2,4,128,256]{3,2,1,0:T(8,128)} %shard_map.42.refs_1_) | copy-start | bytes 3145732

commit v3 on v2

--- a/solution.py
+++ b/solution.py
@@ -99,8 +99,7 @@
     return a * (a + 1) // 2 + b
 
 
-def chain_kernel(swap_ref, k_ref, out_ref, k_s, w_s, low_s, work_s):
-    n = k_ref.shape[-1]
+def chain_kernel(k_ref, out_ref, k_s, w_s, low_s, work_s):
     for i in range(k_ref.shape[0]):
         k_s[i] = k_ref[i]
     for s in range(PANELS):
@@ -108,17 +107,7 @@
         w = w_s[s]
         for k in range(s):
             out_ref[pair(s, k)] = dot6(w, low_s[pair(s, k)])
-        h = n // 2
-
-        @pl.when(swap_ref[0] == 0)
-        def _():
-            out_ref[pair(s, s)] = w
-
-        @pl.when(swap_ref[0] != 0)
-        def _():
-            out_ref[pair(s, s), :, :h] = w[:, h:]
-            out_ref[pair(s, s), :, h:] = w[:, :h]
-
+        out_ref[pair(s, s)] = w
         for a in range(s + 1, PANELS):
             low_s[pair(a, s)] = dot6(k_s[pair(a, s)], w, 1)
         for a in range(s + 1, PANELS):
@@ -126,17 +115,17 @@
                 k_s[pair(a, b)] = k_s[pair(a, b)] - dot6(low_s[pair(a, s)], low_s[pair(b, s)], 1)
 
 
-def chain(swap, corner):
+def chain(corner):
     count, n, _ = corner.shape
     return pl.pallas_call(
         chain_kernel,
         out_shape=jax.ShapeDtypeStruct(corner.shape, jnp.float32),
-        in_specs=[pl.BlockSpec(memory_space=pltpu.SMEM), pl.BlockSpec(memory_space=pltpu.VMEM)],
+        in_specs=[pl.BlockSpec(memory_space=pltpu.VMEM)],
         out_specs=pl.BlockSpec(memory_space=pltpu.VMEM),
         scratch_shapes=[pltpu.VMEM((count, n, n), jnp.float32), pltpu.VMEM((PANELS, n, n), jnp.float32),
                         pltpu.VMEM((count, n, n), jnp.float32), pltpu.VMEM((n, 2 * n), jnp.float32)],
         interpret=INTERPRET,
-    )(swap, corner)
+    )(corner)
 
 
 def spec(space=pltpu.VMEM):
@@ -155,11 +144,12 @@
     keeps, (gives, sem) = refs[:PANELS], refs[PANELS:]
     my_row, my_col, mine = info[PANELS], info[PANELS + 1], info[PANELS + 2]
     half = NB // 2
-    blk_cols = trailing.shape[1] // NB
+    count = trailing.shape[1] // NB // 2
+    stream = info[PANELS + 4]
 
     def copy(row, col, out):
         source = trailing.at[
-            pl.ds(pl.multiple_of(row, half), half), pl.ds(pl.multiple_of(col, NB), NB)
+            pl.ds(pl.multiple_of(row, half), out.shape[0]), pl.ds(pl.multiple_of(col, NB), NB)
         ]
         return pltpu.make_async_copy(source, out, sem)
 
@@ -179,9 +169,9 @@
         owner = lax.rem(info[s], rows) == my_row
         row = lax.div(info[s], rows) * NB
         jobs = []
-        for j in range(blk_cols):
-            jobs.append((row + mine * half, j * NB, keeps[s].at[j]))
-            jobs.append((row + (1 - mine) * half, j * NB, gives.at[s * blk_cols + j]))
+        for j in range(count):
+            jobs.append((row, (2 * j + stream) * NB, keeps[s].at[j]))
+            jobs.append((row, (2 * j + 1 - stream) * NB, gives.at[s * count + j]))
         plans.append((True, owner, jobs))
     for there, owner, jobs in plans:
 
@@ -204,11 +194,10 @@
 
 
 def gather(info, trailing, rows, cols):
-    half = NB // 2
-    blk_cols = trailing.shape[1] // NB
-    part = f32(PANELS * (PANELS + 1) // 2, half, NB)
-    shapes = [part, part] + [f32(blk_cols, half, NB)] * PANELS
-    shapes.append(f32(PANELS * blk_cols, half, NB))
+    count = trailing.shape[1] // NB // 2
+    part = f32(PANELS * (PANELS + 1) // 2, NB // 2, NB)
+    shapes = [part, part] + [f32(count, NB, NB)] * PANELS
+    shapes.append(f32(PANELS * count, NB, NB))
     return pl.pallas_call(
         lambda *refs: gather_kernel(rows, cols, *refs),
         out_shape=shapes,
@@ -244,11 +233,17 @@
     return pl.BlockSpec((1, NB, NB), lambda i: (pair(*name), 0, 0))
 
 
-def col_kernel(cols, info, *refs):
-    raw, solved = refs[: 2 * PANELS - 2], refs[2 * PANELS - 2 : -3]
-    parts, rest, left = refs[-3:]
-    block = pl.program_id(0) * cols + info[PANELS + 1]
-    last = PANELS - 1
+def col_kernel(first, cols, info, *refs):
+    width = (PANELS - 1 if first == 0 else PANELS) - first
+    raw, refs = refs[:width], refs[width:]
+    solved, refs = (refs[:-3], refs[-3:]) if first == 0 else (refs[:1], refs[1:])
+    block = (2 * pl.program_id(0) + info[PANELS + 4]) * cols + info[PANELS + 1]
+    if first:
+        rest, out = refs
+        fac = dot6(solved[0][0], raw[0][0]) - rest[0]
+        out[0, 0] = jnp.where(is_used(info, block, first), 0.0, fac)
+        return
+    out, rest, left = refs
 
     @pl.when(pl.program_id(0) == 0)
     def _():
@@ -256,42 +251,48 @@
             left[n] = left6(ref[0])
 
     facs = []
-    for s in range(last):
-        full = jnp.concatenate([raw[2 * s][0], raw[2 * s + 1][0]], axis=0)
-        fac = bdot(left[pair(s, s)], right6(full))
+    for s in range(width):
+        fac = bdot(left[pair(s, s)], right6(raw[s][0]))
         for k in range(s):
             fac = fac - bdot(left[pair(s, k)], facs[k])
         fac = jnp.where(is_used(info, block, s), 0.0, fac)
         facs.append(right6(fac))
-        for i, part in enumerate(halves(fac)):
-            at = (2 * s + i) * NB
-            parts[0, at : at + NB] = part
+        out[s, 0] = fac
     total = None
-    for k in range(last):
-        term = bdot(left[pair(last, k)], facs[k])
+    for k in range(width):
+        term = bdot(left[pair(width, k)], facs[k])
         total = term if total is None else total + term
     rest[0] = total
 
 
-def col_factor(cols, info, raw, solved):
+def col_factor(first, cols, info, raw, solved, rest):
     count = raw[0].shape[0]
-    last = PANELS - 1
-    names = [(a, b) for a in range(PANELS) for b in range(a + 1)][:-1]
-    part = pl.BlockSpec((1, NB // 2, NB), lambda i: (i, 0, 0))
+    width = len(raw)
+    one = pl.BlockSpec((1, NB, NB), lambda i: (i, 0, 0))
+    outs = [f32(width, count, NB, NB)]
+    specs = [pl.BlockSpec((width, 1, NB, NB), lambda i: (0, i, 0, 0))]
+    scratch = []
+    if first:
+        names = [(first, first)]
+    else:
+        names = [(a, b) for a in range(PANELS) for b in range(a + 1)][:-1]
+        outs.append(f32(count, NB, NB))
+        specs.append(one)
+        scratch.append(pltpu.VMEM((len(names), NB, 6 * NB), jnp.bfloat16))
     return pl.pallas_call(
-        lambda *refs: col_kernel(cols, *refs),
+        lambda *refs: col_kernel(first, cols, *refs),
         grid=(count,),
-        out_shape=[bf16(count, 2 * last * NB, NB), f32(count, NB, NB)],
-        in_specs=[spec(pltpu.SMEM)] + [part] * len(raw) + [block_of(n) for n in names],
-        out_specs=[
-            pl.BlockSpec((1, 2 * last * NB, NB), lambda i: (i, 0, 0)),
-            pl.BlockSpec((1, NB, NB), lambda i: (i, 0, 0)),
-        ],
-        scratch_shapes=[pltpu.VMEM((len(names), NB, 6 * NB), jnp.bfloat16)],
+        out_shape=outs,
+        in_specs=[spec(pltpu.SMEM)]
+        + [one] * width
+        + [block_of(n) for n in names]
+        + [one] * len(rest),
+        out_specs=specs,
+        scratch_shapes=scratch,
         compiler_params=params(),
         interpret=INTERPRET,
-        cost_estimate=cost(60 * count * NB**3, 12),
-    )(info, *raw, *[solved] * len(names))
+        cost_estimate=cost(12 * len(names) * count * NB**3, 8),
+    )(info, *raw, *[solved] * len(names), *rest)
 
 
 def fetch(info, sources, raw, sem):
@@ -317,8 +318,7 @@
     def _():
         fetch(info, sources, raw, sem)
 
-    full = jnp.concatenate([raw[0, step], raw[1, step]], axis=0)
-    fac = dot6(full.T, solved[s][0], 1)
+    fac = dot6(raw[step].T, solved[s][0], 1)
     facs = [ref[...] for ref in before]
     for k in range(s):
         fac = fac - dot6(facs[k], solved[k][0], 1)
@@ -337,7 +337,7 @@
 
 def row_factor(s, rows, info, sources, solved, before):
     raw = sources[0].shape
-    count = raw[1]
+    count = raw[0]
     height = count * NB
     names = [(s, k) for k in range(s + 1)]
     shapes = [f32(height, PANELS * NB), bf16(height, 2 * NB)]
@@ -370,32 +370,6 @@
     )(info, *sources, *[solved] * len(names), *before * s)
 
 
-def own_kernel(ratio, info, half, other, out, sem):
-    group = info[PANELS + 4]
-    copies = []
-    for h, part in enumerate((half, other)):
-        for i in range(out.shape[1]):
-            copies.append(
-                pltpu.make_async_copy(part.at[i * ratio + group], out.at[h, i], sem)
-            )
-    for copy in copies:
-        copy.start()
-    for copy in copies:
-        copy.wait()
-
-
-def own_rows(ratio, info, half, other):
-    return pl.pallas_call(
-        lambda *refs: own_kernel(ratio, *refs),
-        out_shape=f32(2, half.shape[0] // ratio, *half.shape[1:]),
-        in_specs=[spec(pltpu.SMEM), spec(pl.ANY), spec(pl.ANY)],
-        out_specs=spec(),
-        scratch_shapes=[pltpu.SemaphoreType.DMA],
-        interpret=INTERPRET,
-        cost_estimate=pl.CostEstimate(flops=0, bytes_accessed=2 << 20, transcendentals=0),
-    )(info, half, other)
-
-
 def set_left(left, parts):
     for k, part in enumerate(parts):
         for i, at in enumerate((0, 1, 0)):
@@ -403,76 +377,100 @@
             left[:, to : to + NB] = part[:, at * NB : (at + 1) * NB]
 
 
-def early_kernel(info, current, cparts, *refs):
-    rparts, out, left = refs[:-2], refs[-2], refs[-1]
+def set_right(right, own, other):
+    count = pl.num_programs(0) // 2
+    step = pl.program_id(0)
+    for there, fac in ((step < count, own), (step >= count, other)):
+
+        @pl.when(there)
+        def _():
+            for k in range(fac.shape[0]):
+                high, low = halves(fac[k, 0])
+                for i, part in enumerate((low, high, high)):
+                    to = (3 * k + i) * NB
+                    right[to : to + NB] = part
+
+
+def column_at(count, step, info):
+    stream = info[PANELS + 4]
+    mine = step < count
+    return 2 * jnp.where(mine, step, step - count) + jnp.where(mine, stream, 1 - stream)
+
+
+def update_specs(height, width, panels):
+    count = width // NB // 2
+    strip = pl.BlockSpec((height, NB), lambda i, info: (0, column_at(count, i, info)))
+    shape = (panels, 1, NB, NB)
+    own = pl.BlockSpec(shape, lambda i, info: (0, jnp.minimum(i, count - 1), 0, 0))
+    other = pl.BlockSpec(shape, lambda i, info: (0, jnp.maximum(i - count, 0), 0, 0))
+    return strip, own, other
+
+
+def early_kernel(info, current, own, other, *refs):
+    rparts, out, left, right = refs[:-3], *refs[-3:]
 
     @pl.when(pl.program_id(0) == 0)
     def _():
         set_left(left, rparts)
 
-    blocks = []
-    for k in range(len(rparts)):
-        high = cparts[0, 2 * k * NB : (2 * k + 1) * NB]
-        low = cparts[0, (2 * k + 1) * NB : (2 * k + 2) * NB]
-        blocks += [low, high, high]
-    right = jnp.concatenate(blocks, axis=0)
-    out[...] = current[...] - jnp.dot(left[...], right, preferred_element_type=jnp.float32)
-
-
-def early_update(info, current, cparts, rparts):
+    set_right(right, own, other)
+    product = jnp.dot(left[...], right[...], preferred_element_type=jnp.float32)
+    out[...] = current[...] - product
+
+
+def early_update(info, current, own, other, rparts):
     height, width = current.shape
-    strip = pl.BlockSpec((height, NB), lambda i: (0, i))
+    panels = len(rparts)
+    strip, mine, theirs = update_specs(height, width, panels)
     return pl.pallas_call(
         early_kernel,
-        grid=(width // NB,),
+        grid_spec=pltpu.PrefetchScalarGridSpec(
+            num_scalar_prefetch=1,
+            grid=(width // NB,),
+            in_specs=[strip, mine, theirs] + [spec()] * panels,
+            out_specs=strip,
+            scratch_shapes=[
+                pltpu.VMEM((height, 3 * panels * NB), jnp.bfloat16),
+                pltpu.VMEM((3 * panels * NB, NB), jnp.bfloat16),
+            ],
+        ),
         out_shape=f32(height, width),
-        in_specs=[
-            spec(pltpu.SMEM),
-            strip,
-            pl.BlockSpec((1,) + cparts.shape[1:], lambda i: (i, 0, 0)),
-        ]
-        + [spec()] * len(rparts),
-        out_specs=strip,
-        scratch_shapes=[pltpu.VMEM((height, 3 * len(rparts) * NB), jnp.bfloat16)],
         compiler_params=params(),
         interpret=INTERPRET,
         cost_estimate=cost(12 * height * width * NB, 24),
-    )(info, current, cparts, *rparts)
+    )(info, current, own, other, *rparts)
 
 
 def last_kernel(rows, cols, count, info, *refs):
     sources, refs = refs[:count], refs[count:]
-    current, half, other, rest, w, row_rest, _, out, fout = refs[:9]
-    raw, fac_s, parts, left, w6, sem, out_sem = refs[9:]
+    current, own, other, w, row_rest, _, out, fout = refs[:8]
+    raw, fac_s, left, right, sem, out_sem = refs[8:]
     last = PANELS - 1
     step = pl.program_id(0)
-    blk_rows = raw.shape[1]
+    blk_rows = raw.shape[0]
     write = pltpu.make_async_copy(fac_s, fout.at[:, pl.ds(last * NB, NB)], out_sem)
 
     @pl.when(step == 0)
     def _():
         fetch(info, sources, raw, sem)
-        w6[...] = left6(w[0])
+        split = right6(w[0], 1)
         for i in range(blk_rows):
             at = slice(i * NB, (i + 1) * NB)
-            full = jnp.concatenate([raw[0, i], raw[1, i]], axis=0)
-            fac = bdot(w6[...], right6(full)).T - row_rest[at]
+            fac = bdot(left6(raw[i].T), split, 1) - row_rest[at]
             fac = jnp.where(is_used(info, i * rows + info[PANELS], last), 0.0, fac)
             fac_s[at] = fac
             high, low = halves(fac)
-            parts[at, :NB] = high
-            parts[at, NB:] = low
-        set_left(left, [parts])
+            for k, part in enumerate((high, low, high)):
+                left[at, k * NB : (k + 1) * NB] = part
 
     @pl.when(step == 1)
     def _():
         write.start()
 
-    block = step * cols + info[PANELS + 1]
-    fac = bdot(w6[...], right6(jnp.concatenate([half[0], other[0]], axis=0))) - rest[0]
-    high, low = halves(jnp.where(is_used(info, block, last), 0.0, fac))
-    right = jnp.concatenate([low, high, high], axis=0)
-    value = current[...] - jnp.dot(left[...], right, preferred_element_type=jnp.float32)
+    set_right(right, own, other)
+    product = jnp.dot(left[...], right[...], preferred_element_type=jnp.float32)
+    value = current[...] - product
+    block = column_at(pl.num_programs(0) // 2, step, info) * cols + info[PANELS + 1]
     dead = is_used(info, block, PANELS)
     for i in range(blk_rows):
         used = dead | is_used(info, i * rows + info[PANELS], PANELS)
@@ -484,35 +482,35 @@
         write.wait()
 
 
-def last_update(rows, cols, info, sources, current, raw, rest, solved, row_rest, out):
+def last_update(rows, cols, info, sources, current, own, other, solved, row_rest, out):
     height, width = current.shape
-    strip = pl.BlockSpec((height, NB), lambda i: (0, i))
-    part = pl.BlockSpec((1, NB // 2, NB), lambda i: (i, 0, 0))
+    strip, mine, theirs = update_specs(height, width, 1)
     last = PANELS - 1
     count = len(sources)
+    w = pl.BlockSpec((1, NB, NB), lambda i, info: (pair(last, last), 0, 0))
     return pl.pallas_call(
         lambda *refs: last_kernel(rows, cols, count, *refs),
-        grid=(width // NB,),
+        grid_spec=pltpu.PrefetchScalarGridSpec(
+            num_scalar_prefetch=1,
+            grid=(width // NB,),
+            in_specs=[spec(pl.ANY)] * count
+            + [strip, mine, theirs, w, spec(), spec(pl.ANY)],
+            out_specs=[strip, spec(pl.ANY)],
+            scratch_shapes=[
+                pltpu.VMEM(sources[0].shape, jnp.float32),
+                pltpu.VMEM((height, NB), jnp.float32),
+                pltpu.VMEM((height, 3 * NB), jnp.bfloat16),
+                pltpu.VMEM((3 * NB, NB), jnp.bfloat16),
+                pltpu.SemaphoreType.DMA,
+                pltpu.SemaphoreType.DMA,
+            ],
+        ),
         out_shape=[f32(height, width), f32(*out.shape)],
-        in_specs=[spec(pltpu.SMEM)]
-        + [spec(pl.ANY)] * count
-        + [strip, part, part, pl.BlockSpec((1, NB, NB), lambda i: (i, 0, 0))]
-        + [block_of((last, last)), spec(), spec(pl.ANY)],
-        out_specs=[strip, spec(pl.ANY)],
-        scratch_shapes=[
-            pltpu.VMEM(sources[0].shape, jnp.float32),
-            pltpu.VMEM((height, NB), jnp.float32),
-            pltpu.VMEM((height, 2 * NB), jnp.bfloat16),
-            pltpu.VMEM((height, 3 * NB), jnp.bfloat16),
-            pltpu.VMEM((NB, 6 * NB), jnp.bfloat16),
-            pltpu.SemaphoreType.DMA,
-            pltpu.SemaphoreType.DMA,
-        ],
-        input_output_aliases={count + 7: 1},
+        input_output_aliases={count + 6: 1},
         compiler_params=params(),
         interpret=INTERPRET,
         cost_estimate=cost(6 * height * width * NB, 24),
-    )(info, *sources, current, *raw, rest, solved, row_rest, out)
+    )(info, *sources, current, own, other, solved, row_rest, out)
 
 
 class Net:
@@ -538,6 +536,17 @@
 
     def row_step(self, value, step, turn=0):
         return self.send(value, lambda r, c: (r ^ self.step_bit(step, (r + turn) & 1), c))
+
+    def stream(self, r, c):
+        return (r + c + r // self.cols) & 1
+
+    def raw_step(self, value, step):
+        def target(r, c):
+            g = self.stream(r, c)
+            to = r ^ self.step_bit(step, g)
+            return (to if self.stream(to, c) == g else to ^ 1, c)
+
+        return self.send(value, target)
 
     def col_step(self, value, bit):
         return self.send(value, lambda r, c: (r, c ^ bit))
@@ -618,38 +627,48 @@
     my_col = lax.axis_index("col")
     net = Net(rows, cols)
     mine = my_row & 1
-    _, loc_cols = trailing.shape
-    blk_cols = loc_cols // NB
+    loc_cols = trailing.shape[1]
+    count = loc_cols // NB // 2
     ratio = rows // cols
-    half = NB // 2
     group = lax.div(my_row, cols)
+    stream = (my_row + my_col + group) & 1
     code = source_code(net, my_row, my_col)
-    extra = jnp.stack([my_row, my_col, mine, code, group])
+    extra = jnp.stack([my_row, my_col, mine, code, stream])
     info = jnp.concatenate([panel[:PANELS], extra])
     is_source = my_col == lax.rem(my_row, cols)
 
     corner, corner_give, *keeps, gives = gather(info, trailing, rows, cols)
-    got = net.core(gives).reshape(PANELS, blk_cols, half, NB)
+    got = net.core(gives).reshape(PANELS, count, NB, NB)
     corner = corner + net.core(corner_give)
     corner = spread_corner(net, corner.reshape(rows, -1, NB), my_row, mine)
-    solved = chain(info[PANELS + 2 : PANELS + 3], corner.reshape(-1, NB, NB))
-
-    parts, sources = [], []
+    solved = chain(corner.reshape(-1, NB, NB))
+
+    raws, sources = [], []
     for s in range(PANELS):
-        part = keeps[s] + got[s]
+        raw = keeps[s] + got[s]
         for step in range(len(net.row_bits)):
-            part = part + net.row_step(part, step)
-        parts.append((part, net.core(part)))
-        own = own_rows(ratio, info, *parts[s])
+            raw = raw + net.raw_step(raw, step)
+        raws.append(raw)
+        own = raw
+        if ratio != 2:
+            other = net.core(raw)
+            even = jnp.where(stream == 0, raw, other)
+            odd = jnp.where(stream == 0, other, raw)
+            own = jnp.stack([even, odd], axis=1).reshape(-1, ratio, NB, NB)
+            own = lax.dynamic_index_in_dim(own, group, 1, keepdims=False)
         sources.append(spread_rows(net, own, is_source, s == PANELS - 1))
-    cparts, col_rest = col_factor(cols, info, [v for p in parts[:-1] for v in p], solved)
+    last = PANELS - 1
+    early, col_rest = col_factor(0, cols, info, raws[:last], solved, [])
+    early_other = net.core(early)
+    (late,) = col_factor(last, cols, info, raws[last:], solved, [col_rest])
+    late_other = net.core(late)
     out, rparts = (), []
-    for s in range(PANELS - 1):
+    for s in range(last):
         out, *got = row_factor(s, rows, info, sources[s], solved, [out])
         rparts.append(got[0])
-    current = early_update(info, trailing, cparts, rparts)
+    current = early_update(info, trailing, early, early_other, rparts)
     current, out = last_update(
-        rows, cols, info, sources[-1], current, parts[-1], col_rest, solved, got[1], out
+        rows, cols, info, sources[last], current, late, late_other, solved, got[1], out
     )
     return (out, current)
 

time: 253 us -> 235 us (0.929)
  the two profiles are of different devices: /device:TPU:6 before, /device:TPU:21 now
where the time goes in v3:
time: 235 us
  waiting for transfers between devices  69.3 us (29%)
  Pallas kernels  67.7 us (29%)
  starting transfers between devices  66.5 us (28%)
  other arithmetic  19.7 us (8%)
  local copies, waits for them, and re-layouts  10.1 us (4%)
    ppermute x26, waiting for transfers between devices, send(): return lax.ppermute(value, AXES, pairs)  69.3 us
    ppermute x26, starting transfers between devices, send(): return lax.ppermute(value, AXES, pairs)  66.5 us
    pallas_call x2, Pallas kernels, row_factor(): pl.pallas_call(lambda *refs: row_kernel(s, rows, len(sources), *refs), gr...  15 us
    pallas_call x1, Pallas kernels, chain(): pl.pallas_call(chain_kernel, out_shape=jax.ShapeDtypeStruct(corner.shape,...  14.5 us
    pallas_call x2, Pallas kernels, col_factor(): pl.pallas_call(lambda *refs: col_kernel(first, cols, *refs), grid=(count,...  11.6 us
    pallas_call x1, Pallas kernels, early_update(): pl.pallas_call(early_kernel, grid_spec=pltpu.PrefetchScalarGridSpec(num_s...  11.2 us
    pallas_call x1, Pallas kernels, last_update(): pl.pallas_call(lambda *refs: last_kernel(rows, cols, count, *refs), grid_...  9.37 us
    unnamed x34, local copies, waits for them, and re-layouts  8.74 us
  transfers between devices with their start and end apart: 26, of which 10 were waited for; matrix products, arithmetic and copies ran while one was open for 8% of the time, Pallas kernels for 22%

profile of v3, /device:TPU:21, one launch (start us, length us, event | category | flops | bytes accessed | tf_op | source)
XLA Modules:
  0.0 234.6 jit_solution(8043131017550221348)
XLA Ops:
  0.7 1.3 concatenate.12.refs_0_.info
  2.0 5.9 %shard_map.41 = (f32[6,128,256]{2,1,0:T(8,128)}, f32[6,128,256]{2,1,0:T(8,128)}, f32[4,256,256]{2,1,0:T(8,128)}, f32[4,256,256]{2,1,0:T(8,128)}, f32[4,256,256]{2,1,0:T(8,128)}, /*index=5*/f32[12,256,256]{2,1,0:T(8,128)}) custom-call(s32[8]{0:T(128)} %concatenate.12.refs_0_.info, f32[1024,2048]{1,0:T(8,128)} %current.1), custom_call_target="tpu_custom_call" | custom-call | bytes 16777216 | tf_op jit(solution)/shard_map/pallas_call | solution.py:201
  7.9 0.6 collective-permute-start
  8.5 0.1 collective-permute-start.10
  8.6 6.7 %collective-permute-done.10 = f32[6,128,256]{2,1,0:T(8,128)} collective-permute-done((f32[6,128,256]{2,1,0:T(8,128)}, f32[6,128,256]{2,1,0:T(8,128)}, u32[]{:S(2)}, u32[]{:S(2)}) %collective-permute-start.10) | collective-permute-done | bytes 786464 | tf_op jit(solution)/shard_map/ppermute | solution.py:529
  15.2 1.5 add.79
  16.8 0.1 collective-permute-start.11
  16.9 0.7 copy-done.6
  17.6 1.0 copy-done.5
  18.7 3.4 %slice_add_fusion = (f32[4,256,256]{2,1,0:T(8,128)S(1)}, f32[4,256,256]{2,1,0:T(8,128)S(1)}, f32[4,256,256]{2,1,0:T(8,128)}) fusion(f32[4,256,256]{2,1,0:T(8,128)S(1)} %copy-done.13, f32[12,256,256]{2,1,0:T(8,128)} %copy-done.5, f32[4,256,256]{2,1,0:T(8,128)S(1)} %copy-done.12, f32[4,256,256]{2,1,0:T(8,128)S(1)} %copy-done.14), kind=kLoop, calls=%fused_computation.1 | loop fusion | flops 786432 | bytes 9437184 | tf_op jit(solution)/shard_map/add | solution.py:648
  22.1 0.8 collective-permute-start.8
  22.9 0.6 collective-permute-start.6
  23.6 0.3 collective-permute-done.11
  23.9 1.0 bitcast_add_fusion
  25.0 0.6 collective-permute-start.12
  25.6 23.9 %collective-permute-done.12 = f32[2,96,256]{2,1,0:T(8,128)S(1)} collective-permute-done((f32[2,96,256]{2,1,0:T(8,128)S(1)}, f32[2,96,256]{2,1,0:T(8,128)S(1)}, u32[]{:S(2)}, u32[]{:S(2)}) %collective-permute-start.12) | collective-permute-done | bytes 196640 | tf_op jit(solution)/shard_map/ppermute | solution.py:529
  49.6 1.4 add.77
  51.0 2.1 collective-permute-start.9
  53.1 2.5 %collective-permute-done.13 = f32[2,96,256]{2,1,0:T(8,128)S(1)} collective-permute-done((f32[2,96,256]{2,1,0:T(8,128)S(1)}, f32[2,96,256]{2,1,0:T(8,128)S(1)}, u32[]{:S(2)}, u32[]{:S(2)}) %collective-permute-start.13) | collective-permute-done | bytes 196640 | tf_op jit(solution)/shard_map/ppermute | solution.py:529
  55.6 0.2 collective-permute-start.14
  55.8 2.3 add.74
  58.1 2.4 %collective-permute-start.7 = (f32[4,256,256]{2,1,0:T(8,128)}, f32[4,256,256]{2,1,0:T(8,128)}, u32[]{:S(2)}, u32[]{:S(2)}) collective-permute-start(f32[4,256,256]{2,1,0:T(8,128)} %add.74), channel_id=1, source_target_pairs={{0,20},{1,9},{2,22},{3,11},{4,12},{5,17},{6,14},{7,19},{8,28},{9,1... | collective-permute-start | bytes 3145736 | tf_op jit(solution)/shard_map/ppermute | solution.py:529
  60.5 2.9 %collective-permute-done.14 = f32[2,96,256]{2,1,0:T(8,128)S(1)} collective-permute-done((f32[2,96,256]{2,1,0:T(8,128)S(1)}, f32[2,96,256]{2,1,0:T(8,128)S(1)}, u32[]{:S(2)}, u32[]{:S(2)}) %collective-permute-start.14) | collective-permute-done | bytes 196640 | tf_op jit(solution)/shard_map/ppermute | solution.py:529
  63.5 0.9 collective-permute-start.15
  64.4 6.2 %collective-permute-done.15 = f32[2,96,256]{2,1,0:T(8,128)S(1)} collective-permute-done((f32[2,96,256]{2,1,0:T(8,128)S(1)}, f32[2,96,256]{2,1,0:T(8,128)S(1)}, u32[]{:S(2)}, u32[]{:S(2)}) %collective-permute-start.15) | collective-permute-done | bytes 196640 | tf_op jit(solution)/shard_map/ppermute | solution.py:529
  70.7 10.0 %collective-permute-start.16 = (f32[4,96,256]{2,1,0:T(8,128)S(1)}, f32[4,96,256]{2,1,0:T(8,128)}, u32[]{:S(2)}, u32[]{:S(2)}) collective-permute-start(f32[4,96,256]{2,1,0:T(8,128)S(1)} %pad_maximum_fusion.2), channel_id=1, source_target_pairs={{0,8},{1,9},{2,10},{3,11},{4,20},{5,21},{6,22},{7,23},{8,0},{9,1},... | collective-permute-start | bytes 1179656 | tf_op jit(solution)/shard_map/ppermute | solution.py:529
  80.7 0.1 add.78.refs_2_.refs_1_
  80.8 1.4 collective-permute-start.22
  82.3 1.7 add.75.refs_1_
  84.0 1.3 collective-permute-start.19
  85.3 1.0 collective-permute-done.16
  86.2 1.1 broadcast_select_fusion.5
  87.3 1.0 pad_maximum_fusion.1
  88.3 1.4 collective-permute-start.17
  89.7 0.5 collective-permute-start.1
  90.2 6.7 %collective-permute-done.22.refs_2_ = f32[4,256,256]{2,1,0:T(8,128)} collective-permute-done((f32[4,256,256]{2,1,0:T(8,128)S(1)}, f32[4,256,256]{2,1,0:T(8,128)}, u32[]{:S(2)}, u32[]{:S(2)}) %collective-permute-start.22) | collective-permute-done | bytes 1048608 | tf_op jit(solution)/shard_map/ppermute | solution.py:529
  96.9 2.3 collective-permute-start.23
  99.2 17.8 %collective-permute-done.19.refs_2_ = f32[4,256,256]{2,1,0:T(8,128)} collective-permute-done((f32[4,256,256]{2,1,0:T(8,128)S(1)}, f32[4,256,256]{2,1,0:T(8,128)}, u32[]{:S(2)}, u32[]{:S(2)}) %collective-permute-start.19) | collective-permute-done | bytes 1048608 | tf_op jit(solution)/shard_map/ppermute | solution.py:529
  117.0 1.3 collective-permute-start.20
  118.4 1.4 broadcast_select_fusion.3
  119.7 1.2 pad_maximum_fusion
  121.0 14.5 %shard_map.42.refs_3_.refs_4_.refs_5_.refs_6_.refs_7_.refs_8_.refs_2_ = f32[6,256,256]{2,1,0:T(8,128)} custom-call(f32[6,256,256]{2,1,0:T(8,128)} %bitcast.19), custom_call_target="tpu_custom_call" | custom-call | tf_op jit(solution)/shard_map/pallas_call | solution.py:120
  135.5 1.8 add.71
  137.3 0.1 collective-permute-start.2
  137.4 0.1 copy-done
  137.6 9.5 %shard_map.43 = (f32[2,4,256,256]{3,2,1,0:T(8,128)S(1)}, f32[4,256,256]{2,1,0:T(8,128)S(1)}) custom-call(s32[8]{0:T(128)S(1)} %copy-done.3, f32[4,256,256]{2,1,0:T(8,128)S(1)} %add.75.refs_1_, f32[4,256,256]{2,1,0:T(8,128)S(1)} %add.78.refs_2_.refs_1_, f32[6,256,256]{2,1,0:T(8,128)S(1)} %copy-done, f32[6,256,256]{2,1,0:T(8,128)S(1)} %copy-done, ...), custom_call_target="tpu_custom_call" | custom-call | flops 4026531840 | bytes 8388608 | tf_op jit(solution)/shard_map/pallas_call | solution.py:282
  147.1 0.1 collective-permute-start.18
  147.1 1.4 broadcast_select_fusion
  148.5 0.9 collective-permute-start.24
  149.4 0.1 broadcast_select_fusion.1
  149.6 0.7 collective-permute-start.21
  150.3 1.3 collective-permute-done.2
  151.6 0.1 add.72.refs_1_
  151.8 0.7 collective-permute-start.5
  152.5 0.7 collective-permute-start.4
  153.2 2.1 shard_map.47.refs_6_
  155.4 1.3 collective-permute-start.3
  156.7 35.2 %collective-permute-start.25 = (f32[1,4,256,256]{3,2,1,0:T(8,128)S(1)}, f32[1,4,256,256]{3,2,1,0:T(8,128)S(1)}, u32[]{:S(2)}, u32[]{:S(2)}) collective-permute-start(f32[1,4,256,256]{3,2,1,0:T(8,128)S(1)} %shard_map.47.refs_6_), channel_id=1, source_target_pairs={{0,4},{1,5},{2,6},{3,7},{4,0},{5,1},{6,2},{7,3},{8,12},{9,13},{10,... | collective-permute-start | bytes 3145736 | tf_op jit(solution)/shard_map/ppermute | solution.py:529
  191.9 4.8 %shard_map.44 = (f32[1024,768]{1,0:T(8,128)}, bf16[1024,512]{1,0:T(8,128)(2,1)S(1)}) custom-call(s32[8]{0:T(128)S(1)} %copy-done.3, f32[4,256,256]{2,1,0:T(8,128)S(1)} %add.75.refs_1_, f32[4,256,256]{2,1,0:T(8,128)} %collective-permute-done.19.refs_2_, f32[4,256,256]{2,1,0:T(8,128)S(1)} %collective-permute-done.20.refs_3_, ...), custom_call_target="tpu_custom_call" | custom-call | flops 805306368 | bytes 8388608 | tf_op jit(solution)/shard_map/pallas_call | solution.py:356
  196.8 10.2 %shard_map.45 = (f32[1024,768]{1,0:T(8,128)}, bf16[1024,512]{1,0:T(8,128)(2,1)S(1)}, f32[1024,256]{1,0:T(8,128)S(1)}) custom-call(s32[8]{0:T(128)S(1)} %copy-done.3, f32[4,256,256]{2,1,0:T(8,128)S(1)} %add.78.refs_2_.refs_1_, f32[4,256,256]{2,1,0:T(8,128)} %collective-permute-done.22.refs_2_, ...), custom_call_target="tpu_custom_call", output_to_operand_aliasing={{0}: (9, {})} | custom-call | flops 3221225472 | bytes 8388608 | tf_op jit(solution)/shard_map/pallas_call | solution.py:356
  207.0 11.2 %shard_map.46.refs_5_ = f32[1024,2048]{1,0:T(8,128)S(1)} custom-call(s32[8]{0:T(128)S(1)} %copy-done.3, f32[1024,2048]{1,0:T(8,128)S(1)} %bitcast.18, f32[2,4,256,256]{3,2,1,0:T(8,128)S(1)} %get-tuple-element.23.own, f32[2,4,256,256]{3,2,1,0:T(8,128)S(1)} %collective-permute-done.18.other, bf16[1024,512]{1,0:T(8,128)(2,1)S(1)} %get-tuple-element.24.refs_0_, ...), custom_call_target="tpu_custom_call" | custom-call | flops 6442450944 | bytes 25165824 | tf_op jit(solution)/shard_map/pallas_call | solution.py:425
  218.2 3.4 %copy-done.1 = f32[1024,2048]{1,0:T(8,128)} copy-done((f32[1024,2048]{1,0:T(8,128)}, f32[1024,2048]{1,0:T(8,128)S(1)}, u32[]{:S(2)}) %copy-start.1) | copy-done | bytes 8388632
  221.7 3.4 %copy-done.2 = f32[1024,2048]{1,0:T(8,128)S(1)} copy-done((f32[1024,2048]{1,0:T(8,128)S(1)}, f32[1024,2048]{1,0:T(8,128)}, u32[]{:S(2)}) %copy-start.2) | copy-done | bytes 8388632
  225.0 9.4 %shard_map.48 = (f32[1024,2048]{1,0:T(8,128)}, f32[1024,768]{1,0:T(8,128)}) custom-call(s32[8]{0:T(128)S(1)} %copy-done.3, f32[4,256,256]{2,1,0:T(8,128)S(1)} %add.72.refs_1_, f32[4,256,256]{2,1,0:T(8,128)S(1)} %collective-permute-done.3.refs_2_, f32[4,256,256]{2,1,0:T(8,128)S(1)} %collective-permute-done.4.refs_3_, ...), custom_call_target="tpu_custom_call", output_to_operand_aliasing={{1}: (10, {})} | custom-call | flops 3221225472 | bytes 25165824 | tf_op jit(solution)/shard_map/pallas_call | solution.py:491
  (54 shorter events, 0.4 us)
Async XLA Ops:
  7.9 9.0 %collective-permute-start = (f32[12,256,256]{2,1,0:T(8,128)}, f32[12,256,256]{2,1,0:T(8,128)S(1)}, u32[]{:S(2)}, u32[]{:S(2)}) collective-permute-start(f32[12,256,256]{2,1,0:T(8,128)} %get-tuple-element.18), channel_id=1, source_target_pairs={{0,4},{1,5},{2,6},{3,7},{4,0},{5,1},{6,2},{7,3},{8,12},{9,13},{10,... | collective-permute-start | bytes 9437192 | tf_op jit(solution)/shard_map/ppermute | solution.py:529
  8.5 6.8 %collective-permute-start.10 = (f32[6,128,256]{2,1,0:T(8,128)}, f32[6,128,256]{2,1,0:T(8,128)}, u32[]{:S(2)}, u32[]{:S(2)}) collective-permute-start(f32[6,128,256]{2,1,0:T(8,128)} %get-tuple-element.22), channel_id=1, source_target_pairs={{0,4},{1,5},{2,6},{3,7},{4,0},{5,1},{6,2},{7,3},{8,12},{9,13},{10,... | collective-permute-start | bytes 2359304 | tf_op jit(solution)/shard_map/ppermute | solution.py:529
  8.6 10.1 %copy-start.12 = (f32[4,256,256]{2,1,0:T(8,128)S(1)}, f32[4,256,256]{2,1,0:T(8,128)}, u32[]{:S(2)}) copy-start(f32[4,256,256]{2,1,0:T(8,128)} %get-tuple-element.19) | copy-start | bytes 3145732
  8.6 10.1 %copy-start.13 = (f32[4,256,256]{2,1,0:T(8,128)S(1)}, f32[4,256,256]{2,1,0:T(8,128)}, u32[]{:S(2)}) copy-start(f32[4,256,256]{2,1,0:T(8,128)} %get-tuple-element.20) | copy-start | bytes 3145732
  8.6 10.1 %copy-start.14 = (f32[4,256,256]{2,1,0:T(8,128)S(1)}, f32[4,256,256]{2,1,0:T(8,128)}, u32[]{:S(2)}) copy-start(f32[4,256,256]{2,1,0:T(8,128)} %get-tuple-element.17) | copy-start | bytes 3145732
  16.7 0.9 copy-start.6
  16.8 7.1 %collective-permute-start.11 = (f32[4,96,256]{2,1,0:T(8,128)S(1)}, f32[4,96,256]{2,1,0:T(8,128)}, u32[]{:S(2)}, u32[]{:S(2)}) collective-permute-start(f32[4,96,256]{2,1,0:T(8,128)S(1)} %dynamic-slice_bitcast_fusion), channel_id=1, source_target_pairs={{0,8},{1,9},{2,10},{3,11},{4,20},{5,21},{6,22},{7,23},{8,0},{9,1},... | collective-permute-start | bytes 1179656 | tf_op jit(solution)/shard_map/ppermute | solution.py:529
  16.9 1.8 copy-start.5
  18.7 5.2 %copy-start.7 = (f32[6,128,256]{2,1,0:T(8,128)S(1)}, f32[6,128,256]{2,1,0:T(8,128)}, u32[]{:S(2)}) copy-start(f32[6,128,256]{2,1,0:T(8,128)} %copy-done.6) | copy-start | bytes 2359300
  22.1 27.5 %collective-permute-start.8 = (f32[4,256,256]{2,1,0:T(8,128)S(1)}, f32[4,256,256]{2,1,0:T(8,128)}, u32[]{:S(2)}, u32[]{:S(2)}) collective-permute-start(f32[4,256,256]{2,1,0:T(8,128)S(1)} %get-tuple-element.32), channel_id=1, source_target_pairs={{0,8},{1,21},{2,10},{3,23},{4,16},{5,13},{6,18},{7,15},{8,0},{9,29... | collective-permute-start | bytes 3145736 | tf_op jit(solution)/shard_map/ppermute | solution.py:529
  22.9 32.9 %collective-permute-start.6 = (f32[4,256,256]{2,1,0:T(8,128)S(1)}, f32[4,256,256]{2,1,0:T(8,128)}, u32[]{:S(2)}, u32[]{:S(2)}) collective-permute-start(f32[4,256,256]{2,1,0:T(8,128)S(1)} %get-tuple-element.33), channel_id=1, source_target_pairs={{0,8},{1,21},{2,10},{3,23},{4,16},{5,13},{6,18},{7,15},{8,0},{9,29... | collective-permute-start | bytes 3145736 | tf_op jit(solution)/shard_map/ppermute | solution.py:529
  25.0 24.5 %collective-permute-start.12 = (f32[2,96,256]{2,1,0:T(8,128)S(1)}, f32[2,96,256]{2,1,0:T(8,128)S(1)}, u32[]{:S(2)}, u32[]{:S(2)}) collective-permute-start(f32[2,96,256]{2,1,0:T(8,128)S(1)} %dynamic-slice_bitcast_fusion.1), channel_id=1, source_target_pairs={{0,16},{1,17},{2,18},{3,19},{4,12},{5,13},{6,14},{7,15},{8,24},{9,... | collective-permute-start | bytes 589832 | tf_op jit(solution)/shard_map/ppermute | solution.py:529
  49.5 6.1 %collective-permute-start.13 = (f32[2,96,256]{2,1,0:T(8,128)S(1)}, f32[2,96,256]{2,1,0:T(8,128)S(1)}, u32[]{:S(2)}, u32[]{:S(2)}) collective-permute-start(f32[2,96,256]{2,1,0:T(8,128)S(1)} %bitcast_add_fusion.1), channel_id=1, source_target_pairs={{0,1},{1,0},{2,3},{3,2},{4,5},{5,4},{6,7},{7,6},{8,9},{9,8},{10,11... | collective-permute-start | bytes 589832 | tf_op jit(solution)/shard_map/ppermute | solution.py:529
  51.0 29.7 %collective-permute-start.9 = (f32[4,256,256]{2,1,0:T(8,128)S(1)}, f32[4,256,256]{2,1,0:T(8,128)S(1)}, u32[]{:S(2)}, u32[]{:S(2)}) collective-permute-start(f32[4,256,256]{2,1,0:T(8,128)S(1)} %add.77), channel_id=1, source_target_pairs={{0,20},{1,9},{2,22},{3,11},{4,12},{5,17},{6,14},{7,19},{8,28},{9,1... | collective-permute-start | bytes 3145736 | tf_op jit(solution)/shard_map/ppermute | solution.py:529
  55.6 7.8 %collective-permute-start.14 = (f32[2,96,256]{2,1,0:T(8,128)S(1)}, f32[2,96,256]{2,1,0:T(8,128)S(1)}, u32[]{:S(2)}, u32[]{:S(2)}) collective-permute-start(f32[2,96,256]{2,1,0:T(8,128)S(1)} %add.86), channel_id=1, source_target_pairs={{0,2},{1,3},{2,0},{3,1},{4,6},{5,7},{6,4},{7,5},{8,10},{9,11},{10,... | collective-permute-start | bytes 589832 | tf_op jit(solution)/shard_map/ppermute | solution.py:529
  58.1 24.1 %collective-permute-start.7 = (f32[4,256,256]{2,1,0:T(8,128)}, f32[4,256,256]{2,1,0:T(8,128)}, u32[]{:S(2)}, u32[]{:S(2)}) collective-permute-start(f32[4,256,256]{2,1,0:T(8,128)} %add.74), channel_id=1, source_target_pairs={{0,20},{1,9},{2,22},{3,11},{4,12},{5,17},{6,14},{7,19},{8,28},{9,1... | collective-permute-start | bytes 3145736 | tf_op jit(solution)/shard_map/ppermute | solution.py:529
  63.5 7.1 %collective-permute-start.15 = (f32[2,96,256]{2,1,0:T(8,128)S(1)}, f32[2,96,256]{2,1,0:T(8,128)S(1)}, u32[]{:S(2)}, u32[]{:S(2)}) collective-permute-start(f32[2,96,256]{2,1,0:T(8,128)S(1)} %add.87), channel_id=1, source_target_pairs={{0,16},{1,17},{2,18},{3,19},{4,12},{5,13},{6,14},{7,15},{8,24},{9,... | collective-permute-start | bytes 589832 | tf_op jit(solution)/shard_map/ppermute | solution.py:529
  70.6 10.0 %copy-start.8 = (f32[2,96,256]{2,1,0:T(8,128)}, f32[2,96,256]{2,1,0:T(8,128)S(1)}, u32[]{:S(2)}) copy-start(f32[2,96,256]{2,1,0:T(8,128)S(1)} %get-tuple-element.39) | copy-start | bytes 589828
  70.6 10.0 %copy-start.10 = (f32[2,96,256]{2,1,0:T(8,128)}, f32[2,96,256]{2,1,0:T(8,128)S(1)}, u32[]{:S(2)}) copy-start(f32[2,96,256]{2,1,0:T(8,128)S(1)} %get-tuple-element.40) | copy-start | bytes 589828
  70.7 15.6 %collective-permute-start.16 = (f32[4,96,256]{2,1,0:T(8,128)S(1)}, f32[4,96,256]{2,1,0:T(8,128)}, u32[]{:S(2)}, u32[]{:S(2)}) collective-permute-start(f32[4,96,256]{2,1,0:T(8,128)S(1)} %pad_maximum_fusion.2), channel_id=1, source_target_pairs={{0,8},{1,9},{2,10},{3,11},{4,20},{5,21},{6,22},{7,23},{8,0},{9,1},... | collective-permute-start | bytes 1179656 | tf_op jit(solution)/shard_map/ppermute | solution.py:529
  80.8 5.4 %copy-start.9 = (f32[2,96,256]{2,1,0:T(8,128)S(1)}, f32[2,96,256]{2,1,0:T(8,128)}, u32[]{:S(2)}) copy-start(f32[2,96,256]{2,1,0:T(8,128)} %copy-done.8) | copy-start | bytes 589828
  80.8 5.4 %copy-start.11 = (f32[2,96,256]{2,1,0:T(8,128)S(1)}, f32[2,96,256]{2,1,0:T(8,128)}, u32[]{:S(2)}) copy-start(f32[2,96,256]{2,1,0:T(8,128)} %copy-done.10) | copy-start | bytes 589828
  80.8 16.1 %collective-permute-start.22 = (f32[4,256,256]{2,1,0:T(8,128)S(1)}, f32[4,256,256]{2,1,0:T(8,128)}, u32[]{:S(2)}, u32[]{:S(2)}) collective-permute-start(f32[4,256,256]{2,1,0:T(8,128)S(1)} %add.78.refs_2_.refs_1_), channel_id=1, source_target_pairs={{0,1},{5,6},{10,9},{15,14},{16,17},{21,22},{26,25},{31,30}} | collective-permute-start | bytes 3145736 | tf_op jit(solution)/shard_map/ppermute | solution.py:529
  84.0 33.0 %collective-permute-start.19 = (f32[4,256,256]{2,1,0:T(8,128)S(1)}, f32[4,256,256]{2,1,0:T(8,128)}, u32[]{:S(2)}, u32[]{:S(2)}) collective-permute-start(f32[4,256,256]{2,1,0:T(8,128)S(1)} %add.75.refs_1_), channel_id=1, source_target_pairs={{0,1},{5,6},{10,9},{15,14},{16,17},{21,22},{26,25},{31,30}} | collective-permute-start | bytes 3145736 | tf_op jit(solution)/shard_map/ppermute | solution.py:529
  87.3 11.9 %copy-start.4 = (f32[4,96,256]{2,1,0:T(8,128)}, f32[4,96,256]{2,1,0:T(8,128)S(1)}, u32[]{:S(2)}) copy-start(f32[4,96,256]{2,1,0:T(8,128)S(1)} %get-tuple-element.38) | copy-start | bytes 1179652
  88.3 30.1 %collective-permute-start.17 = (f32[8,96,256]{2,1,0:T(8,128)}, f32[8,96,256]{2,1,0:T(8,128)}, u32[]{:S(2)}, u32[]{:S(2)}) collective-permute-start(f32[8,96,256]{2,1,0:T(8,128)} %pad_maximum_fusion.1), channel_id=1, source_target_pairs={{0,4},{1,5},{2,6},{3,7},{4,0},{5,1},{6,2},{7,3},{8,12},{9,13},{10,... | collective-permute-start | bytes 2359304 | tf_op jit(solution)/shard_map/ppermute | solution.py:529
  89.7 45.8 %collective-permute-start.1 = (f32[4,256,256]{2,1,0:T(8,128)}, f32[4,256,256]{2,1,0:T(8,128)}, u32[]{:S(2)}, u32[]{:S(2)}) collective-permute-start(f32[4,256,256]{2,1,0:T(8,128)} %get-tuple-element.34), channel_id=1, source_target_pairs={{0,8},{1,21},{2,10},{3,23},{4,16},{5,13},{6,18},{7,15},{8,0},{9,29... | collective-permute-start | bytes 3145736 | tf_op jit(solution)/shard_map/ppermute | solution.py:529
  96.9 50.2 %collective-permute-start.23 = (f32[4,256,256]{2,1,0:T(8,128)}, f32[4,256,256]{2,1,0:T(8,128)}, u32[]{:S(2)}, u32[]{:S(2)}) collective-permute-start(f32[4,256,256]{2,1,0:T(8,128)} %collective-permute-done.22.refs_2_), channel_id=1, source_target_pairs={{1,2},{6,7},{9,8},{14,13},{17,18},{22,23},{25,24},{30,29}} | collective-permute-start | bytes 3145736 | tf_op jit(solution)/shard_map/ppermute | solution.py:529
  117.0 32.4 %collective-permute-start.20 = (f32[4,256,256]{2,1,0:T(8,128)}, f32[4,256,256]{2,1,0:T(8,128)S(1)}, u32[]{:S(2)}, u32[]{:S(2)}) collective-permute-start(f32[4,256,256]{2,1,0:T(8,128)} %collective-permute-done.19.refs_2_), channel_id=1, source_target_pairs={{1,2},{6,7},{9,8},{14,13},{17,18},{22,23},{25,24},{30,29}} | collective-permute-start | bytes 3145736 | tf_op jit(solution)/shard_map/ppermute | solution.py:529
  121.0 16.4 %copy-start.3 = (s32[8]{0:T(128)S(1)}, s32[8]{0:T(128)}, u32[]{:S(2)}) copy-start(s32[8]{0:T(128)} %concatenate.12.refs_0_.info) | copy-start | bytes 100
  135.5 2.0 copy-start
  137.3 14.3 %collective-permute-start.2 = (f32[4,256,256]{2,1,0:T(8,128)S(1)}, f32[4,256,256]{2,1,0:T(8,128)S(1)}, u32[]{:S(2)}, u32[]{:S(2)}) collective-permute-start(f32[4,256,256]{2,1,0:T(8,128)S(1)} %add.71), channel_id=1, source_target_pairs={{0,20},{1,9},{2,22},{3,11},{4,12},{5,17},{6,14},{7,19},{8,28},{9,1... | collective-permute-start | bytes 3145736 | tf_op jit(solution)/shard_map/ppermute | solution.py:529
  147.1 60.0 %collective-permute-start.18 = (f32[2,4,256,256]{3,2,1,0:T(8,128)S(1)}, f32[2,4,256,256]{3,2,1,0:T(8,128)S(1)}, u32[]{:S(2)}, u32[]{:S(2)}) collective-permute-start(f32[2,4,256,256]{3,2,1,0:T(8,128)S(1)} %get-tuple-element.23.own), channel_id=1, source_target_pairs={{0,4},{1,5},{2,6},{3,7},{4,0},{5,1},{6,2},{7,3},{8,12},{9,13},{10,... | collective-permute-start | bytes 6291464 | tf_op jit(solution)/shard_map/ppermute | solution.py:529
  148.5 6.9 %collective-permute-start.24 = (f32[4,256,256]{2,1,0:T(8,128)S(1)}, f32[4,256,256]{2,1,0:T(8,128)S(1)}, u32[]{:S(2)}, u32[]{:S(2)}) collective-permute-start(f32[4,256,256]{2,1,0:T(8,128)S(1)} %broadcast_select_fusion), channel_id=1, source_target_pairs={{2,3},{5,4},{10,11},{13,12},{18,19},{21,20},{26,27},{29,28}} | collective-permute-start | bytes 3145736 | tf_op jit(solution)/shard_map/ppermute | solution.py:529
  149.6 7.1 %collective-permute-start.21 = (f32[4,256,256]{2,1,0:T(8,128)S(1)}, f32[4,256,256]{2,1,0:T(8,128)S(1)}, u32[]{:S(2)}, u32[]{:S(2)}) collective-permute-start(f32[4,256,256]{2,1,0:T(8,128)S(1)} %broadcast_select_fusion.1), channel_id=1, source_target_pairs={{2,3},{5,4},{10,11},{13,12},{18,19},{21,20},{26,27},{29,28}} | collective-permute-start | bytes 3145736 | tf_op jit(solution)/shard_map/ppermute | solution.py:529
  151.8 69.9 %collective-permute-start.5 = (f32[4,256,256]{2,1,0:T(8,128)S(1)}, f32[4,256,256]{2,1,0:T(8,128)S(1)}, u32[]{:S(2)}, u32[]{:S(2)}) collective-permute-start(f32[4,256,256]{2,1,0:T(8,128)S(1)} %add.72.refs_1_), channel_id=1, source_target_pairs={{0,3},{5,4},{10,11},{15,12},{16,19},{21,20},{26,27},{31,28}} | collective-permute-start | bytes 3145736 | tf_op jit(solution)/shard_map/ppermute | solution.py:529
  152.5 69.1 %collective-permute-start.4 = (f32[4,256,256]{2,1,0:T(8,128)S(1)}, f32[4,256,256]{2,1,0:T(8,128)S(1)}, u32[]{:S(2)}, u32[]{:S(2)}) collective-permute-start(f32[4,256,256]{2,1,0:T(8,128)S(1)} %add.72.refs_1_), channel_id=1, source_target_pairs={{0,2},{5,7},{10,8},{15,13},{16,18},{21,23},{26,24},{31,29}} | collective-permute-start | bytes 3145736 | tf_op jit(solution)/shard_map/ppermute | solution.py:529
  155.4 66.2 %collective-permute-start.3 = (f32[4,256,256]{2,1,0:T(8,128)S(1)}, f32[4,256,256]{2,1,0:T(8,128)S(1)}, u32[]{:S(2)}, u32[]{:S(2)}) collective-permute-start(f32[4,256,256]{2,1,0:T(8,128)S(1)} %add.72.refs_1_), channel_id=1, source_target_pairs={{0,1},{5,6},{10,9},{15,14},{16,17},{21,22},{26,25},{31,30}} | collective-permute-start | bytes 3145736 | tf_op jit(solution)/shard_map/ppermute | solution.py:529
  156.7 64.9 %collective-permute-start.25 = (f32[1,4,256,256]{3,2,1,0:T(8,128)S(1)}, f32[1,4,256,256]{3,2,1,0:T(8,128)S(1)}, u32[]{:S(2)}, u32[]{:S(2)}) collective-permute-start(f32[1,4,256,256]{3,2,1,0:T(8,128)S(1)} %shard_map.47.refs_6_), channel_id=1, source_target_pairs={{0,4},{1,5},{2,6},{3,7},{4,0},{5,1},{6,2},{7,3},{8,12},{9,13},{10,... | collective-permute-start | bytes 3145736 | tf_op jit(solution)/shard_map/ppermute | solution.py:529
  191.9 15.1 %slice-start = ((s8[8388608]{0:T(1024)(128)(4,1)}), s8[4194304]{0:T(1024)(128)(4,1)S(1)}, s32[]{:S(2)}) async-start(s8[8388608]{0:T(1024)(128)(4,1)} %bitcast.17), calls=%async_computation | async-start | bytes 8388608
  196.7 10.3 %slice-start.1 = ((s8[8388608]{0:T(1024)(128)(4,1)}), s8[4194304]{0:T(1024)(128)(4,1)S(1)}, s32[]{:S(2)}) async-start(s8[8388608]{0:T(1024)(128)(4,1)} %bitcast.17), calls=%async_computation.1 | async-start | bytes 8388608
  218.2 3.4 %copy-start.1 = (f32[1024,2048]{1,0:T(8,128)}, f32[1024,2048]{1,0:T(8,128)S(1)}, u32[]{:S(2)}) copy-start(f32[1024,2048]{1,0:T(8,128)S(1)} %shard_map.46.refs_5_) | copy-start | bytes 25165828
  221.7 3.4 %copy-start.2 = (f32[1024,2048]{1,0:T(8,128)S(1)}, f32[1024,2048]{1,0:T(8,128)}, u32[]{:S(2)}) copy-start(f32[1024,2048]{1,0:T(8,128)} %copy-done.1) | copy-start | bytes 25165828

commit v4 on v3

--- a/solution.py
+++ b/solution.py
@@ -142,10 +142,10 @@
 
 def gather_kernel(rows, cols, info, trailing, corner_keep, corner_give, *refs):
     keeps, (gives, sem) = refs[:PANELS], refs[PANELS:]
-    my_row, my_col, mine = info[PANELS], info[PANELS + 1], info[PANELS + 2]
+    my_row, my_col = info[PANELS], info[PANELS + 1]
     half = NB // 2
     count = trailing.shape[1] // NB // 2
-    stream = info[PANELS + 4]
+    stream = info[PANELS + 3]
 
     def copy(row, col, out):
         source = trailing.at[
@@ -159,7 +159,7 @@
             n = pair(a, b)
             owner = (lax.rem(info[a], rows) == my_row) & (lax.rem(info[b], cols) == my_col)
             per = PANELS * (PANELS + 1) // 4
-            place = (n // per == mine, n % per)
+            place = (n // per == stream, n % per)
             row, col = lax.div(info[a], rows) * NB, lax.div(info[b], cols) * NB
             for keep in (True, False):
                 out = corner_keep if keep else corner_give
@@ -237,7 +237,7 @@
     width = (PANELS - 1 if first == 0 else PANELS) - first
     raw, refs = refs[:width], refs[width:]
     solved, refs = (refs[:-3], refs[-3:]) if first == 0 else (refs[:1], refs[1:])
-    block = (2 * pl.program_id(0) + info[PANELS + 4]) * cols + info[PANELS + 1]
+    block = (2 * pl.program_id(0) + info[PANELS + 3]) * cols + info[PANELS + 1]
     if first:
         rest, out = refs
         fac = dot6(solved[0][0], raw[0][0]) - rest[0]
@@ -298,7 +298,7 @@
 def fetch(info, sources, raw, sem):
     for which, source in enumerate(sources):
 
-        @pl.when(info[PANELS + 3] == which)
+        @pl.when(info[PANELS + 2] == which)
         def _():
             copy = pltpu.make_async_copy(source, raw, sem)
             copy.start()
@@ -358,7 +358,7 @@
         grid=(count,),
         out_shape=shapes,
         in_specs=[spec(pltpu.SMEM)]
-        + [spec(pl.ANY)] * len(sources)
+        + [spec(pltpu.HBM)] * len(sources)
         + [block_of(n) for n in names]
         + [column(k) for k in range(s)],
         out_specs=specs,
@@ -392,7 +392,7 @@
 
 
 def column_at(count, step, info):
-    stream = info[PANELS + 4]
+    stream = info[PANELS + 3]
     mine = step < count
     return 2 * jnp.where(mine, step, step - count) + jnp.where(mine, stream, 1 - stream)
 
@@ -493,7 +493,7 @@
         grid_spec=pltpu.PrefetchScalarGridSpec(
             num_scalar_prefetch=1,
             grid=(width // NB,),
-            in_specs=[spec(pl.ANY)] * count
+            in_specs=[spec(pltpu.HBM)] * count
             + [strip, mine, theirs, w, spec(), spec(pl.ANY)],
             out_specs=[strip, spec(pl.ANY)],
             scratch_shapes=[
@@ -534,9 +534,6 @@
     def step_bit(self, step, core):
         return self.row_bits[(step + core) % len(self.row_bits)]
 
-    def row_step(self, value, step, turn=0):
-        return self.send(value, lambda r, c: (r ^ self.step_bit(step, (r + turn) & 1), c))
-
     def stream(self, r, c):
         return (r + c + r // self.cols) & 1
 
@@ -548,36 +545,42 @@
 
         return self.send(value, target)
 
+    def stream_step(self, value, bit):
+        def target(r, c):
+            to = c ^ bit
+            return (r if self.stream(r, to) == self.stream(r, c) else r ^ 1, to)
+
+        return self.send(value, target)
+
     def col_step(self, value, bit):
         return self.send(value, lambda r, c: (r, c ^ bit))
 
-    def my_bit(self, my_row, mine, step, turn):
-        even = (my_row & self.step_bit(step, turn)) != 0
-        odd = (my_row & self.step_bit(step, 1 - turn)) != 0
-        return jnp.where(mine == 0, even, odd).astype(jnp.int32)
+    def my_bit(self, my_row, stream, step):
+        even = (my_row & self.step_bit(step, 0)) != 0
+        odd = (my_row & self.step_bit(step, 1)) != 0
+        return jnp.where(stream == 0, even, odd).astype(jnp.int32)
 
 
 def pick(value, index):
     return lax.dynamic_index_in_dim(value, index, 0, keepdims=False)
 
 
-def spread_corner(net, part, my_row, mine):
+def spread_corner(net, part, my_row, stream):
     tail = part.shape[1:]
     bits = []
-    turn = 0
     for step in range(len(net.row_bits)):
-        bit = net.my_bit(my_row, mine, step, turn)
+        bit = net.my_bit(my_row, stream, step)
         bits.append(bit)
         part = part.reshape((2, -1) + tail)
-        part = pick(part, bit) + net.row_step(pick(part, 1 - bit), step, turn)
+        part = pick(part, bit) + net.raw_step(pick(part, 1 - bit), step)
     for bit in net.col_bits:
-        part = part + net.col_step(part, bit)
+        part = part + net.stream_step(part, bit)
     for step in reversed(range(len(net.row_bits))):
-        other = net.row_step(part, step, turn)
+        other = net.raw_step(part, step)
         low = bits[step] == 0
         part = jnp.concatenate([jnp.where(low, part, other), jnp.where(low, other, part)])
     other = net.core(part)
-    low = mine == 0
+    low = stream == 0
     return jnp.concatenate([jnp.where(low, part, other), jnp.where(low, other, part)])
 
 
@@ -626,26 +629,31 @@
     my_row = lax.axis_index("row")
     my_col = lax.axis_index("col")
     net = Net(rows, cols)
-    mine = my_row & 1
     loc_cols = trailing.shape[1]
     count = loc_cols // NB // 2
     ratio = rows // cols
     group = lax.div(my_row, cols)
     stream = (my_row + my_col + group) & 1
     code = source_code(net, my_row, my_col)
-    extra = jnp.stack([my_row, my_col, mine, code, stream])
+    extra = jnp.stack([my_row, my_col, code, stream])
     info = jnp.concatenate([panel[:PANELS], extra])
     is_source = my_col == lax.rem(my_row, cols)
 
     corner, corner_give, *keeps, gives = gather(info, trailing, rows, cols)
     got = net.core(gives).reshape(PANELS, count, NB, NB)
     corner = corner + net.core(corner_give)
-    corner = spread_corner(net, corner.reshape(rows, -1, NB), my_row, mine)
+    corner = spread_corner(net, corner.reshape(rows, -1, NB), my_row, stream)
     solved = chain(corner.reshape(-1, NB, NB))
 
     raws, sources = [], []
+    mixed = []
     for s in range(PANELS):
-        raw = keeps[s] + got[s]
+        kept = keeps[s]
+        if mixed:
+            kept, _ = lax.optimization_barrier((kept, mixed[0]))
+        mixed.append(kept + got[s])
+    for s in range(PANELS):
+        raw = mixed[s]
         for step in range(len(net.row_bits)):
             raw = raw + net.raw_step(raw, step)
         raws.append(raw)

time: 235 us -> 234 us (level)
  the two profiles are of different devices: /device:TPU:21 before, /device:TPU:6 now
where the time goes in v4:
time: 234 us
  starting transfers between devices  91.8 us (39%)
  Pallas kernels  64.9 us (28%)
  waiting for transfers between devices  45.8 us (20%)
  other arithmetic  19.2 us (8%)
  local copies, waits for them, and re-layouts  10.5 us (4%)
    ppermute x26, starting transfers between devices, send(): return lax.ppermute(value, AXES, pairs)  91.8 us
    ppermute x26, waiting for transfers between devices, send(): return lax.ppermute(value, AXES, pairs)  45.8 us
    pallas_call x1, Pallas kernels, chain(): pl.pallas_call(chain_kernel, out_shape=jax.ShapeDtypeStruct(corner.shape,...  14.6 us
    pallas_call x2, Pallas kernels, row_factor(): pl.pallas_call(lambda *refs: row_kernel(s, rows, len(sources), *refs), gr...  13.6 us
    pallas_call x2, Pallas kernels, col_factor(): pl.pallas_call(lambda *refs: col_kernel(first, cols, *refs), grid=(count,...  11.6 us
    pallas_call x1, Pallas kernels, early_update(): pl.pallas_call(early_kernel, grid_spec=pltpu.PrefetchScalarGridSpec(num_s...  11.2 us
    pallas_call x1, Pallas kernels, last_update(): pl.pallas_call(lambda *refs: last_kernel(rows, cols, count, *refs), grid_...  9.37 us
    unnamed x36, local copies, waits for them, and re-layouts  9.16 us
  transfers between devices with their start and end apart: 26, of which 6 were waited for; matrix products, arithmetic and copies ran while one was open for 8% of the time, Pallas kernels for 22%

profile of v4, /device:TPU:6, one launch (start us, length us, event | category | flops | bytes accessed | tf_op | source)
XLA Modules:
  0.0 233.6 jit_solution(5545107456138212396)
XLA Ops:
  0.6 1.3 concatenate.12.refs_0_.info
  1.9 4.6 %shard_map.41 = (f32[6,128,256]{2,1,0:T(8,128)}, f32[6,128,256]{2,1,0:T(8,128)}, f32[4,256,256]{2,1,0:T(8,128)}, f32[4,256,256]{2,1,0:T(8,128)}, f32[4,256,256]{2,1,0:T(8,128)}, /*index=5*/f32[12,256,256]{2,1,0:T(8,128)}) custom-call(s32[7]{0:T(128)} %concatenate.12.refs_0_.info, f32[1024,2048]{1,0:T(8,128)} %current.1), custom_call_target="tpu_custom_call" | custom-call | bytes 16777216 | tf_op jit(solution)/shard_map/pallas_call | solution.py:201
  6.5 0.1 collective-permute-start
  6.6 0.5 collective-permute-start.10
  7.1 6.6 %collective-permute-done.10 = f32[6,128,256]{2,1,0:T(8,128)} collective-permute-done((f32[6,128,256]{2,1,0:T(8,128)}, f32[6,128,256]{2,1,0:T(8,128)}, u32[]{:S(2)}, u32[]{:S(2)}) %collective-permute-start.10) | collective-permute-done | bytes 786464 | tf_op jit(solution)/shard_map/ppermute | solution.py:529
  13.7 1.6 add.79
  15.4 1.0 collective-permute-start.11
  16.5 1.7 copy-done.5
  18.1 1.5 slice_add_fusion.2
  19.7 0.7 copy-done.6
  20.3 1.3 slice_add_fusion
  21.6 0.8 collective-permute-start.8
  22.4 1.0 collective-permute-start.6
  23.4 1.0 bitcast_add_fusion
  24.5 1.6 collective-permute-start.12
  26.1 6.3 %collective-permute-done.12 = f32[2,96,256]{2,1,0:T(8,128)S(1)} collective-permute-done((f32[2,96,256]{2,1,0:T(8,128)S(1)}, f32[2,96,256]{2,1,0:T(8,128)S(1)}, u32[]{:S(2)}, u32[]{:S(2)}) %collective-permute-start.12) | collective-permute-done | bytes 196640 | tf_op jit(solution)/shard_map/ppermute | solution.py:529
  32.4 0.6 collective-permute-start.13
  33.0 5.1 %collective-permute-done.8 = f32[4,256,256]{2,1,0:T(8,128)} collective-permute-done((f32[4,256,256]{2,1,0:T(8,128)S(1)}, f32[4,256,256]{2,1,0:T(8,128)}, u32[]{:S(2)}, u32[]{:S(2)}) %collective-permute-start.8) | collective-permute-done | bytes 1048608 | tf_op jit(solution)/shard_map/ppermute | solution.py:529
  38.1 1.4 add.77
  39.4 1.6 collective-permute-start.9
  41.1 2.6 %collective-permute-start.14 = (f32[2,96,256]{2,1,0:T(8,128)S(1)}, f32[2,96,256]{2,1,0:T(8,128)S(1)}, u32[]{:S(2)}, u32[]{:S(2)}) collective-permute-start(f32[2,96,256]{2,1,0:T(8,128)S(1)} %add.86), channel_id=1, source_target_pairs={{0,2},{1,3},{2,0},{3,1},{4,6},{5,7},{6,4},{7,5},{8,10},{9,11},{10,... | collective-permute-start | bytes 589832 | tf_op jit(solution)/shard_map/ppermute | solution.py:529
  43.7 11.8 %collective-permute-done.6 = f32[4,256,256]{2,1,0:T(8,128)} collective-permute-done((f32[4,256,256]{2,1,0:T(8,128)S(1)}, f32[4,256,256]{2,1,0:T(8,128)}, u32[]{:S(2)}, u32[]{:S(2)}) %collective-permute-start.6) | collective-permute-done | bytes 1048608 | tf_op jit(solution)/shard_map/ppermute | solution.py:529
  55.5 2.3 add.74
  57.9 2.0 collective-permute-start.7
  59.9 0.1 collective-permute-start.15
  60.0 15.0 %collective-permute-done.15 = f32[2,96,256]{2,1,0:T(8,128)S(1)} collective-permute-done((f32[2,96,256]{2,1,0:T(8,128)S(1)}, f32[2,96,256]{2,1,0:T(8,128)S(1)}, u32[]{:S(2)}, u32[]{:S(2)}) %collective-permute-start.15) | collective-permute-done | bytes 196640 | tf_op jit(solution)/shard_map/ppermute | solution.py:529
  75.0 0.0 copy-start.11
  75.1 1.1 collective-permute-start.16
  76.2 0.1 add.78.refs_2_.refs_1_
  76.3 0.0 copy-start.12
  76.4 1.8 collective-permute-start.22
  78.1 1.7 add.75.refs_1_
  79.8 1.6 collective-permute-start.19
  81.5 1.0 collective-permute-done.16
  82.4 1.1 broadcast_select_fusion.5
  83.5 1.0 pad_maximum_fusion.1
  84.5 2.3 collective-permute-start.1
  86.8 1.3 collective-permute-start.23
  88.1 1.3 collective-permute-start.20
  89.4 1.4 broadcast_select_fusion.3
  90.8 1.2 pad_maximum_fusion
  92.0 14.6 %shard_map.42.refs_3_.refs_4_.refs_5_.refs_6_.refs_7_.refs_8_.refs_2_ = f32[6,256,256]{2,1,0:T(8,128)} custom-call(f32[6,256,256]{2,1,0:T(8,128)} %bitcast.18), custom_call_target="tpu_custom_call" | custom-call | tf_op jit(solution)/shard_map/pallas_call | solution.py:120
  106.6 1.8 add.72
  108.4 18.4 %collective-permute-start.2 = (f32[4,256,256]{2,1,0:T(8,128)S(1)}, f32[4,256,256]{2,1,0:T(8,128)S(1)}, u32[]{:S(2)}, u32[]{:S(2)}) collective-permute-start(f32[4,256,256]{2,1,0:T(8,128)S(1)} %add.72), channel_id=1, source_target_pairs={{0,20},{1,9},{2,22},{3,11},{4,12},{5,17},{6,14},{7,19},{8,28},{9,1... | collective-permute-start | bytes 3145736 | tf_op jit(solution)/shard_map/ppermute | solution.py:529
  126.8 9.5 %shard_map.43 = (f32[2,4,256,256]{3,2,1,0:T(8,128)S(1)}, f32[4,256,256]{2,1,0:T(8,128)S(1)}) custom-call(s32[7]{0:T(128)S(1)} %copy-done.3, f32[4,256,256]{2,1,0:T(8,128)S(1)} %add.75.refs_1_, f32[4,256,256]{2,1,0:T(8,128)S(1)} %add.78.refs_2_.refs_1_, f32[6,256,256]{2,1,0:T(8,128)S(1)} %copy-done, f32[6,256,256]{2,1,0:T(8,128)S(1)} %copy-done, ...), custom_call_target="tpu_custom_call" | custom-call | flops 4026531840 | bytes 8388608 | tf_op jit(solution)/shard_map/pallas_call | solution.py:282
  136.3 0.1 collective-permute-start.18
  136.4 1.4 broadcast_select_fusion
  137.7 0.9 collective-permute-start.24
  138.7 0.1 broadcast_select_fusion.1
  138.8 0.7 collective-permute-start.21
  139.5 0.0 collective-permute-done.2
  139.6 0.1 add.73.refs_1_
  139.7 0.7 collective-permute-start.5
  140.4 1.3 collective-permute-start.4
  141.7 2.1 shard_map.47.refs_6_
  143.9 0.7 collective-permute-start.3
  144.7 47.7 %collective-permute-start.25 = (f32[1,4,256,256]{3,2,1,0:T(8,128)S(1)}, f32[1,4,256,256]{3,2,1,0:T(8,128)S(1)}, u32[]{:S(2)}, u32[]{:S(2)}) collective-permute-start(f32[1,4,256,256]{3,2,1,0:T(8,128)S(1)} %shard_map.47.refs_6_), channel_id=1, source_target_pairs={{0,4},{1,5},{2,6},{3,7},{4,0},{5,1},{6,2},{7,3},{8,12},{9,13},{10,... | collective-permute-start | bytes 3145736 | tf_op jit(solution)/shard_map/ppermute | solution.py:529
  192.4 3.4 %shard_map.44 = (f32[1024,768]{1,0:T(8,128)}, bf16[1024,512]{1,0:T(8,128)(2,1)S(1)}) custom-call(s32[7]{0:T(128)S(1)} %copy-done.3, f32[4,256,256]{2,1,0:T(8,128)S(1)} %add.75.refs_1_, f32[4,256,256]{2,1,0:T(8,128)} %collective-permute-done.19.refs_2_, f32[4,256,256]{2,1,0:T(8,128)S(1)} %collective-permute-done.20.refs_3_, ...), custom_call_target="tpu_custom_call" | custom-call | flops 805306368 | bytes 8388608 | tf_op jit(solution)/shard_map/pallas_call | solution.py:356
  195.7 0.0 slice-start.1
  195.8 10.3 %shard_map.45 = (f32[1024,768]{1,0:T(8,128)}, bf16[1024,512]{1,0:T(8,128)(2,1)S(1)}, f32[1024,256]{1,0:T(8,128)S(1)}) custom-call(s32[7]{0:T(128)S(1)} %copy-done.3, f32[4,256,256]{2,1,0:T(8,128)S(1)} %add.78.refs_2_.refs_1_, f32[4,256,256]{2,1,0:T(8,128)} %collective-permute-done.22.refs_2_, ...), custom_call_target="tpu_custom_call", output_to_operand_aliasing={{0}: (9, {})} | custom-call | flops 3221225472 | bytes 8388608 | tf_op jit(solution)/shard_map/pallas_call | solution.py:356
  206.1 11.2 %shard_map.46.refs_5_ = f32[1024,2048]{1,0:T(8,128)S(1)} custom-call(s32[7]{0:T(128)S(1)} %copy-done.3, f32[1024,2048]{1,0:T(8,128)S(1)} %bitcast.17, f32[2,4,256,256]{3,2,1,0:T(8,128)S(1)} %get-tuple-element.27.own, f32[2,4,256,256]{3,2,1,0:T(8,128)S(1)} %collective-permute-done.18.other, bf16[1024,512]{1,0:T(8,128)(2,1)S(1)} %get-tuple-element.28.refs_0_, ...), custom_call_target="tpu_custom_call" | custom-call | flops 6442450944 | bytes 25165824 | tf_op jit(solution)/shard_map/pallas_call | solution.py:425
  217.3 3.4 %copy-done.1 = f32[1024,2048]{1,0:T(8,128)} copy-done((f32[1024,2048]{1,0:T(8,128)}, f32[1024,2048]{1,0:T(8,128)S(1)}, u32[]{:S(2)}) %copy-start.1) | copy-done | bytes 8388632
  220.7 3.4 %copy-done.2 = f32[1024,2048]{1,0:T(8,128)S(1)} copy-done((f32[1024,2048]{1,0:T(8,128)S(1)}, f32[1024,2048]{1,0:T(8,128)}, u32[]{:S(2)}) %copy-start.2) | copy-done | bytes 8388632
  224.0 9.4 %shard_map.48 = (f32[1024,2048]{1,0:T(8,128)}, f32[1024,768]{1,0:T(8,128)}) custom-call(s32[7]{0:T(128)S(1)} %copy-done.3, f32[4,256,256]{2,1,0:T(8,128)S(1)} %add.73.refs_1_, f32[4,256,256]{2,1,0:T(8,128)S(1)} %collective-permute-done.3.refs_2_, f32[4,256,256]{2,1,0:T(8,128)S(1)} %collective-permute-done.4.refs_3_, ...), custom_call_target="tpu_custom_call", output_to_operand_aliasing={{1}: (10, {})} | custom-call | flops 3221225472 | bytes 25165824 | tf_op jit(solution)/shard_map/pallas_call | solution.py:491
  (57 shorter events, 0.3 us)
Async XLA Ops:
  6.5 9.9 %collective-permute-start = (f32[12,256,256]{2,1,0:T(8,128)}, f32[12,256,256]{2,1,0:T(8,128)S(1)}, u32[]{:S(2)}, u32[]{:S(2)}) collective-permute-start(f32[12,256,256]{2,1,0:T(8,128)} %get-tuple-element.21), channel_id=1, source_target_pairs={{0,4},{1,5},{2,6},{3,7},{4,0},{5,1},{6,2},{7,3},{8,12},{9,13},{10,... | collective-permute-start | bytes 9437192 | tf_op jit(solution)/shard_map/ppermute | solution.py:529
  6.6 7.1 %collective-permute-start.10 = (f32[6,128,256]{2,1,0:T(8,128)}, f32[6,128,256]{2,1,0:T(8,128)}, u32[]{:S(2)}, u32[]{:S(2)}) collective-permute-start(f32[6,128,256]{2,1,0:T(8,128)} %get-tuple-element.26), channel_id=1, source_target_pairs={{0,4},{1,5},{2,6},{3,7},{4,0},{5,1},{6,2},{7,3},{8,12},{9,13},{10,... | collective-permute-start | bytes 2359304 | tf_op jit(solution)/shard_map/ppermute | solution.py:529
  7.1 11.0 %copy-start.13 = (f32[4,256,256]{2,1,0:T(8,128)S(1)}, f32[4,256,256]{2,1,0:T(8,128)}, u32[]{:S(2)}) copy-start(f32[4,256,256]{2,1,0:T(8,128)} %get-tuple-element.20) | copy-start | bytes 3145732
  13.7 5.9 %copy-start.14 = (f32[4,256,256]{2,1,0:T(8,128)S(1)}, f32[4,256,256]{2,1,0:T(8,128)}, u32[]{:S(2)}) copy-start(f32[4,256,256]{2,1,0:T(8,128)} %get-tuple-element.24) | copy-start | bytes 3145732
  13.7 5.9 %copy-start.15 = (f32[4,256,256]{2,1,0:T(8,128)S(1)}, f32[4,256,256]{2,1,0:T(8,128)}, u32[]{:S(2)}) copy-start(f32[4,256,256]{2,1,0:T(8,128)} %get-tuple-element.22) | copy-start | bytes 3145732
  15.3 1.1 copy-start.7
  15.4 8.0 %collective-permute-start.11 = (f32[4,96,256]{2,1,0:T(8,128)S(1)}, f32[4,96,256]{2,1,0:T(8,128)}, u32[]{:S(2)}, u32[]{:S(2)}) collective-permute-start(f32[4,96,256]{2,1,0:T(8,128)S(1)} %dynamic-slice_bitcast_fusion), channel_id=1, source_target_pairs={{0,8},{1,21},{2,10},{3,23},{4,16},{5,13},{6,18},{7,15},{8,0},{9,29... | collective-permute-start | bytes 1179656 | tf_op jit(solution)/shard_map/ppermute | solution.py:529
  16.4 1.7 copy-start.5
  18.1 2.2 copy-start.6
  20.3 3.1 %copy-start.8 = (f32[6,128,256]{2,1,0:T(8,128)S(1)}, f32[6,128,256]{2,1,0:T(8,128)}, u32[]{:S(2)}) copy-start(f32[6,128,256]{2,1,0:T(8,128)} %copy-done.7) | copy-start | bytes 2359300
  21.6 16.4 %collective-permute-start.8 = (f32[4,256,256]{2,1,0:T(8,128)S(1)}, f32[4,256,256]{2,1,0:T(8,128)}, u32[]{:S(2)}, u32[]{:S(2)}) collective-permute-start(f32[4,256,256]{2,1,0:T(8,128)S(1)} %get-tuple-element.36), channel_id=1, source_target_pairs={{0,8},{1,21},{2,10},{3,23},{4,16},{5,13},{6,18},{7,15},{8,0},{9,29... | collective-permute-start | bytes 3145736 | tf_op jit(solution)/shard_map/ppermute | solution.py:529
  22.4 33.1 %collective-permute-start.6 = (f32[4,256,256]{2,1,0:T(8,128)S(1)}, f32[4,256,256]{2,1,0:T(8,128)}, u32[]{:S(2)}, u32[]{:S(2)}) collective-permute-start(f32[4,256,256]{2,1,0:T(8,128)S(1)} %slice_add_fusion.2), channel_id=1, source_target_pairs={{0,8},{1,21},{2,10},{3,23},{4,16},{5,13},{6,18},{7,15},{8,0},{9,29... | collective-permute-start | bytes 3145736 | tf_op jit(solution)/shard_map/ppermute | solution.py:529
  24.5 7.8 %collective-permute-start.12 = (f32[2,96,256]{2,1,0:T(8,128)S(1)}, f32[2,96,256]{2,1,0:T(8,128)S(1)}, u32[]{:S(2)}, u32[]{:S(2)}) collective-permute-start(f32[2,96,256]{2,1,0:T(8,128)S(1)} %dynamic-slice_bitcast_fusion.1), channel_id=1, source_target_pairs={{0,20},{1,9},{2,22},{3,11},{4,12},{5,17},{6,14},{7,19},{8,28},{9,1... | collective-permute-start | bytes 589832 | tf_op jit(solution)/shard_map/ppermute | solution.py:529
  32.4 8.7 %collective-permute-start.13 = (f32[2,96,256]{2,1,0:T(8,128)S(1)}, f32[2,96,256]{2,1,0:T(8,128)S(1)}, u32[]{:S(2)}, u32[]{:S(2)}) collective-permute-start(f32[2,96,256]{2,1,0:T(8,128)S(1)} %bitcast_add_fusion.1), channel_id=1, source_target_pairs={{0,5},{1,4},{2,7},{3,6},{4,1},{5,0},{6,3},{7,2},{8,13},{9,12},{10,... | collective-permute-start | bytes 589832 | tf_op jit(solution)/shard_map/ppermute | solution.py:529
  39.4 36.7 %collective-permute-start.9 = (f32[4,256,256]{2,1,0:T(8,128)S(1)}, f32[4,256,256]{2,1,0:T(8,128)S(1)}, u32[]{:S(2)}, u32[]{:S(2)}) collective-permute-start(f32[4,256,256]{2,1,0:T(8,128)S(1)} %add.77), channel_id=1, source_target_pairs={{0,20},{1,9},{2,22},{3,11},{4,12},{5,17},{6,14},{7,19},{8,28},{9,1... | collective-permute-start | bytes 3145736 | tf_op jit(solution)/shard_map/ppermute | solution.py:529
  41.1 18.8 %collective-permute-start.14 = (f32[2,96,256]{2,1,0:T(8,128)S(1)}, f32[2,96,256]{2,1,0:T(8,128)S(1)}, u32[]{:S(2)}, u32[]{:S(2)}) collective-permute-start(f32[2,96,256]{2,1,0:T(8,128)S(1)} %add.86), channel_id=1, source_target_pairs={{0,2},{1,3},{2,0},{3,1},{4,6},{5,7},{6,4},{7,5},{8,10},{9,11},{10,... | collective-permute-start | bytes 589832 | tf_op jit(solution)/shard_map/ppermute | solution.py:529
  57.9 20.3 %collective-permute-start.7 = (f32[4,256,256]{2,1,0:T(8,128)}, f32[4,256,256]{2,1,0:T(8,128)}, u32[]{:S(2)}, u32[]{:S(2)}) collective-permute-start(f32[4,256,256]{2,1,0:T(8,128)} %add.74), channel_id=1, source_target_pairs={{0,20},{1,9},{2,22},{3,11},{4,12},{5,17},{6,14},{7,19},{8,28},{9,1... | collective-permute-start | bytes 3145736 | tf_op jit(solution)/shard_map/ppermute | solution.py:529
  59.9 15.1 %collective-permute-start.15 = (f32[2,96,256]{2,1,0:T(8,128)S(1)}, f32[2,96,256]{2,1,0:T(8,128)S(1)}, u32[]{:S(2)}, u32[]{:S(2)}) collective-permute-start(f32[2,96,256]{2,1,0:T(8,128)S(1)} %add.87), channel_id=1, source_target_pairs={{0,20},{1,9},{2,22},{3,11},{4,12},{5,17},{6,14},{7,19},{8,28},{9,1... | collective-permute-start | bytes 589832 | tf_op jit(solution)/shard_map/ppermute | solution.py:529
  75.0 1.2 copy-start.9
  75.0 1.2 copy-start.11
  75.1 7.4 %collective-permute-start.16 = (f32[4,96,256]{2,1,0:T(8,128)S(1)}, f32[4,96,256]{2,1,0:T(8,128)}, u32[]{:S(2)}, u32[]{:S(2)}) collective-permute-start(f32[4,96,256]{2,1,0:T(8,128)S(1)} %pad_maximum_fusion.2), channel_id=1, source_target_pairs={{0,8},{1,21},{2,10},{3,23},{4,16},{5,13},{6,18},{7,15},{8,0},{9,29... | collective-permute-start | bytes 1179656 | tf_op jit(solution)/shard_map/ppermute | solution.py:529
  76.3 6.1 %copy-start.10 = (f32[2,96,256]{2,1,0:T(8,128)S(1)}, f32[2,96,256]{2,1,0:T(8,128)}, u32[]{:S(2)}) copy-start(f32[2,96,256]{2,1,0:T(8,128)} %copy-done.9) | copy-start | bytes 589828
  76.3 6.1 %copy-start.12 = (f32[2,96,256]{2,1,0:T(8,128)S(1)}, f32[2,96,256]{2,1,0:T(8,128)}, u32[]{:S(2)}) copy-start(f32[2,96,256]{2,1,0:T(8,128)} %copy-done.11) | copy-start | bytes 589828
  76.4 10.4 %collective-permute-start.22 = (f32[4,256,256]{2,1,0:T(8,128)S(1)}, f32[4,256,256]{2,1,0:T(8,128)}, u32[]{:S(2)}, u32[]{:S(2)}) collective-permute-start(f32[4,256,256]{2,1,0:T(8,128)S(1)} %add.78.refs_2_.refs_1_), channel_id=1, source_target_pairs={{0,1},{5,6},{10,9},{15,14},{16,17},{21,22},{26,25},{31,30}} | collective-permute-start | bytes 3145736 | tf_op jit(solution)/shard_map/ppermute | solution.py:529
  79.8 8.3 %collective-permute-start.19 = (f32[4,256,256]{2,1,0:T(8,128)S(1)}, f32[4,256,256]{2,1,0:T(8,128)}, u32[]{:S(2)}, u32[]{:S(2)}) collective-permute-start(f32[4,256,256]{2,1,0:T(8,128)S(1)} %add.75.refs_1_), channel_id=1, source_target_pairs={{0,1},{5,6},{10,9},{15,14},{16,17},{21,22},{26,25},{31,30}} | collective-permute-start | bytes 3145736 | tf_op jit(solution)/shard_map/ppermute | solution.py:529
  83.5 4.6 %copy-start.4 = (f32[4,96,256]{2,1,0:T(8,128)}, f32[4,96,256]{2,1,0:T(8,128)S(1)}, u32[]{:S(2)}) copy-start(f32[4,96,256]{2,1,0:T(8,128)S(1)} %get-tuple-element.41) | copy-start | bytes 1179652
  84.5 4.9 %collective-permute-start.17 = (f32[8,96,256]{2,1,0:T(8,128)}, f32[8,96,256]{2,1,0:T(8,128)}, u32[]{:S(2)}, u32[]{:S(2)}) collective-permute-start(f32[8,96,256]{2,1,0:T(8,128)} %pad_maximum_fusion.1), channel_id=1, source_target_pairs={{0,4},{1,5},{2,6},{3,7},{4,0},{5,1},{6,2},{7,3},{8,12},{9,13},{10,... | collective-permute-start | bytes 2359304 | tf_op jit(solution)/shard_map/ppermute | solution.py:529
  84.5 22.1 %collective-permute-start.1 = (f32[4,256,256]{2,1,0:T(8,128)}, f32[4,256,256]{2,1,0:T(8,128)}, u32[]{:S(2)}, u32[]{:S(2)}) collective-permute-start(f32[4,256,256]{2,1,0:T(8,128)} %get-tuple-element.37), channel_id=1, source_target_pairs={{0,8},{1,21},{2,10},{3,23},{4,16},{5,13},{6,18},{7,15},{8,0},{9,29... | collective-permute-start | bytes 3145736 | tf_op jit(solution)/shard_map/ppermute | solution.py:529
  86.8 49.6 %collective-permute-start.23 = (f32[4,256,256]{2,1,0:T(8,128)}, f32[4,256,256]{2,1,0:T(8,128)}, u32[]{:S(2)}, u32[]{:S(2)}) collective-permute-start(f32[4,256,256]{2,1,0:T(8,128)} %collective-permute-done.22.refs_2_), channel_id=1, source_target_pairs={{1,2},{6,7},{9,8},{14,13},{17,18},{22,23},{25,24},{30,29}} | collective-permute-start | bytes 3145736 | tf_op jit(solution)/shard_map/ppermute | solution.py:529
  88.1 50.6 %collective-permute-start.20 = (f32[4,256,256]{2,1,0:T(8,128)}, f32[4,256,256]{2,1,0:T(8,128)S(1)}, u32[]{:S(2)}, u32[]{:S(2)}) collective-permute-start(f32[4,256,256]{2,1,0:T(8,128)} %collective-permute-done.19.refs_2_), channel_id=1, source_target_pairs={{1,2},{6,7},{9,8},{14,13},{17,18},{22,23},{25,24},{30,29}} | collective-permute-start | bytes 3145736 | tf_op jit(solution)/shard_map/ppermute | solution.py:529
  92.0 34.8 %copy-start.3 = (s32[7]{0:T(128)S(1)}, s32[7]{0:T(128)}, u32[]{:S(2)}) copy-start(s32[7]{0:T(128)} %concatenate.12.refs_0_.info) | copy-start | bytes 88
  106.6 20.2 %copy-start = (f32[6,256,256]{2,1,0:T(8,128)S(1)}, f32[6,256,256]{2,1,0:T(8,128)}, u32[]{:S(2)}) copy-start(f32[6,256,256]{2,1,0:T(8,128)} %shard_map.42.refs_3_.refs_4_.refs_5_.refs_6_.refs_7_.refs_8_.refs_2_) | copy-start | bytes 4718596
  108.4 31.2 %collective-permute-start.2 = (f32[4,256,256]{2,1,0:T(8,128)S(1)}, f32[4,256,256]{2,1,0:T(8,128)S(1)}, u32[]{:S(2)}, u32[]{:S(2)}) collective-permute-start(f32[4,256,256]{2,1,0:T(8,128)S(1)} %add.72), channel_id=1, source_target_pairs={{0,20},{1,9},{2,22},{3,11},{4,12},{5,17},{6,14},{7,19},{8,28},{9,1... | collective-permute-start | bytes 3145736 | tf_op jit(solution)/shard_map/ppermute | solution.py:529
  136.3 69.7 %collective-permute-start.18 = (f32[2,4,256,256]{3,2,1,0:T(8,128)S(1)}, f32[2,4,256,256]{3,2,1,0:T(8,128)S(1)}, u32[]{:S(2)}, u32[]{:S(2)}) collective-permute-start(f32[2,4,256,256]{3,2,1,0:T(8,128)S(1)} %get-tuple-element.27.own), channel_id=1, source_target_pairs={{0,4},{1,5},{2,6},{3,7},{4,0},{5,1},{6,2},{7,3},{8,12},{9,13},{10,... | collective-permute-start | bytes 6291464 | tf_op jit(solution)/shard_map/ppermute | solution.py:529
  137.7 6.2 %collective-permute-start.24 = (f32[4,256,256]{2,1,0:T(8,128)S(1)}, f32[4,256,256]{2,1,0:T(8,128)S(1)}, u32[]{:S(2)}, u32[]{:S(2)}) collective-permute-start(f32[4,256,256]{2,1,0:T(8,128)S(1)} %broadcast_select_fusion), channel_id=1, source_target_pairs={{2,3},{5,4},{10,11},{13,12},{18,19},{21,20},{26,27},{29,28}} | collective-permute-start | bytes 3145736 | tf_op jit(solution)/shard_map/ppermute | solution.py:529
  138.8 5.8 %collective-permute-start.21 = (f32[4,256,256]{2,1,0:T(8,128)S(1)}, f32[4,256,256]{2,1,0:T(8,128)S(1)}, u32[]{:S(2)}, u32[]{:S(2)}) collective-permute-start(f32[4,256,256]{2,1,0:T(8,128)S(1)} %broadcast_select_fusion.1), channel_id=1, source_target_pairs={{2,3},{5,4},{10,11},{13,12},{18,19},{21,20},{26,27},{29,28}} | collective-permute-start | bytes 3145736 | tf_op jit(solution)/shard_map/ppermute | solution.py:529
  139.7 80.9 %collective-permute-start.5 = (f32[4,256,256]{2,1,0:T(8,128)S(1)}, f32[4,256,256]{2,1,0:T(8,128)S(1)}, u32[]{:S(2)}, u32[]{:S(2)}) collective-permute-start(f32[4,256,256]{2,1,0:T(8,128)S(1)} %add.73.refs_1_), channel_id=1, source_target_pairs={{0,3},{5,4},{10,11},{15,12},{16,19},{21,20},{26,27},{31,28}} | collective-permute-start | bytes 3145736 | tf_op jit(solution)/shard_map/ppermute | solution.py:529
  140.4 80.2 %collective-permute-start.4 = (f32[4,256,256]{2,1,0:T(8,128)S(1)}, f32[4,256,256]{2,1,0:T(8,128)S(1)}, u32[]{:S(2)}, u32[]{:S(2)}) collective-permute-start(f32[4,256,256]{2,1,0:T(8,128)S(1)} %add.73.refs_1_), channel_id=1, source_target_pairs={{0,2},{5,7},{10,8},{15,13},{16,18},{21,23},{26,24},{31,29}} | collective-permute-start | bytes 3145736 | tf_op jit(solution)/shard_map/ppermute | solution.py:529
  143.9 76.7 %collective-permute-start.3 = (f32[4,256,256]{2,1,0:T(8,128)S(1)}, f32[4,256,256]{2,1,0:T(8,128)S(1)}, u32[]{:S(2)}, u32[]{:S(2)}) collective-permute-start(f32[4,256,256]{2,1,0:T(8,128)S(1)} %add.73.refs_1_), channel_id=1, source_target_pairs={{0,1},{5,6},{10,9},{15,14},{16,17},{21,22},{26,25},{31,30}} | collective-permute-start | bytes 3145736 | tf_op jit(solution)/shard_map/ppermute | solution.py:529
  144.7 76.0 %collective-permute-start.25 = (f32[1,4,256,256]{3,2,1,0:T(8,128)S(1)}, f32[1,4,256,256]{3,2,1,0:T(8,128)S(1)}, u32[]{:S(2)}, u32[]{:S(2)}) collective-permute-start(f32[1,4,256,256]{3,2,1,0:T(8,128)S(1)} %shard_map.47.refs_6_), channel_id=1, source_target_pairs={{0,4},{1,5},{2,6},{3,7},{4,0},{5,1},{6,2},{7,3},{8,12},{9,13},{10,... | collective-permute-start | bytes 3145736 | tf_op jit(solution)/shard_map/ppermute | solution.py:529
  192.4 13.7 %slice-start = ((s8[8388608]{0:T(1024)(128)(4,1)}), s8[4194304]{0:T(1024)(128)(4,1)S(1)}, s32[]{:S(2)}) async-start(s8[8388608]{0:T(1024)(128)(4,1)} %bitcast.16), calls=%async_computation | async-start | bytes 8388608
  195.7 10.3 %slice-start.1 = ((s8[8388608]{0:T(1024)(128)(4,1)}), s8[4194304]{0:T(1024)(128)(4,1)S(1)}, s32[]{:S(2)}) async-start(s8[8388608]{0:T(1024)(128)(4,1)} %bitcast.16), calls=%async_computation.1 | async-start | bytes 8388608
  217.2 3.4 %copy-start.1 = (f32[1024,2048]{1,0:T(8,128)}, f32[1024,2048]{1,0:T(8,128)S(1)}, u32[]{:S(2)}) copy-start(f32[1024,2048]{1,0:T(8,128)S(1)} %shard_map.46.refs_5_) | copy-start | bytes 25165828
  220.7 3.4 %copy-start.2 = (f32[1024,2048]{1,0:T(8,128)S(1)}, f32[1024,2048]{1,0:T(8,128)}, u32[]{:S(2)}) copy-start(f32[1024,2048]{1,0:T(8,128)} %copy-done.1) | copy-start | bytes 25165828

commit v5 on v4

--- a/solution.py
+++ b/solution.py
@@ -10,7 +10,7 @@
 PANELS = 3
 AXES = ("row", "col")
 INTERPRET = False
-VMEM_LIMIT = 24 << 20
+VMEM_LIMIT = 14 << 20
 
 
 def thirds(x):
@@ -494,8 +494,8 @@
             num_scalar_prefetch=1,
             grid=(width // NB,),
             in_specs=[spec(pltpu.HBM)] * count
-            + [strip, mine, theirs, w, spec(), spec(pl.ANY)],
-            out_specs=[strip, spec(pl.ANY)],
+            + [strip, mine, theirs, w, spec(), spec(pltpu.HBM)],
+            out_specs=[strip, spec(pltpu.HBM)],
             scratch_shapes=[
                 pltpu.VMEM(sources[0].shape, jnp.float32),
                 pltpu.VMEM((height, NB), jnp.float32),
@@ -584,7 +584,7 @@
     return jnp.concatenate([jnp.where(low, part, other), jnp.where(low, other, part)])
 
 
-def spread_rows(net, source, is_source, direct):
+def spread_rows(net, source, is_source, near):
     if (net.rows, net.cols) != (8, 4):
         value = jnp.where(is_source, source, 0.0)
         for bit in net.col_bits:
@@ -604,23 +604,20 @@
         return target
 
     got1 = net.send(source, hop({0: 1}, {1: 2}))
-    if direct:
-        got2 = net.send(source, hop({0: 2}, {1: 3}))
-        got3 = net.send(source, hop({0: 3}, {1: 0}))
-        return [source, got1, got2, got3]
-    got2 = net.send(got1, hop({1: 2}, {2: 3}))
-    third = jnp.where(is_source, source, got2)
-    got3 = net.send(third, hop({2: 3}, {1: 0}))
+    got2 = net.send(source, hop({0: 2}, {1: 0}))
+    third = jnp.where(near, got2, got1)
+    got3 = net.send(third, hop({2: 3}, {2: 3}))
     return [source, got1, got2, got3]
 
 
 def source_code(net, my_row, my_col):
     if (net.rows, net.cols) != (8, 4):
-        return jnp.int32(0)
+        return jnp.int32(0), True
     up = (my_row & 2) == 0
     line = jnp.where(up, my_col, 3 - my_col)
     near = ((my_row & 1) == 0) == up
-    return jnp.where(near, line, (line + 3) & 3)
+    far = jnp.where(line == 3, 3, jnp.where(line == 0, 2, line - 1))
+    return jnp.where(near, line, far), near
 
 
 def run(panel, trailing):
@@ -634,7 +631,7 @@
     ratio = rows // cols
     group = lax.div(my_row, cols)
     stream = (my_row + my_col + group) & 1
-    code = source_code(net, my_row, my_col)
+    code, near = source_code(net, my_row, my_col)
     extra = jnp.stack([my_row, my_col, code, stream])
     info = jnp.concatenate([panel[:PANELS], extra])
     is_source = my_col == lax.rem(my_row, cols)
@@ -655,7 +652,8 @@
     for s in range(PANELS):
         raw = mixed[s]
         for step in range(len(net.row_bits)):
-            raw = raw + net.raw_step(raw, step)
+            moved = net.raw_step(raw, step)
+            raw = raw + moved
         raws.append(raw)
         own = raw
         if ratio != 2:
@@ -664,7 +662,7 @@
             odd = jnp.where(stream == 0, other, raw)
             own = jnp.stack([even, odd], axis=1).reshape(-1, ratio, NB, NB)
             own = lax.dynamic_index_in_dim(own, group, 1, keepdims=False)
-        sources.append(spread_rows(net, own, is_source, s == PANELS - 1))
+        sources.append(spread_rows(net, own, is_source, near))
     last = PANELS - 1
     early, col_rest = col_factor(0, cols, info, raws[:last], solved, [])
     early_other = net.core(early)

time: 234 us -> 238 us (1.017)
  the two profiles are of different devices: /device:TPU:6 before, /device:TPU:3 now
where the time goes in v5:
time: 238 us; the launch traced here: 237 us
  waiting for transfers between devices  114 us (48%)
  Pallas kernels  65 us (27%)
  starting transfers between devices  28.9 us (12%)
  other arithmetic  21.1 us (9%)
  local copies, waits for them, and re-layouts  7.1 us (3%)
    ppermute x26, waiting for transfers between devices, send(): return lax.ppermute(value, AXES, pairs)  114 us
    ppermute x26, starting transfers between devices, send(): return lax.ppermute(value, AXES, pairs)  28.9 us
    pallas_call x1, Pallas kernels, chain(): pl.pallas_call(chain_kernel, out_shape=jax.ShapeDtypeStruct(corner.shape,...  14.5 us
    pallas_call x2, Pallas kernels, row_factor(): pl.pallas_call(lambda *refs: row_kernel(s, rows, len(sources), *refs), gr...  12.2 us
    pallas_call x2, Pallas kernels, col_factor(): pl.pallas_call(lambda *refs: col_kernel(first, cols, *refs), grid=(count,...  12 us
    pallas_call x1, Pallas kernels, early_update(): pl.pallas_call(early_kernel, grid_spec=pltpu.PrefetchScalarGridSpec(num_s...  11.2 us
    pallas_call x1, Pallas kernels, last_update(): pl.pallas_call(lambda *refs: last_kernel(rows, cols, count, *refs), grid_...  9.37 us
    add x6, other arithmetic, run(): raw = raw + moved  8.01 us
  transfers between devices with their start and end apart: 26, of which 13 were waited for; matrix products, arithmetic and copies ran while one was open for 9% of the time, Pallas kernels for 21%

profile of v5, /device:TPU:3, one launch (start us, length us, event | category | flops | bytes accessed | tf_op | source)
XLA Modules:
  0.0 237.2 jit_solution(17207424656326457206)
XLA Ops:
  0.7 1.3 concatenate.12.refs_0_.info
  1.9 5.6 %shard_map.41 = (f32[6,128,256]{2,1,0:T(8,128)}, f32[6,128,256]{2,1,0:T(8,128)}, f32[4,256,256]{2,1,0:T(8,128)}, f32[4,256,256]{2,1,0:T(8,128)}, f32[4,256,256]{2,1,0:T(8,128)}, /*index=5*/f32[12,256,256]{2,1,0:T(8,128)}) custom-call(s32[7]{0:T(128)} %concatenate.12.refs_0_.info, f32[1024,2048]{1,0:T(8,128)} %current.1), custom_call_target="tpu_custom_call" | custom-call | bytes 16777216 | tf_op jit(solution)/shard_map/pallas_call | solution.py:201
  7.7 0.5 collective-permute-start.10
  8.1 6.6 %collective-permute-done.10 = f32[6,128,256]{2,1,0:T(8,128)} collective-permute-done((f32[6,128,256]{2,1,0:T(8,128)}, f32[6,128,256]{2,1,0:T(8,128)}, u32[]{:S(2)}, u32[]{:S(2)}) %collective-permute-start.10) | collective-permute-done | bytes 786464 | tf_op jit(solution)/shard_map/ppermute | solution.py:529
  14.8 1.5 add.76
  16.3 0.9 copy-done.5
  17.2 0.8 collective-permute-start.11
  18.0 6.8 %collective-permute-done.11 = f32[4,96,256]{2,1,0:T(8,128)} collective-permute-done((f32[4,96,256]{2,1,0:T(8,128)S(1)}, f32[4,96,256]{2,1,0:T(8,128)}, u32[]{:S(2)}, u32[]{:S(2)}) %collective-permute-start.11) | collective-permute-done | bytes 393248 | tf_op jit(solution)/shard_map/ppermute | solution.py:529
  24.8 1.2 bitcast_add_fusion
  26.0 0.7 dynamic-slice_bitcast_fusion.1
  26.9 4.9 %collective-permute-done.12 = f32[2,96,256]{2,1,0:T(8,128)} collective-permute-done((f32[2,96,256]{2,1,0:T(8,128)}, f32[2,96,256]{2,1,0:T(8,128)}, u32[]{:S(2)}, u32[]{:S(2)}) %collective-permute-start.12) | collective-permute-done | bytes 196640 | tf_op jit(solution)/shard_map/ppermute | solution.py:529
  31.8 1.0 bitcast_add_fusion.1
  32.8 2.0 collective-permute-start.13
  34.7 5.5 %collective-permute-done.13 = f32[2,96,256]{2,1,0:T(8,128)S(1)} collective-permute-done((f32[2,96,256]{2,1,0:T(8,128)S(1)}, f32[2,96,256]{2,1,0:T(8,128)S(1)}, u32[]{:S(2)}, u32[]{:S(2)}) %collective-permute-start.13) | collective-permute-done | bytes 196640 | tf_op jit(solution)/shard_map/ppermute | solution.py:529
  40.2 2.4 collective-permute-start.14
  42.6 1.7 copy-done.3
  44.3 1.8 slice_add_fusion.2
  46.1 0.7 copy-done.4
  46.8 1.6 slice_add_fusion
  48.4 1.4 collective-permute-start.8
  49.8 0.4 collective-permute-start.6
  50.2 1.3 collective-permute-done.14
  51.7 0.4 copy-done.7
  52.2 6.4 %collective-permute-done.15 = f32[2,96,256]{2,1,0:T(8,128)} collective-permute-done((f32[2,96,256]{2,1,0:T(8,128)S(1)}, f32[2,96,256]{2,1,0:T(8,128)}, u32[]{:S(2)}, u32[]{:S(2)}) %collective-permute-start.15) | collective-permute-done | bytes 196640 | tf_op jit(solution)/shard_map/ppermute | solution.py:529
  58.6 1.1 broadcast_select_fusion.8
  59.7 0.8 pad_maximum_fusion.2
  60.4 2.7 %collective-permute-start.16 = (f32[4,96,256]{2,1,0:T(8,128)}, f32[4,96,256]{2,1,0:T(8,128)}, u32[]{:S(2)}, u32[]{:S(2)}) collective-permute-start(f32[4,96,256]{2,1,0:T(8,128)} %pad_maximum_fusion.2), channel_id=1, source_target_pairs={{0,8},{1,21},{2,10},{3,23},{4,16},{5,13},{6,18},{7,15},{8,0},{9,29... | collective-permute-start | bytes 1179656 | tf_op jit(solution)/shard_map/ppermute | solution.py:529
  63.2 2.0 collective-permute-done.8
  65.2 1.4 add.74
  66.5 1.1 collective-permute-start.9
  67.6 15.0 %collective-permute-done.6 = f32[4,256,256]{2,1,0:T(8,128)} collective-permute-done((f32[4,256,256]{2,1,0:T(8,128)S(1)}, f32[4,256,256]{2,1,0:T(8,128)}, u32[]{:S(2)}, u32[]{:S(2)}) %collective-permute-start.6) | collective-permute-done | bytes 1048608 | tf_op jit(solution)/shard_map/ppermute | solution.py:529
  82.6 1.4 add.71
  83.9 1.9 collective-permute-start.7
  85.9 5.1 %collective-permute-done.16 = f32[4,96,256]{2,1,0:T(8,128)} collective-permute-done((f32[4,96,256]{2,1,0:T(8,128)}, f32[4,96,256]{2,1,0:T(8,128)}, u32[]{:S(2)}, u32[]{:S(2)}) %collective-permute-start.16) | collective-permute-done | bytes 393248 | tf_op jit(solution)/shard_map/ppermute | solution.py:529
  91.0 1.1 broadcast_select_fusion.6
  92.1 2.4 %collective-permute-start.17 = (f32[8,96,256]{2,1,0:T(8,128)S(1)}, f32[8,96,256]{2,1,0:T(8,128)S(1)}, u32[]{:S(2)}, u32[]{:S(2)}) collective-permute-start(f32[8,96,256]{2,1,0:T(8,128)S(1)} %pad_maximum_fusion.1), channel_id=1, source_target_pairs={{0,4},{1,5},{2,6},{3,7},{4,0},{5,1},{6,2},{7,3},{8,12},{9,13},{10,... | collective-permute-start | bytes 2359304 | tf_op jit(solution)/shard_map/ppermute | solution.py:529
  94.5 18.9 %collective-permute-done.1 = f32[4,256,256]{2,1,0:T(8,128)} collective-permute-done((f32[4,256,256]{2,1,0:T(8,128)S(1)}, f32[4,256,256]{2,1,0:T(8,128)}, u32[]{:S(2)}, u32[]{:S(2)}) %collective-permute-start.1) | collective-permute-done | bytes 1048608 | tf_op jit(solution)/shard_map/ppermute | solution.py:529
  113.5 2.4 add.69
  115.8 1.8 collective-permute-start.2
  117.7 0.7 collective-permute-start.20
  118.5 0.7 collective-permute-start.19
  119.2 1.1 add.75.refs_2_.refs_1_
  120.3 1.7 collective-permute-start.23
  122.0 1.6 collective-permute-start.22
  123.8 1.3 pad_maximum_fusion
  125.1 14.5 %shard_map.42.refs_3_.refs_4_.refs_5_.refs_6_.refs_7_.refs_8_.refs_2_ = f32[6,256,256]{2,1,0:T(8,128)} custom-call(f32[6,256,256]{2,1,0:T(8,128)} %bitcast.18), custom_call_target="tpu_custom_call" | custom-call | tf_op jit(solution)/shard_map/pallas_call | solution.py:120
  139.6 1.4 copy-done
  141.1 9.9 %shard_map.43 = (f32[2,4,256,256]{3,2,1,0:T(8,128)S(1)}, f32[4,256,256]{2,1,0:T(8,128)S(1)}) custom-call(s32[7]{0:T(128)S(1)} %copy-done.2, f32[4,256,256]{2,1,0:T(8,128)S(1)} %add.72.refs_1_, f32[4,256,256]{2,1,0:T(8,128)} %add.75.refs_2_.refs_1_, f32[6,256,256]{2,1,0:T(8,128)S(1)} %copy-done, f32[6,256,256]{2,1,0:T(8,128)S(1)} %copy-done, ...), custom_call_target="tpu_custom_call" | custom-call | flops 4026531840 | bytes 8388608 | tf_op jit(solution)/shard_map/pallas_call | solution.py:282
  151.1 1.7 add.70.refs_1_
  152.8 1.0 collective-permute-start.4
  153.9 0.7 collective-permute-start.3
  154.8 1.3 collective-permute-start.21
  156.1 1.4 broadcast_select_fusion
  157.4 1.3 collective-permute-start.24
  158.8 2.1 shard_map.47.refs_6_
  160.9 0.5 collective-permute-start.25
  161.6 1.3 collective-permute-start.5
  162.9 20.9 %collective-permute-done.21.refs_4_ = f32[4,256,256]{2,1,0:T(8,128)S(1)} collective-permute-done((f32[4,256,256]{2,1,0:T(8,128)S(1)}, f32[4,256,256]{2,1,0:T(8,128)S(1)}, u32[]{:S(2)}, u32[]{:S(2)}) %collective-permute-start.21) | collective-permute-done | bytes 1048608 | tf_op jit(solution)/shard_map/ppermute | solution.py:529
  183.8 3.4 %shard_map.44 = (f32[1024,768]{1,0:T(8,128)}, bf16[1024,512]{1,0:T(8,128)(2,1)S(1)}) custom-call(s32[7]{0:T(128)S(1)} %copy-done.2, f32[4,256,256]{2,1,0:T(8,128)S(1)} %add.72.refs_1_, f32[4,256,256]{2,1,0:T(8,128)S(1)} %collective-permute-done.19.refs_2_, f32[4,256,256]{2,1,0:T(8,128)S(1)} %collective-permute-done.20.refs_3_, ...), custom_call_target="tpu_custom_call" | custom-call | flops 805306368 | bytes 8388608 | tf_op jit(solution)/shard_map/pallas_call | solution.py:356
  187.2 19.1 %collective-permute-done.24.refs_4_ = f32[4,256,256]{2,1,0:T(8,128)S(1)} collective-permute-done((f32[4,256,256]{2,1,0:T(8,128)S(1)}, f32[4,256,256]{2,1,0:T(8,128)S(1)}, u32[]{:S(2)}, u32[]{:S(2)}) %collective-permute-start.24) | collective-permute-done | bytes 1048608 | tf_op jit(solution)/shard_map/ppermute | solution.py:529
  206.3 8.8 %shard_map.45 = (f32[1024,768]{1,0:T(8,128)}, bf16[1024,512]{1,0:T(8,128)(2,1)S(1)}, f32[1024,256]{1,0:T(8,128)S(1)}) custom-call(s32[7]{0:T(128)S(1)} %copy-done.2, f32[4,256,256]{2,1,0:T(8,128)} %add.75.refs_2_.refs_1_, f32[4,256,256]{2,1,0:T(8,128)} %collective-permute-done.22.refs_2_, ...), custom_call_target="tpu_custom_call", output_to_operand_aliasing={{0}: (9, {})} | custom-call | flops 3221225472 | bytes 8388608 | tf_op jit(solution)/shard_map/pallas_call | solution.py:356
  215.1 11.2 %shard_map.46.refs_5_ = f32[1024,2048]{1,0:T(8,128)S(1)} custom-call(s32[7]{0:T(128)S(1)} %copy-done.2, f32[1024,2048]{1,0:T(8,128)S(1)} %bitcast.17, f32[2,4,256,256]{3,2,1,0:T(8,128)S(1)} %get-tuple-element.27.own, f32[2,4,256,256]{3,2,1,0:T(8,128)S(1)} %collective-permute-done.18.other, bf16[1024,512]{1,0:T(8,128)(2,1)S(1)} %get-tuple-element.28.refs_0_, ...), custom_call_target="tpu_custom_call" | custom-call | flops 6442450944 | bytes 25165824 | tf_op jit(solution)/shard_map/pallas_call | solution.py:425
  226.3 1.4 collective-permute-done.5.refs_4_
  227.7 9.4 %shard_map.48 = (f32[1024,2048]{1,0:T(8,128)}, f32[1024,768]{1,0:T(8,128)}) custom-call(s32[7]{0:T(128)S(1)} %copy-done.2, f32[4,256,256]{2,1,0:T(8,128)S(1)} %add.70.refs_1_, f32[4,256,256]{2,1,0:T(8,128)S(1)} %collective-permute-done.3.refs_2_, f32[4,256,256]{2,1,0:T(8,128)S(1)} %collective-permute-done.4.refs_3_, ...), custom_call_target="tpu_custom_call", output_to_operand_aliasing={{1}: (10, {})} | custom-call | flops 3221225472 | bytes 25165824 | tf_op jit(solution)/shard_map/pallas_call | solution.py:491
  (42 shorter events, 1.4 us)
Async XLA Ops:
  7.6 35.0 %collective-permute-start = (f32[12,256,256]{2,1,0:T(8,128)}, f32[12,256,256]{2,1,0:T(8,128)S(1)}, u32[]{:S(2)}, u32[]{:S(2)}) collective-permute-start(f32[12,256,256]{2,1,0:T(8,128)} %get-tuple-element.21), channel_id=1, source_target_pairs={{0,4},{1,5},{2,6},{3,7},{4,0},{5,1},{6,2},{7,3},{8,12},{9,13},{10,... | collective-permute-start | bytes 9437192 | tf_op jit(solution)/shard_map/ppermute | solution.py:529
  7.7 7.1 %collective-permute-start.10 = (f32[6,128,256]{2,1,0:T(8,128)}, f32[6,128,256]{2,1,0:T(8,128)}, u32[]{:S(2)}, u32[]{:S(2)}) collective-permute-start(f32[6,128,256]{2,1,0:T(8,128)} %get-tuple-element.26), channel_id=1, source_target_pairs={{0,4},{1,5},{2,6},{3,7},{4,0},{5,1},{6,2},{7,3},{8,12},{9,13},{10,... | collective-permute-start | bytes 2359304 | tf_op jit(solution)/shard_map/ppermute | solution.py:529
  16.2 0.9 copy-start.5
  17.2 7.7 %collective-permute-start.11 = (f32[4,96,256]{2,1,0:T(8,128)S(1)}, f32[4,96,256]{2,1,0:T(8,128)}, u32[]{:S(2)}, u32[]{:S(2)}) collective-permute-start(f32[4,96,256]{2,1,0:T(8,128)S(1)} %dynamic-slice_bitcast_fusion), channel_id=1, source_target_pairs={{0,8},{1,21},{2,10},{3,23},{4,16},{5,13},{6,18},{7,15},{8,0},{9,29... | collective-permute-start | bytes 1179656 | tf_op jit(solution)/shard_map/ppermute | solution.py:529
  26.7 5.1 %collective-permute-start.12 = (f32[2,96,256]{2,1,0:T(8,128)}, f32[2,96,256]{2,1,0:T(8,128)}, u32[]{:S(2)}, u32[]{:S(2)}) collective-permute-start(f32[2,96,256]{2,1,0:T(8,128)} %dynamic-slice_bitcast_fusion.1), channel_id=1, source_target_pairs={{0,20},{1,9},{2,22},{3,11},{4,12},{5,17},{6,14},{7,19},{8,28},{9,1... | collective-permute-start | bytes 589832 | tf_op jit(solution)/shard_map/ppermute | solution.py:529
  26.9 19.2 %copy-start.6 = (f32[4,256,256]{2,1,0:T(8,128)S(1)}, f32[4,256,256]{2,1,0:T(8,128)}, u32[]{:S(2)}) copy-start(f32[4,256,256]{2,1,0:T(8,128)} %get-tuple-element.24) | copy-start | bytes 3145732
  32.8 7.4 %collective-permute-start.13 = (f32[2,96,256]{2,1,0:T(8,128)S(1)}, f32[2,96,256]{2,1,0:T(8,128)S(1)}, u32[]{:S(2)}, u32[]{:S(2)}) collective-permute-start(f32[2,96,256]{2,1,0:T(8,128)S(1)} %bitcast_add_fusion.1), channel_id=1, source_target_pairs={{0,5},{1,4},{2,7},{3,6},{4,1},{5,0},{6,3},{7,2},{8,13},{9,12},{10,... | collective-permute-start | bytes 589832 | tf_op jit(solution)/shard_map/ppermute | solution.py:529
  40.2 11.2 %collective-permute-start.14 = (f32[2,96,256]{2,1,0:T(8,128)S(1)}, f32[2,96,256]{2,1,0:T(8,128)S(1)}, u32[]{:S(2)}, u32[]{:S(2)}) collective-permute-start(f32[2,96,256]{2,1,0:T(8,128)S(1)} %add.83), channel_id=1, source_target_pairs={{0,2},{1,3},{2,0},{3,1},{4,6},{5,7},{6,4},{7,5},{8,10},{9,11},{10,... | collective-permute-start | bytes 589832 | tf_op jit(solution)/shard_map/ppermute | solution.py:529
  42.6 1.7 copy-start.3
  44.3 2.5 %copy-start.4 = (f32[12,256,256]{2,1,0:T(8,128)S(1)}, f32[12,256,256]{2,1,0:T(8,128)}, u32[]{:S(2)}) copy-start(f32[12,256,256]{2,1,0:T(8,128)} %copy-done.3) | copy-start | bytes 9437188
  48.4 16.8 %collective-permute-start.8 = (f32[4,256,256]{2,1,0:T(8,128)S(1)}, f32[4,256,256]{2,1,0:T(8,128)}, u32[]{:S(2)}, u32[]{:S(2)}) collective-permute-start(f32[4,256,256]{2,1,0:T(8,128)S(1)} %get-tuple-element.36), channel_id=1, source_target_pairs={{0,8},{1,21},{2,10},{3,23},{4,16},{5,13},{6,18},{7,15},{8,0},{9,29... | collective-permute-start | bytes 3145736 | tf_op jit(solution)/shard_map/ppermute | solution.py:529
  49.8 32.8 %collective-permute-start.6 = (f32[4,256,256]{2,1,0:T(8,128)S(1)}, f32[4,256,256]{2,1,0:T(8,128)}, u32[]{:S(2)}, u32[]{:S(2)}) collective-permute-start(f32[4,256,256]{2,1,0:T(8,128)S(1)} %slice_add_fusion.2), channel_id=1, source_target_pairs={{0,8},{1,21},{2,10},{3,23},{4,16},{5,13},{6,18},{7,15},{8,0},{9,29... | collective-permute-start | bytes 3145736 | tf_op jit(solution)/shard_map/ppermute | solution.py:529
  51.5 0.7 copy-start.7
  51.5 7.1 %collective-permute-start.15 = (f32[2,96,256]{2,1,0:T(8,128)S(1)}, f32[2,96,256]{2,1,0:T(8,128)}, u32[]{:S(2)}, u32[]{:S(2)}) collective-permute-start(f32[2,96,256]{2,1,0:T(8,128)S(1)} %add.84), channel_id=1, source_target_pairs={{0,20},{1,9},{2,22},{3,11},{4,12},{5,17},{6,14},{7,19},{8,28},{9,1... | collective-permute-start | bytes 589832 | tf_op jit(solution)/shard_map/ppermute | solution.py:529
  60.4 30.6 %collective-permute-start.16 = (f32[4,96,256]{2,1,0:T(8,128)}, f32[4,96,256]{2,1,0:T(8,128)}, u32[]{:S(2)}, u32[]{:S(2)}) collective-permute-start(f32[4,96,256]{2,1,0:T(8,128)} %pad_maximum_fusion.2), channel_id=1, source_target_pairs={{0,8},{1,21},{2,10},{3,23},{4,16},{5,13},{6,18},{7,15},{8,0},{9,29... | collective-permute-start | bytes 1179656 | tf_op jit(solution)/shard_map/ppermute | solution.py:529
  63.2 50.3 %collective-permute-start.1 = (f32[4,256,256]{2,1,0:T(8,128)S(1)}, f32[4,256,256]{2,1,0:T(8,128)}, u32[]{:S(2)}, u32[]{:S(2)}) collective-permute-start(f32[4,256,256]{2,1,0:T(8,128)S(1)} %get-tuple-element.37), channel_id=1, source_target_pairs={{0,8},{1,21},{2,10},{3,23},{4,16},{5,13},{6,18},{7,15},{8,0},{9,29... | collective-permute-start | bytes 3145736 | tf_op jit(solution)/shard_map/ppermute | solution.py:529
  66.5 52.7 %collective-permute-start.9 = (f32[4,256,256]{2,1,0:T(8,128)S(1)}, f32[4,256,256]{2,1,0:T(8,128)S(1)}, u32[]{:S(2)}, u32[]{:S(2)}) collective-permute-start(f32[4,256,256]{2,1,0:T(8,128)S(1)} %add.74), channel_id=1, source_target_pairs={{0,20},{1,9},{2,22},{3,11},{4,12},{5,17},{6,14},{7,19},{8,28},{9,1... | collective-permute-start | bytes 3145736 | tf_op jit(solution)/shard_map/ppermute | solution.py:529
  83.9 33.7 %collective-permute-start.7 = (f32[4,256,256]{2,1,0:T(8,128)S(1)}, f32[4,256,256]{2,1,0:T(8,128)S(1)}, u32[]{:S(2)}, u32[]{:S(2)}) collective-permute-start(f32[4,256,256]{2,1,0:T(8,128)S(1)} %add.71), channel_id=1, source_target_pairs={{0,20},{1,9},{2,22},{3,11},{4,12},{5,17},{6,14},{7,19},{8,28},{9,1... | collective-permute-start | bytes 3145736 | tf_op jit(solution)/shard_map/ppermute | solution.py:529
  92.1 29.9 %collective-permute-start.17 = (f32[8,96,256]{2,1,0:T(8,128)S(1)}, f32[8,96,256]{2,1,0:T(8,128)S(1)}, u32[]{:S(2)}, u32[]{:S(2)}) collective-permute-start(f32[8,96,256]{2,1,0:T(8,128)S(1)} %pad_maximum_fusion.1), channel_id=1, source_target_pairs={{0,4},{1,5},{2,6},{3,7},{4,0},{5,1},{6,2},{7,3},{8,12},{9,13},{10,... | collective-permute-start | bytes 2359304 | tf_op jit(solution)/shard_map/ppermute | solution.py:529
  115.8 35.1 %collective-permute-start.2 = (f32[4,256,256]{2,1,0:T(8,128)}, f32[4,256,256]{2,1,0:T(8,128)}, u32[]{:S(2)}, u32[]{:S(2)}) collective-permute-start(f32[4,256,256]{2,1,0:T(8,128)} %add.69), channel_id=1, source_target_pairs={{0,20},{1,9},{2,22},{3,11},{4,12},{5,17},{6,14},{7,19},{8,28},{9,1... | collective-permute-start | bytes 3145736 | tf_op jit(solution)/shard_map/ppermute | solution.py:529
  117.7 35.1 %collective-permute-start.20 = (f32[4,256,256]{2,1,0:T(8,128)S(1)}, f32[4,256,256]{2,1,0:T(8,128)S(1)}, u32[]{:S(2)}, u32[]{:S(2)}) collective-permute-start(f32[4,256,256]{2,1,0:T(8,128)S(1)} %add.72.refs_1_), channel_id=1, source_target_pairs={{0,2},{5,4},{10,11},{15,13},{16,18},{21,20},{26,27},{31,29}} | collective-permute-start | bytes 3145736 | tf_op jit(solution)/shard_map/ppermute | solution.py:529
  118.5 35.4 %collective-permute-start.19 = (f32[4,256,256]{2,1,0:T(8,128)S(1)}, f32[4,256,256]{2,1,0:T(8,128)S(1)}, u32[]{:S(2)}, u32[]{:S(2)}) collective-permute-start(f32[4,256,256]{2,1,0:T(8,128)S(1)} %add.72.refs_1_), channel_id=1, source_target_pairs={{0,1},{5,6},{10,9},{15,14},{16,17},{21,22},{26,25},{31,30}} | collective-permute-start | bytes 3145736 | tf_op jit(solution)/shard_map/ppermute | solution.py:529
  120.3 34.4 %collective-permute-start.23 = (f32[4,256,256]{2,1,0:T(8,128)}, f32[4,256,256]{2,1,0:T(8,128)}, u32[]{:S(2)}, u32[]{:S(2)}) collective-permute-start(f32[4,256,256]{2,1,0:T(8,128)} %add.75.refs_2_.refs_1_), channel_id=1, source_target_pairs={{0,2},{5,4},{10,11},{15,13},{16,18},{21,20},{26,27},{31,29}} | collective-permute-start | bytes 3145736 | tf_op jit(solution)/shard_map/ppermute | solution.py:529
  122.0 34.1 %collective-permute-start.22 = (f32[4,256,256]{2,1,0:T(8,128)}, f32[4,256,256]{2,1,0:T(8,128)}, u32[]{:S(2)}, u32[]{:S(2)}) collective-permute-start(f32[4,256,256]{2,1,0:T(8,128)} %add.75.refs_2_.refs_1_), channel_id=1, source_target_pairs={{0,1},{5,6},{10,9},{15,14},{16,17},{21,22},{26,25},{31,30}} | collective-permute-start | bytes 3145736 | tf_op jit(solution)/shard_map/ppermute | solution.py:529
  123.8 15.9 %copy-start.2 = (s32[7]{0:T(128)S(1)}, s32[7]{0:T(128)}, u32[]{:S(2)}) copy-start(s32[7]{0:T(128)} %concatenate.12.refs_0_.info) | copy-start | bytes 88
  139.6 1.4 copy-start
  151.0 64.1 %collective-permute-start.18 = (f32[2,4,256,256]{3,2,1,0:T(8,128)S(1)}, f32[2,4,256,256]{3,2,1,0:T(8,128)S(1)}, u32[]{:S(2)}, u32[]{:S(2)}) collective-permute-start(f32[2,4,256,256]{3,2,1,0:T(8,128)S(1)} %get-tuple-element.27.own), channel_id=1, source_target_pairs={{0,4},{1,5},{2,6},{3,7},{4,0},{5,1},{6,2},{7,3},{8,12},{9,13},{10,... | collective-permute-start | bytes 6291464 | tf_op jit(solution)/shard_map/ppermute | solution.py:529
  152.8 6.0 %copy-start.1 = (f32[6,256,256]{2,1,0:T(8,128)S(1)}, f32[6,256,256]{2,1,0:T(8,128)}, u32[]{:S(2)}) copy-start(f32[6,256,256]{2,1,0:T(8,128)} %shard_map.42.refs_3_.refs_4_.refs_5_.refs_6_.refs_7_.refs_8_.refs_2_) | copy-start | bytes 4718596
  152.8 8.1 %collective-permute-start.4 = (f32[4,256,256]{2,1,0:T(8,128)S(1)}, f32[4,256,256]{2,1,0:T(8,128)S(1)}, u32[]{:S(2)}, u32[]{:S(2)}) collective-permute-start(f32[4,256,256]{2,1,0:T(8,128)S(1)} %add.70.refs_1_), channel_id=1, source_target_pairs={{0,2},{5,4},{10,11},{15,13},{16,18},{21,20},{26,27},{31,29}} | collective-permute-start | bytes 3145736 | tf_op jit(solution)/shard_map/ppermute | solution.py:529
  153.9 7.6 %collective-permute-start.3 = (f32[4,256,256]{2,1,0:T(8,128)S(1)}, f32[4,256,256]{2,1,0:T(8,128)S(1)}, u32[]{:S(2)}, u32[]{:S(2)}) collective-permute-start(f32[4,256,256]{2,1,0:T(8,128)S(1)} %add.70.refs_1_), channel_id=1, source_target_pairs={{0,1},{5,6},{10,9},{15,14},{16,17},{21,22},{26,25},{31,30}} | collective-permute-start | bytes 3145736 | tf_op jit(solution)/shard_map/ppermute | solution.py:529
  154.8 29.0 %collective-permute-start.21 = (f32[4,256,256]{2,1,0:T(8,128)S(1)}, f32[4,256,256]{2,1,0:T(8,128)S(1)}, u32[]{:S(2)}, u32[]{:S(2)}) collective-permute-start(f32[4,256,256]{2,1,0:T(8,128)S(1)} %broadcast_select_fusion.1), channel_id=1, source_target_pairs={{2,3},{6,7},{9,8},{13,12},{18,19},{22,23},{25,24},{29,28}} | collective-permute-start | bytes 3145736 | tf_op jit(solution)/shard_map/ppermute | solution.py:529
  157.4 48.8 %collective-permute-start.24 = (f32[4,256,256]{2,1,0:T(8,128)S(1)}, f32[4,256,256]{2,1,0:T(8,128)S(1)}, u32[]{:S(2)}, u32[]{:S(2)}) collective-permute-start(f32[4,256,256]{2,1,0:T(8,128)S(1)} %broadcast_select_fusion), channel_id=1, source_target_pairs={{2,3},{6,7},{9,8},{13,12},{18,19},{22,23},{25,24},{29,28}} | collective-permute-start | bytes 3145736 | tf_op jit(solution)/shard_map/ppermute | solution.py:529
  160.9 65.4 %collective-permute-start.25 = (f32[1,4,256,256]{3,2,1,0:T(8,128)S(1)}, f32[1,4,256,256]{3,2,1,0:T(8,128)S(1)}, u32[]{:S(2)}, u32[]{:S(2)}) collective-permute-start(f32[1,4,256,256]{3,2,1,0:T(8,128)S(1)} %shard_map.47.refs_6_), channel_id=1, source_target_pairs={{0,4},{1,5},{2,6},{3,7},{4,0},{5,1},{6,2},{7,3},{8,12},{9,13},{10,... | collective-permute-start | bytes 3145736 | tf_op jit(solution)/shard_map/ppermute | solution.py:529
  161.6 66.1 %collective-permute-start.5 = (f32[4,256,256]{2,1,0:T(8,128)S(1)}, f32[4,256,256]{2,1,0:T(8,128)S(1)}, u32[]{:S(2)}, u32[]{:S(2)}) collective-permute-start(f32[4,256,256]{2,1,0:T(8,128)S(1)} %broadcast_select_fusion.2), channel_id=1, source_target_pairs={{2,3},{6,7},{9,8},{13,12},{18,19},{22,23},{25,24},{29,28}} | collective-permute-start | bytes 3145736 | tf_op jit(solution)/shard_map/ppermute | solution.py:529
  183.8 31.3 %slice-start = ((s8[8388608]{0:T(1024)(128)(4,1)}), s8[4194304]{0:T(1024)(128)(4,1)S(1)}, s32[]{:S(2)}) async-start(s8[8388608]{0:T(1024)(128)(4,1)} %bitcast.16), calls=%async_computation | async-start | bytes 8388608
  206.3 8.8 %slice-start.1 = ((s8[8388608]{0:T(1024)(128)(4,1)}), s8[4194304]{0:T(1024)(128)(4,1)S(1)}, s32[]{:S(2)}) async-start(s8[8388608]{0:T(1024)(128)(4,1)} %bitcast.16), calls=%async_computation.1 | async-start | bytes 8388608
